TPU v7x, 128 devices: a whole 4x4x4 slice. The times are simulated.
128 devices in a mesh: slab: 4 (over x), tile: 32 (over y, z, core).
Axes of the slice: x: 4, y: 4, z: 4, core: 2. Of those that a mesh axis runs over, the one named last changes fastest.
Arguments:
- features: bfloat16 [262144, 128], P(('slab', 'tile')), may hold values from -6 to 6
- conv_weight: bfloat16 [27, 128, 128], replicated, may hold values from -0.15625 to 0.15625
- down_weight: bfloat16 [8, 128, 128], replicated, may hold values from -0.25 to 0.25
- coarse_grad: bfloat16 [65536, 128], P(('slab', 'tile')), may hold values from -6 to 6
- rulebook: int32 [27, 262144], P(None, ('slab', 'tile')), may hold values from 0 to 3072, as said below
- boundary_rows: int32 [512, 256], P(('slab', 'tile')), may hold values from 0 to 2047, as said below
- parent_code: int32 [262144], P(('slab', 'tile')), may hold values from 0 to 4096, as said below
Outputs:
- coarse: bfloat16 [65536, 128], P(('slab', 'tile'))
- input_grad: float32 [262144, 128], P(('slab', 'tile'))
- conv_grad: float32 [27, 128, 128], replicated
- down_grad: float32 [8, 128, 128], replicated
Inputs may be any that keep to these rules, and one draw needn't show every extreme that they name: `rulebook`: each partition has some number of live blocks of 128 rows, at least one and fewer than 16, at its start; rows of the remaining blocks are dead. For a live row, the centre offset (13) reads the row itself; other entries read a live local row, a received row (2048 to 3071) or the empty row 3072. For each offset and each aligned block of 128 rows of a partition, all entries other than 3072 lie in one aligned block of 128 rows of the extended table. Every entry of a dead row is 3072. `boundary_rows`: entries are live rows of the partition; repeats may occur. `parent_code`: within a partition the live rows with one parent have distinct child positions, at most 4 per parent; the parents of the rows of local block b lie in coarse rows b * 32 to (b + 1) * 32 - 1; dead rows have the code 8 * 512.
All inputs are finite; a program needn't handle non-finite values.
Results may differ from a plain program's by a relative error of at most 0.02.
Values may be sent and summed in bfloat16 or wider, within the bound.
No kernel may reach another device: no remote copies, remote signals or barrier semaphores. Data moves between devices by JAX's collectives and lax.ppermute only.
A program may use at most 64 MiB of HBM per device.

v0:
```python
import jax
import jax.numpy as jnp
from jax import lax
from jax.sharding import PartitionSpec as P

BLOCK = 128


def with_halo(shard, sides, width):
    for axis, dim in sides:
        devices, length = (lax.axis_size(axis), shard.shape[dim])
        up = [(i, (i + 1) % devices) for i in range(devices - 1)]
        down = [(j, i) for i, j in up]
        last = lax.slice_in_dim(shard, length - width, length, axis=dim)
        first = lax.slice_in_dim(shard, 0, width, axis=dim)
        before = lax.ppermute(last, axis, up)
        after = lax.ppermute(first, axis, down)
        shard = jnp.concatenate([before, shard, after], axis=dim)
    return shard


def body(features, conv_weight, down_weight, coarse_grad, rulebook, boundary_rows, parent_code):
    row_count = features.shape[0]
    chan_count = features.shape[1]
    coarse_rows = coarse_grad.shape[0]
    out_chans = coarse_grad.shape[1]
    list_len = boundary_rows.shape[1]
    child_count = down_weight.shape[0]
    kernel_count = conv_weight.shape[0]
    block_len = BLOCK
    block_total = row_count // block_len
    ext_len = row_count + 4 * list_len
    table_blocks = ext_len // block_len + 1
    outgoing = features[boundary_rows]
    arrived = with_halo(outgoing[None, None], (("slab", 0), ("tile", 1)), 1)
    received = jnp.stack([arrived[0, 1, 0], arrived[2, 1, 1], arrived[1, 0, 2], arrived[1, 2, 3]])
    extended = jnp.concatenate(
        [
            features,
            received.reshape(4 * list_len, chan_count),
            jnp.zeros((block_len, chan_count), jnp.bfloat16),
        ],
        axis=0,
    )
    ext_flat = extended.reshape(table_blocks, block_len * chan_count)
    book_rows = rulebook.reshape(kernel_count, block_total, block_len)
    book_block = book_rows // block_len
    source = jnp.min(book_block, axis=2)
    inner_idx = book_rows % block_len
    in_block = book_block == source[:, :, None]
    columns = jnp.arange(block_len, dtype=jnp.int32)
    block_ids = jnp.arange(table_blocks, dtype=jnp.int32)

    def block_pick(src_block):
        return src_block[:, None] == block_ids[None, :]

    def row_pick(inner_one, valid_one):
        return (inner_one[:, :, None] == columns[None, None, :]) & valid_one[:, :, None]

    def forward_step(running, pieces):
        src_block, inner_one, valid_one, weight_one = pieces
        picked = jnp.dot(
            block_pick(src_block).astype(jnp.bfloat16), ext_flat, preferred_element_type=jnp.float32
        )
        picked = picked.astype(jnp.bfloat16).reshape(block_total, block_len, chan_count)
        rows_one = jnp.einsum(
            "bij,bjc->bic",
            row_pick(inner_one, valid_one).astype(jnp.bfloat16),
            picked,
            preferred_element_type=jnp.float32,
        )
        rows_one = rows_one.astype(jnp.bfloat16).reshape(row_count, chan_count)
        return (
            running + jnp.dot(rows_one, weight_one, preferred_element_type=jnp.float32),
            rows_one,
        )

    pre_act, gathered = lax.scan(
        forward_step,
        jnp.zeros((row_count, chan_count), jnp.float32),
        (source, inner_idx, in_block, conv_weight),
    )
    hidden = jnp.maximum(pre_act, 0.0).astype(jnp.bfloat16)
    parent = parent_code // 8
    slot_idx = parent_code % 8
    has_parent = parent < coarse_rows
    quarter = coarse_rows // block_total
    local_parent = parent - jnp.arange(row_count, dtype=jnp.int32) // block_len * quarter
    child_hot = (
        local_parent.reshape(block_total, 1, block_len, 1)
        == jnp.arange(quarter, dtype=jnp.int32)[None, :, None, None]
    )
    child_hot = child_hot & (
        slot_idx.reshape(block_total, 1, block_len, 1)
        == jnp.arange(child_count, dtype=jnp.int32)[None, None, None, :]
    )
    child_hot = child_hot & has_parent.reshape(block_total, 1, block_len, 1)
    children = jnp.einsum(
        "bqrs,brc->bqsc",
        child_hot.astype(jnp.bfloat16),
        hidden.reshape(block_total, block_len, chan_count),
        preferred_element_type=jnp.float32,
    )
    children = children.astype(jnp.bfloat16).reshape(coarse_rows, child_count * chan_count)
    down_flat = down_weight.reshape(child_count * chan_count, out_chans)
    coarse = jnp.dot(children, down_flat, preferred_element_type=jnp.float32).astype(jnp.bfloat16)
    down_part = lax.dot_general(
        children, coarse_grad, (((0,), (0,)), ((), ())), preferred_element_type=jnp.float32
    )
    spread_grad = lax.dot_general(
        coarse_grad, down_flat, (((1,), (1,)), ((), ())), preferred_element_type=jnp.float32
    )
    spread_grad = spread_grad.reshape(block_total, quarter, child_count, chan_count)
    hidden_grad = jnp.einsum(
        "bqrs,bqsc->brc",
        child_hot.astype(jnp.float32),
        spread_grad,
        precision=lax.Precision.HIGHEST,
    ).reshape(row_count, chan_count)
    pre_grad = jnp.where(pre_act > 0, hidden_grad, 0.0).astype(jnp.bfloat16)

    def backward_step(ext_total, pieces):
        src_block, inner_one, valid_one, weight_one, rows_one = pieces
        conv_one = lax.dot_general(
            rows_one, pre_grad, (((0,), (0,)), ((), ())), preferred_element_type=jnp.float32
        )
        back_terms = lax.dot_general(
            pre_grad, weight_one, (((1,), (1,)), ((), ())), preferred_element_type=jnp.float32
        )
        back_terms = back_terms.reshape(block_total, block_len, chan_count)
        within = jnp.einsum(
            "bij,bic->bjc",
            row_pick(inner_one, valid_one).astype(jnp.float32),
            back_terms,
            precision=lax.Precision.HIGHEST,
        )
        placed = jnp.einsum(
            "bn,bjc->njc",
            block_pick(src_block).astype(jnp.float32),
            within,
            precision=lax.Precision.HIGHEST,
        )
        return (ext_total + placed, conv_one)

    ext_grad, conv_part = lax.scan(
        backward_step,
        jnp.zeros((table_blocks, block_len, chan_count), jnp.float32),
        (source, inner_idx, in_block, conv_weight, gathered),
    )
    ext_rows = ext_grad.reshape(table_blocks * block_len, chan_count)
    halo_grad = ext_rows[row_count:ext_len].reshape(4, list_len, chan_count)
    coming = with_halo(
        halo_grad[None, None].astype(jnp.bfloat16), (("slab", 0), ("tile", 1)), 1
    ).astype(jnp.float32)
    returned = jnp.stack([coming[2, 1, 0], coming[0, 1, 1], coming[1, 2, 2], coming[1, 0, 3]])
    input_grad = (
        ext_rows[:row_count]
        .at[boundary_rows.reshape(4 * list_len)]
        .add(returned.reshape(4 * list_len, chan_count))
    )
    conv_grad, down_total = lax.psum((conv_part, down_part), ("slab", "tile"))
    return (coarse, input_grad, conv_grad, down_total.reshape(child_count, chan_count, out_chans))


def solution(mesh):
    return jax.shard_map(
        body,
        mesh=mesh,
        in_specs=(
            P(("slab", "tile"), None),
            P(),
            P(),
            P(("slab", "tile"), None),
            P(None, ("slab", "tile")),
            P(("slab", "tile"), None),
            P(("slab", "tile")),
        ),
        out_specs=(P(("slab", "tile"), None), P(("slab", "tile"), None), P(), P()),
        check_vma=False,
    )
```

profile of v0, /device:TPU:8, one launch (start us, length us, event | category | flops | bytes accessed | tf_op | source)
XLA Modules:
  0.0 674.0 jit_solution(17505798018044980897)
XLA Ops:
  32.8 5.9 collective-permute-done.3
  39.6 6.0 collective-permute-done.2
  47.4 130.2 %while.26 = (s32[]{:T(128)}, f32[2048,128]{1,0:T(8,128)S(1)}, bf16[27,2048,128]{2,1,0:T(8,128)(2,1)}, s32[27,16,128]{2,1,0:T(8,128)}, pred[27,16,128]{2,1,0:T(8,...) while((s32[]{:T(128)}, f32[2048,128]{1,0:T(8,128)S(1)}, ...), condition=%wide.region_2.3_spmd.clone, body=%wide.region_1.2_spmd.clone.sunk | while | flops 148898192 | bytes 7175483 | solution.py:78
  178.6 310.9 %while.27 = (s32[]{:T(128)}, f32[25,128,128]{2,0,1:T(8,128)}, f32[27,128,128]{2,1,0:T(8,128)}, s32[27,16]{1,0:T(8,128)S(1)}, s32[27,16,128]{2,1,0:T(8,128)}, /*i...) while((s32[]{:T(128)}, f32[25,128,128]{2,0,1:T(8,128)}, ...), condition=%wide.region_4.5_spmd.clone, body=%wide.region_3.4_spmd.clone.sunk | while | flops 616857984 | bytes 11272003 | solution.py:145
  193.6 4.6 select_add_fusion.2
  205.2 4.6 select_add_fusion.2
  216.7 4.6 select_add_fusion.2
  228.3 4.6 select_add_fusion.2
  239.9 4.6 select_add_fusion.2
  251.5 4.6 select_add_fusion.2
  263.0 4.6 select_add_fusion.2
  274.6 4.6 select_add_fusion.2
  286.2 4.6 select_add_fusion.2
  297.8 4.6 select_add_fusion.2
  309.3 4.6 select_add_fusion.2
  320.9 4.6 select_add_fusion.2
  332.5 4.6 select_add_fusion.2
  344.1 4.6 select_add_fusion.2
  355.6 4.6 select_add_fusion.2
  367.2 4.6 select_add_fusion.2
  378.8 4.6 select_add_fusion.2
  390.4 4.6 select_add_fusion.2
  401.9 4.6 select_add_fusion.2
  413.5 4.6 select_add_fusion.2
  425.1 4.6 select_add_fusion.2
  436.7 4.6 select_add_fusion.2
  448.2 4.6 select_add_fusion.2
  459.8 4.6 select_add_fusion.2
  483.0 4.6 select_add_fusion.2
  506.9 5.9 collective-permute-start.7
  524.2 6.4 scatter_fusion
  530.6 132.8 %all-reduce.3.cloned.1.call-done = (f32[27,128,128]{2,1,0:T(8,128)}, f32[8,128,128]{2,1,0:T(8,128)}) async-done(((f32[27,128,128]{2,1,0:T(8,128)}, f32[8,128,128]{2,1,0:T(8,128)}), (f32[27,128,128]{2,1,0:T(8,128)}, f32[8,128,128]{2,1,0:T(8,128)})) %all-reduce.3.cloned.1.call-update) | async-done | bytes 2293776 | tf_op jit(solution)/shard_map/psum | solution.py:161
  (503 shorter events, 386.2 us)
Async XLA Ops:
  7.2 9.8 %copy-start = (bf16[8,128,128]{2,1,0:T(8,128)(2,1)S(1)}, bf16[8,128,128]{2,1,0:T(8,128)(2,1)}, u32[]{:S(2)}) copy-start(bf16[8,128,128]{2,1,0:T(8,128)(2,1)} %param.13) | copy-start | bytes 786436
  7.2 9.6 %copy-start.16 = (s32[2048]{0:T(1024)S(1)}, s32[2048]{0:T(1024)}, u32[]{:S(2)}) copy-start(s32[2048]{0:T(1024)} %param.17) | copy-start | bytes 24580
  7.2 9.6 %copy-start.15 = (s32[27,2048]{1,0:T(8,128)S(1)}, s32[27,2048]{1,0:T(8,128)}, u32[]{:S(2)}) copy-start(s32[27,2048]{1,0:T(8,128)} %param.15) | copy-start | bytes 663556
  7.2 9.7 %copy-start.14 = (bf16[512,128]{1,0:T(8,128)(2,1)S(1)}, bf16[512,128]{1,0:T(8,128)(2,1)}, u32[]{:S(2)}) copy-start(bf16[512,128]{1,0:T(8,128)(2,1)} %param.14) | copy-start | bytes 393220
  7.2 656.2 %all-reduce.3.cloned.1.call-start = ((), (), s32[]{:S(2)}) async-start(), calls=%async_computation | async-start | bytes 4587520 | tf_op jit(solution)/shard_map/psum | solution.py:161
  12.0 9.9 %collective-permute-start = (bf16[1,1,4,256,128]{4,3,2,1,0:T(8,128)(2,1)S(1)}, bf16[1,1,4,256,128]{4,3,2,1,0:T(8,128)(2,1)S(1)}, u32[]{:S(2)}, u32[]{:S(2)}) collective-permute-start(bf16[1,1,4,256,128]{4,3,2,1,0:T(8,128)(2,1)S(1)} %bitcast.179), channel_id=1, source_target_pairs={{0,32},{32,64},{64,96},{1,33},{33,65},{65,97},{2,34},{34,66},{66,9... | collective-permute-start | bytes 786440 | tf_op jit(solution)/shard_map/ppermute | solution.py:16
  15.4 9.7 %collective-permute-start.1 = (bf16[1,1,4,256,128]{4,3,2,1,0:T(8,128)(2,1)S(1)}, bf16[1,1,4,256,128]{4,3,2,1,0:T(8,128)(2,1)S(1)}, u32[]{:S(2)}, u32[]{:S(2)}) collective-permute-start(bf16[1,1,4,256,128]{4,3,2,1,0:T(8,128)(2,1)S(1)} %bitcast.180), channel_id=1, source_target_pairs={{32,0},{64,32},{96,64},{33,1},{65,33},{97,65},{34,2},{66,34},{98,6... | collective-permute-start | bytes 786440 | tf_op jit(solution)/shard_map/ppermute | solution.py:17
  20.8 25.7 %copy-start.3 = (bf16[2048,128]{1,0:T(8,128)(2,1)S(1)}, bf16[2048,128]{1,0:T(8,128)(2,1)}, u32[]{:S(2)}) copy-start(bf16[2048,128]{1,0:T(8,128)(2,1)} %param.11) | copy-start | bytes 1572868
  25.2 13.6 %collective-permute-start.3 = (bf16[3,1,4,256,128]{4,3,2,1,0:T(8,128)(2,1)S(1)}, bf16[3,1,4,256,128]{4,3,2,1,0:T(8,128)(2,1)}, u32[]{:S(2)}, u32[]{:S(2)}) collective-permute-start(bf16[3,1,4,256,128]{4,3,2,1,0:T(8,128)(2,1)S(1)} %pad_maximum_fusion), channel_id=1, source_target_pairs={{1,0},{2,1},{3,2},{4,3},{5,4},{6,5},{7,6},{8,7},{9,8},{10,9},{11,1... | collective-permute-start | bytes 2359304 | tf_op jit(solution)/shard_map/ppermute | solution.py:17
  30.1 15.5 %collective-permute-start.2 = (bf16[3,1,4,256,128]{4,3,2,1,0:T(8,128)(2,1)S(1)}, bf16[3,1,4,256,128]{4,3,2,1,0:T(8,128)(2,1)}, u32[]{:S(2)}, u32[]{:S(2)}) collective-permute-start(bf16[3,1,4,256,128]{4,3,2,1,0:T(8,128)(2,1)S(1)} %pad_maximum_fusion), channel_id=1, source_target_pairs={{0,1},{1,2},{2,3},{3,4},{4,5},{5,6},{6,7},{7,8},{8,9},{9,10},{10,1... | collective-permute-start | bytes 2359304 | tf_op jit(solution)/shard_map/ppermute | solution.py:16
  47.4 130.2 %copy-start.10 = (bf16[16,128,128,1]{2,1,3,0:T(8,128)(2,1)S(1)}, bf16[16,128,128,1]{2,1,3,0:T(8,128)(2,1)}, u32[]{:S(2)}) copy-start(bf16[16,128,128,1]{2,1,3,0:T(8,128)(2,1)} %fusion.61) | copy-start | bytes 1572868
  489.5 7.4 %copy-start.11 = (bf16[2048,128]{1,0:T(8,128)(2,1)S(1)}, bf16[2048,128]{1,0:T(8,128)(2,1)}, u32[]{:S(2)}) copy-start(bf16[2048,128]{1,0:T(8,128)(2,1)} %get-tuple-element.227) | copy-start | bytes 1572868
  489.5 7.4 %copy-start.12 = (pred[16,32,128,8]{2,1,3,0:T(32,128)(4,1)S(1)}, pred[16,32,128,8]{2,1,3,0:T(32,128)(4,1)}, u32[]{:S(2)}) copy-start(pred[16,32,128,8]{2,1,3,0:T(32,128)(4,1)} %and_and_fusion) | copy-start | bytes 1572868
  492.2 7.3 %collective-permute-start.4 = (bf16[1,1,4,256,128]{4,3,2,1,0:T(8,128)(2,1)S(1)}, bf16[1,1,4,256,128]{4,3,2,1,0:T(8,128)(2,1)S(1)}, u32[]{:S(2)}, u32[]{:S(2)}) collective-permute-start(bf16[1,1,4,256,128]{4,3,2,1,0:T(8,128)(2,1)S(1)} %bitcast.168), channel_id=1, source_target_pairs={{0,32},{32,64},{64,96},{1,33},{33,65},{65,97},{2,34},{34,66},{66,9... | collective-permute-start | bytes 786440 | tf_op jit(solution)/shard_map/ppermute | solution.py:16
  495.6 8.3 %collective-permute-start.5 = (bf16[1,1,4,256,128]{4,3,2,1,0:T(8,128)(2,1)S(1)}, bf16[1,1,4,256,128]{4,3,2,1,0:T(8,128)(2,1)S(1)}, u32[]{:S(2)}, u32[]{:S(2)}) collective-permute-start(bf16[1,1,4,256,128]{4,3,2,1,0:T(8,128)(2,1)S(1)} %bitcast.169), channel_id=1, source_target_pairs={{32,0},{64,32},{96,64},{33,1},{65,33},{97,65},{34,2},{66,34},{98,6... | collective-permute-start | bytes 786440 | tf_op jit(solution)/shard_map/ppermute | solution.py:17
  497.4 15.5 %copy-start.8 = (bf16[16,32,8,128]{3,2,1,0:T(8,128)(2,1)}, bf16[16,32,8,128]{3,2,1,0:T(8,128)(2,1)S(1)}, u32[]{:S(2)}) copy-start(bf16[16,32,8,128]{3,2,1,0:T(8,128)(2,1)S(1)} %fusion.37) | copy-start | bytes 3145732
  499.5 4.4 copy-start.4
  503.9 1.0 copy-start.6
  504.9 9.3 %copy-start.17 = (s32[4,256]{1,0:T(4,128)S(1)}, s32[4,256]{1,0:T(4,128)}, u32[]{:S(2)}) copy-start(s32[4,256]{1,0:T(4,128)} %param.16) | copy-start | bytes 12292
  504.9 9.4 %copy-start.1 = (f32[25,128,128]{2,0,1:T(8,128)S(1)}, f32[25,128,128]{2,0,1:T(8,128)}, u32[]{:S(2)}) copy-start(f32[25,128,128]{2,0,1:T(8,128)} %get-tuple-element.117) | copy-start | bytes 4915204
  504.9 15.7 %collective-permute-start.6 = (bf16[3,1,4,256,128]{4,3,2,1,0:T(8,128)(2,1)}, bf16[3,1,4,256,128]{4,3,2,1,0:T(8,128)(2,1)S(1)}, u32[]{:S(2)}, u32[]{:S(2)}) collective-permute-start(bf16[3,1,4,256,128]{4,3,2,1,0:T(8,128)(2,1)} %pad_maximum_fusion.1), channel_id=1, source_target_pairs={{0,1},{1,2},{2,3},{3,4},{4,5},{5,6},{6,7},{7,8},{8,9},{9,10},{10,1... | collective-permute-start | bytes 2359304 | tf_op jit(solution)/shard_map/ppermute | solution.py:16
  506.9 16.3 %collective-permute-start.7 = (bf16[3,1,4,256,128]{4,3,2,1,0:T(8,128)(2,1)}, bf16[3,1,4,256,128]{4,3,2,1,0:T(8,128)(2,1)}, u32[]{:S(2)}, u32[]{:S(2)}) collective-permute-start(bf16[3,1,4,256,128]{4,3,2,1,0:T(8,128)(2,1)} %pad_maximum_fusion.1), channel_id=1, source_target_pairs={{1,0},{2,1},{3,2},{4,3},{5,4},{6,5},{7,6},{8,7},{9,8},{10,9},{11,1... | collective-permute-start | bytes 2359304 | tf_op jit(solution)/shard_map/ppermute | solution.py:17
  514.3 1.2 copy-start.9
  514.4 8.9 %copy-start.5 = (bf16[1,1,4,256,128]{4,3,2,1,0:T(8,128)(2,1)S(1)}, bf16[1,1,4,256,128]{4,3,2,1,0:T(8,128)(2,1)}, u32[]{:S(2)}) copy-start(bf16[1,1,4,256,128]{4,3,2,1,0:T(8,128)(2,1)} %copy-done.4) | copy-start | bytes 786436
  514.4 8.8 %copy-start.7 = (bf16[1,1,4,256,128]{4,3,2,1,0:T(8,128)(2,1)S(1)}, bf16[1,1,4,256,128]{4,3,2,1,0:T(8,128)(2,1)}, u32[]{:S(2)}) copy-start(bf16[1,1,4,256,128]{4,3,2,1,0:T(8,128)(2,1)} %copy-done.6) | copy-start | bytes 786436
  530.6 136.5 %copy-start.2 = (f32[2048,128]{1,0:T(8,128)}, f32[2048,128]{1,0:T(8,128)S(1)}, u32[]{:S(2)}) copy-start(f32[2048,128]{1,0:T(8,128)S(1)} %scatter_fusion) | copy-start | bytes 3145732
  663.4 2.9 copy-start.13
Sparse Core Ops, SparseCore 0:
  514.3 149.0 all-reduce.2
where the time goes:
time: 684 us; the launch traced here: 674 us
  matrix products  335 us (49%)
  waiting for transfers between devices  161 us (24%)
  local copies, waits for them, and re-layouts  123 us (18%)
  starting transfers between devices  23.4 us (3%)
  between operations  14.5 us (2%)
  other arithmetic  14.2 us (2%)
    psum x1, waiting for transfers between devices, body(): conv_grad, down_total = lax.psum((conv_part, down_part), ('slab', 'tile'))  133 us
    dot_general x27, matrix products, backward_step(): jnp.einsum('bn,bjc->njc', block_pick(src_block).astype(jnp.float32), with...  121 us
    dot_general x27, matrix products, backward_step(): jnp.einsum('bij,bic->bjc', row_pick(inner_one, valid_one).astype(jnp.floa...  59.4 us
    dot_general x27, matrix products, backward_step(): lax.dot_general(rows_one, pre_grad, (((0,), (0,)), ((), ())), preferred_e...  54.3 us
    eq x54, local copies, waits for them, and re-layouts, row_pick(): inner_one[:, :, None] == columns[None, None, :]  38.1 us
    and x54, local copies, waits for them, and re-layouts, row_pick(): (inner_one[:, :, None] == columns[None, None, :]) & valid_one[:, :, None]  36.8 us
    dot_general x27, matrix products, forward_step(): jnp.dot(rows_one, weight_one, preferred_element_type=jnp.float32)  31.6 us
    dot_general x27, matrix products, backward_step(): lax.dot_general(pre_grad, weight_one, (((1,), (1,)), ((), ())), preferred...  28.4 us
  transfers between devices with their start and end apart: 9, of which 8 were waited for; matrix products, arithmetic and copies ran while one was open for 3% of the time, Pallas kernels for 0%

commit v1 on v0

v1 whole, which is shorter than its diff:
```python
import functools

import jax
import jax.numpy as jnp
from jax import lax
from jax.experimental import pallas as pl
from jax.experimental.pallas import tpu as pltpu
from jax.sharding import PartitionSpec as P

BLOCK = 128
BF = jnp.bfloat16
F32 = jnp.float32
VMEM_LIMIT = 56 * 1024 * 1024
VM = pl.BlockSpec(memory_space=pltpu.VMEM)
SM = pl.BlockSpec(memory_space=pltpu.SMEM)

NN = (((1,), (0,)), ((), ()))
NT = (((1,), (1,)), ((), ()))
TN = (((0,), (0,)), ((), ()))


def mm(a, b, dims=NN):
    return lax.dot_general(a, b, dims, preferred_element_type=F32)


def sub_iota(rows, dtype=F32):
    return lax.broadcasted_iota(jnp.int32, (rows, BLOCK), 0).astype(F32).astype(dtype)


def onehot_t(row, ids):
    wide = jnp.broadcast_to(row, (16, BLOCK)).astype(BF)
    wide = jnp.concatenate([wide] * (ids.shape[0] // 16), axis=0)
    return jnp.where(ids == wide, jnp.ones((), BF), jnp.zeros((), BF))


def pick_kernel(feat_ref, rows_ref, out_ref, xt_ref):
    blocks = feat_ref.shape[0] // BLOCK
    for b in range(blocks):
        xt_ref[b] = feat_ref[b * BLOCK : (b + 1) * BLOCK, :].T
    ids = sub_iota(BLOCK, jnp.int32)
    for g in range(rows_ref.shape[0]):
        row = rows_ref[g : g + 1, :]
        acc = jnp.zeros((BLOCK, BLOCK), F32)
        for b in range(blocks):
            hot = onehot_i(row - b * BLOCK, ids)
            acc = acc + mm(xt_ref[b], hot)
        out_ref[g * BLOCK : (g + 1) * BLOCK, :] = acc.T.astype(BF)


def onehot_i(row, ids):
    return jnp.where(ids == row, 1.0, 0.0).astype(BF)


def main_kernel(
    src_ref, xt_loc_ref, recv_ref, book_ref, cell_ref, w_ref, dw_ref, cg_ref,
    coarse_ref, pgt_ref, part_ref,
    xt_ref, wt_ref, gt_ref, conv_ref, sg_ref, ch_ref,
):
    kvol = w_ref.shape[0]
    blocks = xt_loc_ref.shape[0]
    far = recv_ref.shape[0] // BLOCK
    child = dw_ref.shape[0]
    quarter = cg_ref.shape[0] // blocks
    ids = sub_iota(BLOCK, BF)
    ids2 = jnp.concatenate([ids, ids + jnp.asarray(BLOCK, BF)], axis=0)

    for k in range(kvol):
        wt_ref[:, k * BLOCK : (k + 1) * BLOCK] = w_ref[k].T
    for b in range(blocks):
        xt_ref[b] = xt_loc_ref[b]
    for b in range(far):
        xt_ref[blocks + b] = recv_ref[b * BLOCK : (b + 1) * BLOCK, :].T
    xt_ref[blocks + far] = jnp.zeros((BLOCK, BLOCK), BF)
    for j in range(child):
        part = mm(cg_ref[...], dw_ref[j], NT).astype(BF)
        for b in range(blocks):
            sg_ref[b, j * quarter : (j + 1) * quarter, :] = part[b * quarter : (b + 1) * quarter, :]
    conv_ref[...] = jnp.zeros_like(conv_ref)

    @pl.loop(0, blocks // 2)
    def _(p):
        for k in range(kvol):
            for h in range(2):
                b = 2 * p + h
                hot = onehot_t(book_ref[k, pl.ds(b, 1), :], ids)
                got = mm(xt_ref[src_ref[k, b]], hot)
                gt_ref[k * BLOCK : (k + 1) * BLOCK, h * BLOCK : (h + 1) * BLOCK] = got.astype(BF)
        pre = mm(wt_ref[...], gt_ref[...])
        hid = jnp.maximum(pre, 0.0).astype(BF)
        halves = []
        for h in range(2):
            b = 2 * p + h
            hot = onehot_t(cell_ref[pl.ds(b, 1), :], ids2)
            kids = mm(hot, hid[:, h * BLOCK : (h + 1) * BLOCK], NT).astype(BF)
            for j in range(child):
                ch_ref[pl.ds(pl.multiple_of(b * quarter, quarter), quarter), j * BLOCK : (j + 1) * BLOCK] = (
                    kids[j * quarter : (j + 1) * quarter, :]
                )
            halves.append(mm(sg_ref[b], hot, TN))
        grad = jnp.concatenate(halves, axis=1)
        pgt = jnp.where(pre > 0, grad, 0.0).astype(BF)
        pgt_ref[p] = pgt
        conv_ref[...] += mm(gt_ref[...], pgt, NT)

    kids = ch_ref[...]
    coarse_ref[...] = mm(kids, dw_ref[...].reshape(child * BLOCK, BLOCK)).astype(BF)
    rows = kvol * BLOCK
    part_ref[0:rows, :] = conv_ref[...].astype(BF)
    part_ref[rows : rows + child * BLOCK, :] = mm(kids, cg_ref[...], TN).astype(BF)
    rest = part_ref.shape[0] - rows - child * BLOCK
    part_ref[rows + child * BLOCK :, :] = jnp.zeros((rest, BLOCK), BF)


def back_kernel(src_ref, book_ref, w_ref, pgt_ref, local_ref, far_ref, acc_ref):
    kvol = w_ref.shape[0]
    blocks = local_ref.shape[0] // BLOCK
    far = far_ref.shape[0] // BLOCK
    ids = sub_iota(BLOCK, BF)
    acc_ref[...] = jnp.zeros_like(acc_ref)

    @pl.loop(0, blocks // 2)
    def _(p):
        pgt = pgt_ref[p]
        for k in range(kvol):
            back = mm(w_ref[k], pgt).astype(BF)
            for h in range(2):
                b = 2 * p + h
                hot = onehot_t(book_ref[k, pl.ds(b, 1), :], ids)
                acc_ref[h, src_ref[k, b]] += mm(hot, back[:, h * BLOCK : (h + 1) * BLOCK], NT)

    for b in range(blocks):
        local_ref[b * BLOCK : (b + 1) * BLOCK, :] = acc_ref[0, b] + acc_ref[1, b]
    for b in range(far):
        far_ref[b * BLOCK : (b + 1) * BLOCK, :] = (acc_ref[0, blocks + b] + acc_ref[1, blocks + b]).astype(BF)


def add_kernel(local_ref, rows_ref, ret_ref, out_ref):
    blocks = local_ref.shape[0] // BLOCK
    groups = rows_ref.shape[0]
    ids = sub_iota(BLOCK, jnp.int32)
    for b in range(blocks):
        hot = jnp.concatenate([onehot_i(rows_ref[g : g + 1, :] - b * BLOCK, ids) for g in range(groups)], axis=1)
        out_ref[b * BLOCK : (b + 1) * BLOCK, :] = local_ref[b * BLOCK : (b + 1) * BLOCK, :] + mm(hot, ret_ref[...])


def call(kernel, outs, ins, scratch=()):
    single = len(outs) == 1
    shapes = tuple(jax.ShapeDtypeStruct(s, d) for s, d in outs)
    return pl.pallas_call(
        kernel,
        out_shape=shapes[0] if single else shapes,
        in_specs=ins,
        out_specs=VM if single else tuple(VM for _ in outs),
        scratch_shapes=list(scratch),
        compiler_params=pltpu.CompilerParams(vmem_limit_bytes=VMEM_LIMIT),
    )


def wide(v):
    return v.astype(F32)


def total_over_devices(y):
    tile, slab = lax.axis_index("tile"), lax.axis_index("slab")
    chips = lax.axis_size("tile") // 8
    index = {"c": tile % 2, "z": (tile // 2) % 4, "y": tile // 8, "x": slab}
    stride = {"c": 1, "z": 2, "y": 8}
    size = {"c": 2, "z": 4, "y": chips}

    def send(v, axis, to):
        if axis == "x":
            return lax.ppermute(v, "slab", [(i, to(i)) for i in range(lax.axis_size("slab"))])
        st, n = stride[axis], size[axis]
        pairs = []
        for i in range(lax.axis_size("tile")):
            q = (i // st) % n
            pairs.append((i, i + (to(q) - q) * st))
        return lax.ppermute(v, "tile", pairs)

    def split4(v, axis):
        i, m = index[axis], v.shape[0] // 4
        total = wide(lax.dynamic_slice_in_dim(v, i * m, m, 0))
        got = []
        for sh in (2, 1, 3):
            piece = lax.dynamic_slice_in_dim(v, ((i + sh) % 4) * m, m, 0)
            got.append(send(piece, axis, lambda q, sh=sh: (q + sh) % 4))
        for g in got:
            total = total + wide(g)
        return total.astype(BF)

    def join4(v, axis):
        i, m = index[axis], v.shape[0]
        out = jnp.zeros((4 * m, v.shape[1]), v.dtype)
        out = lax.dynamic_update_slice_in_dim(out, v, i * m, 0)
        got = [(sh, send(v, axis, lambda q, sh=sh: (q + sh) % 4)) for sh in (2, 1, 3)]
        for sh, g in got:
            out = lax.dynamic_update_slice_in_dim(out, g, ((i - sh) % 4) * m, 0)
        return out

    def all4(v, axis):
        g = {sh: wide(send(v, axis, lambda q, sh=sh: (q + sh) % 4)) for sh in (2, 1, 3)}
        return ((wide(v) + g[2]) + (g[1] + g[3])).astype(BF)

    half = y.shape[0] // 2
    core = index["c"]
    keep = lax.dynamic_slice_in_dim(y, core * half, half, 0)
    give = lax.dynamic_slice_in_dim(y, (1 - core) * half, half, 0)
    y = (wide(keep) + wide(send(give, "c", lambda q: 1 - q))).astype(BF)
    y = split4(y, "x")
    y = split4(y, "y")
    y = all4(y, "z")
    y = join4(y, "y")
    y = join4(y, "x")
    other = send(y, "c", lambda q: 1 - q)
    first = jnp.where(core == 0, y, other)
    second = jnp.where(core == 0, other, y)
    return jnp.concatenate([first, second], axis=0)


def body(features, conv_weight, down_weight, coarse_grad, rulebook, boundary_rows, parent_code):
    row_count, chans = features.shape
    coarse_rows, out_chans = coarse_grad.shape
    list_len = boundary_rows.shape[1]
    child = down_weight.shape[0]
    kvol = conv_weight.shape[0]
    blocks = row_count // BLOCK
    far_rows = 4 * list_len
    quarter = coarse_rows // blocks
    slabs, tiles = lax.axis_size("slab"), lax.axis_size("tile")

    lists = boundary_rows.reshape(far_rows // BLOCK, BLOCK)
    outgoing, xt = call(
        pick_kernel, [((far_rows, chans), BF), ((blocks, BLOCK, BLOCK), BF)], [VM, VM]
    )(features, lists)
    outgoing = outgoing.reshape(4, list_len, chans)
    up = {"slab": [(i, i + 1) for i in range(slabs - 1)], "tile": [(i, i + 1) for i in range(tiles - 1)]}
    down = {a: [(j, i) for i, j in pairs] for a, pairs in up.items()}
    received = jnp.concatenate(
        [
            lax.ppermute(outgoing[0], "slab", up["slab"]),
            lax.ppermute(outgoing[1], "slab", down["slab"]),
            lax.ppermute(outgoing[2], "tile", up["tile"]),
            lax.ppermute(outgoing[3], "tile", down["tile"]),
        ]
    )

    book = rulebook.reshape(kvol, blocks, BLOCK)
    source = jnp.min(book, axis=2) // BLOCK
    inner = (book - source[:, :, None] * BLOCK).astype(F32)
    code = parent_code.reshape(blocks, BLOCK)
    cell = (code % child) * quarter + code // child - jnp.arange(blocks, dtype=jnp.int32)[:, None] * quarter
    cell = jnp.where(code < child * coarse_rows, cell, -1).astype(F32)

    grad_rows = (kvol + child) * BLOCK
    part_rows = -(-grad_rows // 512) * 512
    table = blocks + far_rows // BLOCK + 1
    coarse, pgt, part = call(
        main_kernel,
        [((coarse_rows, out_chans), BF), ((blocks // 2, BLOCK, 2 * BLOCK), BF), ((part_rows, out_chans), BF)],
        [SM] + [VM] * 7,
        [
            pltpu.VMEM((table, BLOCK, BLOCK), BF),
            pltpu.VMEM((BLOCK, kvol * BLOCK), BF),
            pltpu.VMEM((kvol * BLOCK, 2 * BLOCK), BF),
            pltpu.VMEM((kvol * BLOCK, BLOCK), F32),
            pltpu.VMEM((blocks, child * quarter, BLOCK), BF),
            pltpu.VMEM((coarse_rows, child * BLOCK), BF),
        ],
    )(source, xt, received, inner, cell, conv_weight, down_weight, coarse_grad)

    total = total_over_devices(part)

    local, far = call(
        back_kernel,
        [((row_count, chans), F32), ((far_rows, chans), BF)],
        [SM] + [VM] * 3,
        [pltpu.VMEM((2, table, BLOCK, BLOCK), F32)],
    )(source, inner, conv_weight, pgt)
    far = far.reshape(4, list_len, chans)
    returned = jnp.concatenate(
        [
            lax.ppermute(far[0], "slab", down["slab"]),
            lax.ppermute(far[1], "slab", up["slab"]),
            lax.ppermute(far[2], "tile", down["tile"]),
            lax.ppermute(far[3], "tile", up["tile"]),
        ]
    )
    input_grad = call(add_kernel, [((row_count, chans), F32)], [VM] * 3)(local, lists, returned)
    total = total.astype(F32)
    return (
        coarse,
        input_grad,
        total[: kvol * BLOCK].reshape(kvol, chans, chans),
        total[kvol * BLOCK : grad_rows].reshape(child, chans, out_chans),
    )


def solution(mesh):
    return jax.shard_map(
        body,
        mesh=mesh,
        in_specs=(
            P(("slab", "tile"), None),
            P(),
            P(),
            P(("slab", "tile"), None),
            P(None, ("slab", "tile")),
            P(("slab", "tile"), None),
            P(("slab", "tile")),
        ),
        out_specs=(P(("slab", "tile"), None), P(("slab", "tile"), None), P(), P()),
        check_vma=False,
    )
```

time: 684 us -> 160 us (0.23); the launches traced: 674 us -> 160 us
  matrix products: 335 us -> 0 us
  waiting for transfers between devices: 161 us -> 24 us
  local copies, waits for them, and re-layouts: 123 us -> 6.1 us
  Pallas kernels: 0 us -> 69.7 us
  starting transfers between devices: 23.4 us -> 53.7 us
  between operations: 14.5 us -> 0.97 us
  other arithmetic: 14.2 us -> 5.44 us
    dot_general x194 -> x0, matrix products: 335 us -> none  [the longest x27 121 us: backward_step(): jnp.einsum('bn,bjc->njc', block_pick(src_block).astype(jnp.float32), with...]
    psum x1 -> x0, waiting for transfers between devices: 133 us -> none  [body(): conv_grad, down_total = lax.psum((conv_part, down_part), ('slab', 'tile'))]
    pallas_call x0 -> x4, Pallas kernels: none -> 69.7 us  [the longest x1 42.1 us: body(): call(back_kernel, [((row_count, chans), F32), ((far_rows, chans), BF)], [...]
    eq x108 -> x0, local copies, waits for them, and re-layouts: 38.6 us -> none  [the longest x54 38.1 us: row_pick(): inner_one[:, :, None] == columns[None, None, :]]
    and x54 -> x0, local copies, waits for them, and re-layouts: 36.8 us -> none  [row_pick(): (inner_one[:, :, None] == columns[None, None, :]) & valid_one[:, :, None]]
    ppermute x8 -> x25, starting transfers between devices: 23.4 us -> 53.7 us  [the longest x11 17.2 us: send(): return lax.ppermute(v, 'tile', pairs)]
    dynamic_update_slice x27 -> x7, local copies, waits for them, and re-layouts: 23 us -> 0.13 us  [the longest x6 0.1 us: join4(): out = lax.dynamic_update_slice_in_dim(out, g, (i - sh) % 4 * m, 0)]
    reshape x28 -> x1, local copies, waits for them, and re-layouts: 9.13 us -> 1.32 us  [body(): lists = boundary_rows.reshape(far_rows // BLOCK, BLOCK)]
  transfers between devices with their start and end apart: 9 -> 25, of which waited for: 8 -> 12; matrix products, arithmetic and copies ran while one was open for 3% -> 3% of each run, Pallas kernels for 0% -> 29%
where the time goes in v1:
time: 160 us
  Pallas kernels  69.7 us (44%)
  starting transfers between devices  53.7 us (34%)
  waiting for transfers between devices  24 us (15%)
  local copies, waits for them, and re-layouts  6.1 us (4%)
  other arithmetic  5.44 us (3%)
    pallas_call x1, Pallas kernels, body(): call(back_kernel, [((row_count, chans), F32), ((far_rows, chans), BF)], [...  42.1 us
    pallas_call x1, Pallas kernels, body(): call(main_kernel, [((coarse_rows, out_chans), BF), ((blocks // 2, BLOCK,...  21 us
    ppermute x11, starting transfers between devices, send(): return lax.ppermute(v, 'tile', pairs)  17.2 us
    ppermute x6, starting transfers between devices, send(): lax.ppermute(v, 'slab', [(i, to(i)) for i in range(lax.axis_size('slab'))])  10.4 us
    ppermute x6, waiting for transfers between devices, send(): lax.ppermute(v, 'slab', [(i, to(i)) for i in range(lax.axis_size('slab'))])  10.2 us
    ppermute x11, waiting for transfers between devices, send(): return lax.ppermute(v, 'tile', pairs)  8.04 us
    ppermute x1, starting transfers between devices, body(): lax.ppermute(far[2], 'tile', down['tile'])  5.88 us
    ppermute x1, starting transfers between devices, body(): lax.ppermute(outgoing[3], 'tile', down['tile'])  5.75 us
  transfers between devices with their start and end apart: 25, of which 12 were waited for; matrix products, arithmetic and copies ran while one was open for 3% of the time, Pallas kernels for 29%

profile of v1, /device:TPU:8, one launch (start us, length us, event | category | flops | bytes accessed | tf_op | source)
XLA Modules:
  0.0 159.9 jit_solution(12690708328123603351)
XLA Ops:
  0.7 1.3 reshape.66.rows_ref
  2.0 3.1 %shard_map.102 = (bf16[1024,128]{1,0:T(8,128)(2,1)}, bf16[16,128,128]{2,1,0:T(8,128)(2,1)}) custom-call(bf16[2048,128]{1,0:T(8,128)(2,1)} %feat_ref.1, s32[8,128]{1,0:T(8,128)} %reshape.66.rows_ref), custom_call_target="tpu_custom_call" | custom-call | tf_op jit(solution)/shard_map/pallas_call | solution.py:232
  6.1 3.4 %collective-permute-start = (bf16[256,128]{1,0:T(8,128)(2,1)S(1)}, bf16[256,128]{1,0:T(8,128)(2,1)S(1)}, u32[]{:S(2)}, u32[]{:S(2)}) collective-permute-start(bf16[256,128]{1,0:T(8,128)(2,1)S(1)} %get-tuple-element.29), channel_id=1, source_target_pairs={{0,32},{32,64},{64,96},{1,33},{33,65},{65,97},{2,34},{34,66},{66,9... | collective-permute-start | bytes 196616 | tf_op jit(solution)/shard_map/ppermute | solution.py:240
  10.8 1.9 %collective-permute-start.2 = (bf16[256,128]{1,0:T(8,128)(2,1)S(1)}, bf16[256,128]{1,0:T(8,128)(2,1)S(1)}, u32[]{:S(2)}, u32[]{:S(2)}) collective-permute-start(bf16[256,128]{1,0:T(8,128)(2,1)S(1)} %get-tuple-element.31), channel_id=1, source_target_pairs={{0,1},{1,2},{2,3},{3,4},{4,5},{5,6},{6,7},{7,8},{8,9},{9,10},{10,1... | collective-permute-start | bytes 196616 | tf_op jit(solution)/shard_map/ppermute | solution.py:242
  12.7 5.8 %collective-permute-start.3 = (bf16[256,128]{1,0:T(8,128)(2,1)S(1)}, bf16[256,128]{1,0:T(8,128)(2,1)S(1)}, u32[]{:S(2)}, u32[]{:S(2)}) collective-permute-start(bf16[256,128]{1,0:T(8,128)(2,1)S(1)} %get-tuple-element.30), channel_id=1, source_target_pairs={{1,0},{2,1},{3,2},{4,3},{5,4},{6,5},{7,6},{8,7},{9,8},{10,9},{11,1... | collective-permute-start | bytes 196616 | tf_op jit(solution)/shard_map/ppermute | solution.py:243
  21.9 21.0 %shard_map.103 = (bf16[512,128]{1,0:T(8,128)(2,1)}, bf16[8,128,256]{2,1,0:T(8,128)(2,1)}, bf16[4608,128]{1,0:T(8,128)(2,1)}) custom-call(s32[27,16]{1,0:T(8,128)} %get-tuple-element.37.src_ref, bf16[16,128,128]{2,1,0:T(8,128)(2,1)} %get-tuple-element.11.xt_loc_ref, bf16[1024,128]{1,0:T(8,128)(2,1)} %pad_maximum_fusion.recv_ref, ...), custom_call_target="tpu_custom_call" | custom-call | tf_op jit(solution)/shard_map/pallas_call | solution.py:257
  44.3 1.9 %collective-permute-done.8 = bf16[2304,128]{1,0:T(8,128)(2,1)S(1)} collective-permute-done((bf16[2304,128]{1,0:T(8,128)(2,1)S(1)}, bf16[2304,128]{1,0:T(8,128)(2,1)S(1)}, u32[]{:S(2)}, u32[]{:S(2)}) %collective-permute-start.8) | collective-permute-done | bytes 589856 | tf_op jit(solution)/shard_map/ppermute | solution.py:178
  46.4 2.7 %collective-permute-start.10 = (bf16[576,128]{1,0:T(8,128)(2,1)S(1)}, bf16[576,128]{1,0:T(8,128)(2,1)S(1)}, u32[]{:S(2)}, u32[]{:S(2)}) collective-permute-start(bf16[576,128]{1,0:T(8,128)(2,1)S(1)} %get-tuple-element.24), channel_id=1, source_target_pairs={{0,32},{32,64},{64,96},{96,0},{1,33},{33,65},{65,97},{97,1},{2,34}... | collective-permute-start | bytes 442376 | tf_op jit(solution)/shard_map/ppermute | solution.py:172
  49.1 1.4 collective-permute-start.11
  50.5 2.2 %collective-permute-start.9 = (bf16[576,128]{1,0:T(8,128)(2,1)S(1)}, bf16[576,128]{1,0:T(8,128)(2,1)S(1)}, u32[]{:S(2)}, u32[]{:S(2)}) collective-permute-start(bf16[576,128]{1,0:T(8,128)(2,1)S(1)} %get-tuple-element.22), channel_id=1, source_target_pairs={{0,64},{32,96},{64,0},{96,32},{1,65},{33,97},{65,1},{97,33},{2,66}... | collective-permute-start | bytes 442376 | tf_op jit(solution)/shard_map/ppermute | solution.py:172
  52.7 1.9 %collective-permute-done.10 = bf16[576,128]{1,0:T(8,128)(2,1)S(1)} collective-permute-done((bf16[576,128]{1,0:T(8,128)(2,1)S(1)}, bf16[576,128]{1,0:T(8,128)(2,1)S(1)}, u32[]{:S(2)}, u32[]{:S(2)}) %collective-permute-start.10) | collective-permute-done | bytes 147488 | tf_op jit(solution)/shard_map/ppermute | solution.py:172
  55.9 3.0 %collective-permute-done.9 = bf16[576,128]{1,0:T(8,128)(2,1)S(1)} collective-permute-done((bf16[576,128]{1,0:T(8,128)(2,1)S(1)}, bf16[576,128]{1,0:T(8,128)(2,1)S(1)}, u32[]{:S(2)}, u32[]{:S(2)}) %collective-permute-start.9) | collective-permute-done | bytes 147488 | tf_op jit(solution)/shard_map/ppermute | solution.py:172
  59.0 2.4 %collective-permute-start.12 = (bf16[144,128]{1,0:T(8,128)(2,1)S(1)}, bf16[144,128]{1,0:T(8,128)(2,1)S(1)}, u32[]{:S(2)}, u32[]{:S(2)}) collective-permute-start(bf16[144,128]{1,0:T(8,128)(2,1)S(1)} %get-tuple-element.33), channel_id=1, source_target_pairs={{0,16},{1,17},{2,18},{3,19},{4,20},{5,21},{6,22},{7,23},{8,24},{9,... | collective-permute-start | bytes 110600 | tf_op jit(solution)/shard_map/ppermute | solution.py:178
  61.4 2.0 %collective-permute-start.14 = (bf16[144,128]{1,0:T(8,128)(2,1)S(1)}, bf16[144,128]{1,0:T(8,128)(2,1)S(1)}, u32[]{:S(2)}, u32[]{:S(2)}) collective-permute-start(bf16[144,128]{1,0:T(8,128)(2,1)S(1)} %get-tuple-element.34), channel_id=1, source_target_pairs={{0,24},{1,25},{2,26},{3,27},{4,28},{5,29},{6,30},{7,31},{8,0},{9,1... | collective-permute-start | bytes 110600 | tf_op jit(solution)/shard_map/ppermute | solution.py:178
  65.4 2.6 %collective-permute-start.15 = (bf16[144,128]{1,0:T(8,128)(2,1)S(1)}, bf16[144,128]{1,0:T(8,128)(2,1)S(1)}, u32[]{:S(2)}, u32[]{:S(2)}) collective-permute-start(bf16[144,128]{1,0:T(8,128)(2,1)S(1)} %add_convert_fusion.3), channel_id=1, source_target_pairs={{0,4},{1,5},{2,6},{3,7},{4,0},{5,1},{6,2},{7,3},{8,12},{9,13},{10,... | collective-permute-start | bytes 110600 | tf_op jit(solution)/shard_map/ppermute | solution.py:178
  68.0 1.5 collective-permute-start.16
  69.5 1.7 %collective-permute-start.17 = (bf16[144,128]{1,0:T(8,128)(2,1)S(1)}, bf16[144,128]{1,0:T(8,128)(2,1)S(1)}, u32[]{:S(2)}, u32[]{:S(2)}) collective-permute-start(bf16[144,128]{1,0:T(8,128)(2,1)S(1)} %add_convert_fusion.3), channel_id=1, source_target_pairs={{0,6},{1,7},{2,0},{3,1},{4,2},{5,3},{6,4},{7,5},{8,14},{9,15},{10,... | collective-permute-start | bytes 110600 | tf_op jit(solution)/shard_map/ppermute | solution.py:178
  71.2 1.9 %collective-permute-done.16 = bf16[144,128]{1,0:T(8,128)(2,1)S(1)} collective-permute-done((bf16[144,128]{1,0:T(8,128)(2,1)S(1)}, bf16[144,128]{1,0:T(8,128)(2,1)S(1)}, u32[]{:S(2)}, u32[]{:S(2)}) %collective-permute-start.16) | collective-permute-done | bytes 36896 | tf_op jit(solution)/shard_map/ppermute | solution.py:178
  73.5 4.6 %collective-permute-start.18 = (bf16[144,128]{1,0:T(8,128)(2,1)S(1)}, bf16[144,128]{1,0:T(8,128)(2,1)S(1)}, u32[]{:S(2)}, u32[]{:S(2)}) collective-permute-start(bf16[144,128]{1,0:T(8,128)(2,1)S(1)} %get-tuple-element.19), channel_id=1, source_target_pairs={{0,16},{1,17},{2,18},{3,19},{4,20},{5,21},{6,22},{7,23},{8,24},{9,... | collective-permute-start | bytes 110600 | tf_op jit(solution)/shard_map/ppermute | solution.py:178
  78.2 2.0 %collective-permute-start.20 = (bf16[144,128]{1,0:T(8,128)(2,1)S(1)}, bf16[144,128]{1,0:T(8,128)(2,1)S(1)}, u32[]{:S(2)}, u32[]{:S(2)}) collective-permute-start(bf16[144,128]{1,0:T(8,128)(2,1)S(1)} %get-tuple-element.19), channel_id=1, source_target_pairs={{0,24},{1,25},{2,26},{3,27},{4,28},{5,29},{6,30},{7,31},{8,0},{9,1... | collective-permute-start | bytes 110600 | tf_op jit(solution)/shard_map/ppermute | solution.py:178
  80.2 1.9 %collective-permute-done.19 = bf16[144,128]{1,0:T(8,128)(2,1)S(1)} collective-permute-done((bf16[144,128]{1,0:T(8,128)(2,1)S(1)}, bf16[144,128]{1,0:T(8,128)(2,1)S(1)}, u32[]{:S(2)}, u32[]{:S(2)}) %collective-permute-start.19) | collective-permute-done | bytes 36896 | tf_op jit(solution)/shard_map/ppermute | solution.py:178
  83.1 1.9 %collective-permute-start.22 = (bf16[576,128]{1,0:T(8,128)(2,1)S(1)}, bf16[576,128]{1,0:T(8,128)(2,1)S(1)}, u32[]{:S(2)}, u32[]{:S(2)}) collective-permute-start(bf16[576,128]{1,0:T(8,128)(2,1)S(1)} %constant_dynamic-update-slice_fusion.4), channel_id=1, source_target_pairs={{0,32},{32,64},{64,96},{96,0},{1,33},{33,65},{65,97},{97,1},{2,34}... | collective-permute-start | bytes 442376 | tf_op jit(solution)/shard_map/ppermute | solution.py:172
  85.0 1.3 collective-permute-start.23
  86.4 2.6 %collective-permute-done.21 = bf16[576,128]{1,0:T(8,128)(2,1)S(1)} collective-permute-done((bf16[576,128]{1,0:T(8,128)(2,1)S(1)}, bf16[576,128]{1,0:T(8,128)(2,1)S(1)}, u32[]{:S(2)}, u32[]{:S(2)}) %collective-permute-start.21) | collective-permute-done | bytes 147488 | tf_op jit(solution)/shard_map/ppermute | solution.py:172
  89.0 1.5 collective-permute-done.22
  90.8 42.1 %shard_map.104 = (f32[2048,128]{1,0:T(8,128)}, bf16[1024,128]{1,0:T(8,128)(2,1)}) custom-call(s32[27,16]{1,0:T(8,128)} %get-tuple-element.37.src_ref, f32[27,16,128]{2,1,0:T(8,128)} %subtract_convert_fusion.book_ref, bf16[27,128,128]{2,1,0:T(8,128)(2,1)} %w_ref.3, bf16[8,128,256]{2,1,0:T(8,128)(2,1)} %get-tuple-element.14.pgt_ref), custom_call_target="tpu_custom_call" | custom-call | tf_op jit(solution)/shard_map/pallas_call | solution.py:273
  135.2 4.5 %collective-permute-start.5 = (bf16[256,128]{1,0:T(8,128)(2,1)S(1)}, bf16[256,128]{1,0:T(8,128)(2,1)S(1)}, u32[]{:S(2)}, u32[]{:S(2)}) collective-permute-start(bf16[256,128]{1,0:T(8,128)(2,1)S(1)} %get-tuple-element.28), channel_id=1, source_target_pairs={{0,32},{32,64},{64,96},{1,33},{33,65},{65,97},{2,34},{34,66},{66,9... | collective-permute-start | bytes 196616 | tf_op jit(solution)/shard_map/ppermute | solution.py:283
  139.7 5.9 %collective-permute-start.6 = (bf16[256,128]{1,0:T(8,128)(2,1)S(1)}, bf16[256,128]{1,0:T(8,128)(2,1)S(1)}, u32[]{:S(2)}, u32[]{:S(2)}) collective-permute-start(bf16[256,128]{1,0:T(8,128)(2,1)S(1)} %get-tuple-element.27), channel_id=1, source_target_pairs={{1,0},{2,1},{3,2},{4,3},{5,4},{6,5},{7,6},{8,7},{9,8},{10,9},{11,1... | collective-permute-start | bytes 196616 | tf_op jit(solution)/shard_map/ppermute | solution.py:284
  145.6 1.9 %collective-permute-start.7 = (bf16[256,128]{1,0:T(8,128)(2,1)S(1)}, bf16[256,128]{1,0:T(8,128)(2,1)S(1)}, u32[]{:S(2)}, u32[]{:S(2)}) collective-permute-start(bf16[256,128]{1,0:T(8,128)(2,1)S(1)} %get-tuple-element.26), channel_id=1, source_target_pairs={{0,1},{1,2},{2,3},{3,4},{4,5},{5,6},{6,7},{7,8},{8,9},{9,10},{10,1... | collective-permute-start | bytes 196616 | tf_op jit(solution)/shard_map/ppermute | solution.py:285
  147.6 5.7 %collective-permute-done.7 = bf16[256,128]{1,0:T(8,128)(2,1)S(1)} collective-permute-done((bf16[256,128]{1,0:T(8,128)(2,1)S(1)}, bf16[256,128]{1,0:T(8,128)(2,1)S(1)}, u32[]{:S(2)}, u32[]{:S(2)}) %collective-permute-start.7) | collective-permute-done | bytes 65568 | tf_op jit(solution)/shard_map/ppermute | solution.py:285
  154.0 3.5 %shard_map.105 = f32[2048,128]{1,0:T(8,128)} custom-call(f32[2048,128]{1,0:T(8,128)} %get-tuple-element.15.local_ref, s32[8,128]{1,0:T(8,128)} %reshape.66.rows_ref, bf16[1024,128]{1,0:T(8,128)(2,1)} %pad_maximum_fusion.1.ret_ref), custom_call_target="tpu_custom_call" | custom-call | tf_op jit(solution)/shard_map/pallas_call | solution.py:288
  158.6 1.3 slice.48
  (59 shorter events, 16.3 us)
Async XLA Ops:
  0.6 17.8 %copy-start.1 = (s32[27,2048]{1,0:T(8,128)S(1)}, s32[27,2048]{1,0:T(8,128)}, u32[]{:S(2)}) copy-start(s32[27,2048]{1,0:T(8,128)} %param.11) | copy-start | bytes 663556
  0.6 19.9 %copy-start.2 = (s32[2048]{0:T(1024)S(1)}, s32[2048]{0:T(1024)}, u32[]{:S(2)}) copy-start(s32[2048]{0:T(1024)} %param.13) | copy-start | bytes 24580
  6.1 15.1 %collective-permute-start = (bf16[256,128]{1,0:T(8,128)(2,1)S(1)}, bf16[256,128]{1,0:T(8,128)(2,1)S(1)}, u32[]{:S(2)}, u32[]{:S(2)}) collective-permute-start(bf16[256,128]{1,0:T(8,128)(2,1)S(1)} %get-tuple-element.29), channel_id=1, source_target_pairs={{0,32},{32,64},{64,96},{1,33},{33,65},{65,97},{2,34},{34,66},{66,9... | collective-permute-start | bytes 196616 | tf_op jit(solution)/shard_map/ppermute | solution.py:240
  9.5 11.7 %collective-permute-start.1 = (bf16[256,128]{1,0:T(8,128)(2,1)S(1)}, bf16[256,128]{1,0:T(8,128)(2,1)S(1)}, u32[]{:S(2)}, u32[]{:S(2)}) collective-permute-start(bf16[256,128]{1,0:T(8,128)(2,1)S(1)} %get-tuple-element.32), channel_id=1, source_target_pairs={{32,0},{64,32},{96,64},{33,1},{65,33},{97,65},{34,2},{66,34},{98,6... | collective-permute-start | bytes 196616 | tf_op jit(solution)/shard_map/ppermute | solution.py:241
  10.8 10.4 %collective-permute-start.2 = (bf16[256,128]{1,0:T(8,128)(2,1)S(1)}, bf16[256,128]{1,0:T(8,128)(2,1)S(1)}, u32[]{:S(2)}, u32[]{:S(2)}) collective-permute-start(bf16[256,128]{1,0:T(8,128)(2,1)S(1)} %get-tuple-element.31), channel_id=1, source_target_pairs={{0,1},{1,2},{2,3},{3,4},{4,5},{5,6},{6,7},{7,8},{8,9},{9,10},{10,1... | collective-permute-start | bytes 196616 | tf_op jit(solution)/shard_map/ppermute | solution.py:242
  12.7 8.5 %collective-permute-start.3 = (bf16[256,128]{1,0:T(8,128)(2,1)S(1)}, bf16[256,128]{1,0:T(8,128)(2,1)S(1)}, u32[]{:S(2)}, u32[]{:S(2)}) collective-permute-start(bf16[256,128]{1,0:T(8,128)(2,1)S(1)} %get-tuple-element.30), channel_id=1, source_target_pairs={{1,0},{2,1},{3,2},{4,3},{5,4},{6,5},{7,6},{8,7},{9,8},{10,9},{11,1... | collective-permute-start | bytes 196616 | tf_op jit(solution)/shard_map/ppermute | solution.py:243
  42.9 3.3 %copy-start = (bf16[4608,128]{1,0:T(8,128)(2,1)S(1)}, bf16[4608,128]{1,0:T(8,128)(2,1)}, u32[]{:S(2)}) copy-start(bf16[4608,128]{1,0:T(8,128)(2,1)} %get-tuple-element.17) | copy-start | bytes 3538948
  44.1 2.1 %collective-permute-start.8 = (bf16[2304,128]{1,0:T(8,128)(2,1)S(1)}, bf16[2304,128]{1,0:T(8,128)(2,1)S(1)}, u32[]{:S(2)}, u32[]{:S(2)}) collective-permute-start(bf16[2304,128]{1,0:T(8,128)(2,1)S(1)} %constant_dynamic-slice_fusion.6), channel_id=1, source_target_pairs={{0,1},{1,0},{2,3},{3,2},{4,5},{5,4},{6,7},{7,6},{8,9},{9,8},{10,11... | collective-permute-start | bytes 1769480 | tf_op jit(solution)/shard_map/ppermute | solution.py:178
  46.4 8.1 %collective-permute-start.10 = (bf16[576,128]{1,0:T(8,128)(2,1)S(1)}, bf16[576,128]{1,0:T(8,128)(2,1)S(1)}, u32[]{:S(2)}, u32[]{:S(2)}) collective-permute-start(bf16[576,128]{1,0:T(8,128)(2,1)S(1)} %get-tuple-element.24), channel_id=1, source_target_pairs={{0,32},{32,64},{64,96},{96,0},{1,33},{33,65},{65,97},{97,1},{2,34}... | collective-permute-start | bytes 442376 | tf_op jit(solution)/shard_map/ppermute | solution.py:172
  49.1 6.7 %collective-permute-start.11 = (bf16[576,128]{1,0:T(8,128)(2,1)S(1)}, bf16[576,128]{1,0:T(8,128)(2,1)S(1)}, u32[]{:S(2)}, u32[]{:S(2)}) collective-permute-start(bf16[576,128]{1,0:T(8,128)(2,1)S(1)} %get-tuple-element.23), channel_id=1, source_target_pairs={{0,96},{32,0},{64,32},{96,64},{1,97},{33,1},{65,33},{97,65},{2,98}... | collective-permute-start | bytes 442376 | tf_op jit(solution)/shard_map/ppermute | solution.py:172
  50.5 8.4 %collective-permute-start.9 = (bf16[576,128]{1,0:T(8,128)(2,1)S(1)}, bf16[576,128]{1,0:T(8,128)(2,1)S(1)}, u32[]{:S(2)}, u32[]{:S(2)}) collective-permute-start(bf16[576,128]{1,0:T(8,128)(2,1)S(1)} %get-tuple-element.22), channel_id=1, source_target_pairs={{0,64},{32,96},{64,0},{96,32},{1,65},{33,97},{65,1},{97,33},{2,66}... | collective-permute-start | bytes 442376 | tf_op jit(solution)/shard_map/ppermute | solution.py:172
  59.0 5.7 %collective-permute-start.12 = (bf16[144,128]{1,0:T(8,128)(2,1)S(1)}, bf16[144,128]{1,0:T(8,128)(2,1)S(1)}, u32[]{:S(2)}, u32[]{:S(2)}) collective-permute-start(bf16[144,128]{1,0:T(8,128)(2,1)S(1)} %get-tuple-element.33), channel_id=1, source_target_pairs={{0,16},{1,17},{2,18},{3,19},{4,20},{5,21},{6,22},{7,23},{8,24},{9,... | collective-permute-start | bytes 110600 | tf_op jit(solution)/shard_map/ppermute | solution.py:178
  61.4 4.0 %collective-permute-start.13 = (bf16[144,128]{1,0:T(8,128)(2,1)S(1)}, bf16[144,128]{1,0:T(8,128)(2,1)S(1)}, u32[]{:S(2)}, u32[]{:S(2)}) collective-permute-start(bf16[144,128]{1,0:T(8,128)(2,1)S(1)} %get-tuple-element.35), channel_id=1, source_target_pairs={{0,8},{1,9},{2,10},{3,11},{4,12},{5,13},{6,14},{7,15},{8,16},{9,17... | collective-permute-start | bytes 110600 | tf_op jit(solution)/shard_map/ppermute | solution.py:178
  61.4 4.0 %collective-permute-start.14 = (bf16[144,128]{1,0:T(8,128)(2,1)S(1)}, bf16[144,128]{1,0:T(8,128)(2,1)S(1)}, u32[]{:S(2)}, u32[]{:S(2)}) collective-permute-start(bf16[144,128]{1,0:T(8,128)(2,1)S(1)} %get-tuple-element.34), channel_id=1, source_target_pairs={{0,24},{1,25},{2,26},{3,27},{4,28},{5,29},{6,30},{7,31},{8,0},{9,1... | collective-permute-start | bytes 110600 | tf_op jit(solution)/shard_map/ppermute | solution.py:178
  65.4 5.8 %collective-permute-start.15 = (bf16[144,128]{1,0:T(8,128)(2,1)S(1)}, bf16[144,128]{1,0:T(8,128)(2,1)S(1)}, u32[]{:S(2)}, u32[]{:S(2)}) collective-permute-start(bf16[144,128]{1,0:T(8,128)(2,1)S(1)} %add_convert_fusion.3), channel_id=1, source_target_pairs={{0,4},{1,5},{2,6},{3,7},{4,0},{5,1},{6,2},{7,3},{8,12},{9,13},{10,... | collective-permute-start | bytes 110600 | tf_op jit(solution)/shard_map/ppermute | solution.py:178
  68.0 5.2 %collective-permute-start.16 = (bf16[144,128]{1,0:T(8,128)(2,1)S(1)}, bf16[144,128]{1,0:T(8,128)(2,1)S(1)}, u32[]{:S(2)}, u32[]{:S(2)}) collective-permute-start(bf16[144,128]{1,0:T(8,128)(2,1)S(1)} %add_convert_fusion.3), channel_id=1, source_target_pairs={{0,2},{1,3},{2,4},{3,5},{4,6},{5,7},{6,0},{7,1},{8,10},{9,11},{10,... | collective-permute-start | bytes 110600 | tf_op jit(solution)/shard_map/ppermute | solution.py:178
  69.5 4.0 %collective-permute-start.17 = (bf16[144,128]{1,0:T(8,128)(2,1)S(1)}, bf16[144,128]{1,0:T(8,128)(2,1)S(1)}, u32[]{:S(2)}, u32[]{:S(2)}) collective-permute-start(bf16[144,128]{1,0:T(8,128)(2,1)S(1)} %add_convert_fusion.3), channel_id=1, source_target_pairs={{0,6},{1,7},{2,0},{3,1},{4,2},{5,3},{6,4},{7,5},{8,14},{9,15},{10,... | collective-permute-start | bytes 110600 | tf_op jit(solution)/shard_map/ppermute | solution.py:178
  73.5 6.7 %collective-permute-start.18 = (bf16[144,128]{1,0:T(8,128)(2,1)S(1)}, bf16[144,128]{1,0:T(8,128)(2,1)S(1)}, u32[]{:S(2)}, u32[]{:S(2)}) collective-permute-start(bf16[144,128]{1,0:T(8,128)(2,1)S(1)} %get-tuple-element.19), channel_id=1, source_target_pairs={{0,16},{1,17},{2,18},{3,19},{4,20},{5,21},{6,22},{7,23},{8,24},{9,... | collective-permute-start | bytes 110600 | tf_op jit(solution)/shard_map/ppermute | solution.py:178
  78.2 4.0 %collective-permute-start.19 = (bf16[144,128]{1,0:T(8,128)(2,1)S(1)}, bf16[144,128]{1,0:T(8,128)(2,1)S(1)}, u32[]{:S(2)}, u32[]{:S(2)}) collective-permute-start(bf16[144,128]{1,0:T(8,128)(2,1)S(1)} %get-tuple-element.19), channel_id=1, source_target_pairs={{0,8},{1,9},{2,10},{3,11},{4,12},{5,13},{6,14},{7,15},{8,16},{9,17... | collective-permute-start | bytes 110600 | tf_op jit(solution)/shard_map/ppermute | solution.py:178
  78.2 4.0 %collective-permute-start.20 = (bf16[144,128]{1,0:T(8,128)(2,1)S(1)}, bf16[144,128]{1,0:T(8,128)(2,1)S(1)}, u32[]{:S(2)}, u32[]{:S(2)}) collective-permute-start(bf16[144,128]{1,0:T(8,128)(2,1)S(1)} %get-tuple-element.19), channel_id=1, source_target_pairs={{0,24},{1,25},{2,26},{3,27},{4,28},{5,29},{6,30},{7,31},{8,0},{9,1... | collective-permute-start | bytes 110600 | tf_op jit(solution)/shard_map/ppermute | solution.py:178
  82.2 6.8 %collective-permute-start.21 = (bf16[576,128]{1,0:T(8,128)(2,1)S(1)}, bf16[576,128]{1,0:T(8,128)(2,1)S(1)}, u32[]{:S(2)}, u32[]{:S(2)}) collective-permute-start(bf16[576,128]{1,0:T(8,128)(2,1)S(1)} %constant_dynamic-update-slice_fusion.4), channel_id=1, source_target_pairs={{0,64},{32,96},{64,0},{96,32},{1,65},{33,97},{65,1},{97,33},{2,66}... | collective-permute-start | bytes 442376 | tf_op jit(solution)/shard_map/ppermute | solution.py:172
  83.1 7.4 %collective-permute-start.22 = (bf16[576,128]{1,0:T(8,128)(2,1)S(1)}, bf16[576,128]{1,0:T(8,128)(2,1)S(1)}, u32[]{:S(2)}, u32[]{:S(2)}) collective-permute-start(bf16[576,128]{1,0:T(8,128)(2,1)S(1)} %constant_dynamic-update-slice_fusion.4), channel_id=1, source_target_pairs={{0,32},{32,64},{64,96},{96,0},{1,33},{33,65},{65,97},{97,1},{2,34}... | collective-permute-start | bytes 442376 | tf_op jit(solution)/shard_map/ppermute | solution.py:172
  85.0 5.5 %collective-permute-start.23 = (bf16[576,128]{1,0:T(8,128)(2,1)S(1)}, bf16[576,128]{1,0:T(8,128)(2,1)S(1)}, u32[]{:S(2)}, u32[]{:S(2)}) collective-permute-start(bf16[576,128]{1,0:T(8,128)(2,1)S(1)} %constant_dynamic-update-slice_fusion.4), channel_id=1, source_target_pairs={{0,96},{32,0},{64,32},{96,64},{1,97},{33,1},{65,33},{97,65},{2,98}... | collective-permute-start | bytes 442376 | tf_op jit(solution)/shard_map/ppermute | solution.py:172
  90.5 67.0 %collective-permute-start.24 = (bf16[2304,128]{1,0:T(8,128)(2,1)S(1)}, bf16[2304,128]{1,0:T(8,128)(2,1)S(1)}, u32[]{:S(2)}, u32[]{:S(2)}) collective-permute-start(bf16[2304,128]{1,0:T(8,128)(2,1)S(1)} %constant_dynamic-update-slice_fusion), channel_id=1, source_target_pairs={{0,1},{1,0},{2,3},{3,2},{4,5},{5,4},{6,7},{7,6},{8,9},{9,8},{10,11... | collective-permute-start | bytes 1769480 | tf_op jit(solution)/shard_map/ppermute | solution.py:178
  133.9 13.7 %collective-permute-start.4 = (bf16[256,128]{1,0:T(8,128)(2,1)S(1)}, bf16[256,128]{1,0:T(8,128)(2,1)S(1)}, u32[]{:S(2)}, u32[]{:S(2)}) collective-permute-start(bf16[256,128]{1,0:T(8,128)(2,1)S(1)} %get-tuple-element.25), channel_id=1, source_target_pairs={{32,0},{64,32},{96,64},{33,1},{65,33},{97,65},{34,2},{66,34},{98,6... | collective-permute-start | bytes 196616 | tf_op jit(solution)/shard_map/ppermute | solution.py:282
  135.2 12.4 %collective-permute-start.5 = (bf16[256,128]{1,0:T(8,128)(2,1)S(1)}, bf16[256,128]{1,0:T(8,128)(2,1)S(1)}, u32[]{:S(2)}, u32[]{:S(2)}) collective-permute-start(bf16[256,128]{1,0:T(8,128)(2,1)S(1)} %get-tuple-element.28), channel_id=1, source_target_pairs={{0,32},{32,64},{64,96},{1,33},{33,65},{65,97},{2,34},{34,66},{66,9... | collective-permute-start | bytes 196616 | tf_op jit(solution)/shard_map/ppermute | solution.py:283
  139.7 7.8 %collective-permute-start.6 = (bf16[256,128]{1,0:T(8,128)(2,1)S(1)}, bf16[256,128]{1,0:T(8,128)(2,1)S(1)}, u32[]{:S(2)}, u32[]{:S(2)}) collective-permute-start(bf16[256,128]{1,0:T(8,128)(2,1)S(1)} %get-tuple-element.27), channel_id=1, source_target_pairs={{1,0},{2,1},{3,2},{4,3},{5,4},{6,5},{7,6},{8,7},{9,8},{10,9},{11,1... | collective-permute-start | bytes 196616 | tf_op jit(solution)/shard_map/ppermute | solution.py:284
  145.6 7.7 %collective-permute-start.7 = (bf16[256,128]{1,0:T(8,128)(2,1)S(1)}, bf16[256,128]{1,0:T(8,128)(2,1)S(1)}, u32[]{:S(2)}, u32[]{:S(2)}) collective-permute-start(bf16[256,128]{1,0:T(8,128)(2,1)S(1)} %get-tuple-element.26), channel_id=1, source_target_pairs={{0,1},{1,2},{2,3},{3,4},{4,5},{5,6},{6,7},{7,8},{8,9},{9,10},{10,1... | collective-permute-start | bytes 196616 | tf_op jit(solution)/shard_map/ppermute | solution.py:285

commit v2 on v1

v2 whole, which is shorter than its diff:
```python
import functools

import jax
import jax.numpy as jnp
from jax import lax
from jax.experimental import pallas as pl
from jax.experimental.pallas import tpu as pltpu
from jax.sharding import PartitionSpec as P

BLOCK = 128
BF = jnp.bfloat16
F32 = jnp.float32
VMEM_LIMIT = 56 * 1024 * 1024
VM = pl.BlockSpec(memory_space=pltpu.VMEM)
SM = pl.BlockSpec(memory_space=pltpu.SMEM)

NN = (((1,), (0,)), ((), ()))
NT = (((1,), (1,)), ((), ()))
TN = (((0,), (0,)), ((), ()))


def mm(a, b, dims=NN):
    return lax.dot_general(a, b, dims, preferred_element_type=F32)


def sub_iota(rows, dtype=F32):
    return lax.broadcasted_iota(jnp.int32, (rows, BLOCK), 0).astype(F32).astype(dtype)


def onehot_t(row, ids):
    wide = jnp.broadcast_to(row, (16, BLOCK)).astype(BF)
    wide = jnp.concatenate([wide] * (ids.shape[0] // 16), axis=0)
    return jnp.where(ids == wide, jnp.ones((), BF), jnp.zeros((), BF))


def pick_kernel(feat_ref, rows_ref, *refs):
    out_refs, xt_ref, full_ref, hot_ref = refs[:-3], refs[-3], refs[-2], refs[-1]
    blocks = feat_ref.shape[0] // BLOCK
    length = rows_ref.shape[1]
    for b in range(blocks):
        block = feat_ref[b * BLOCK : (b + 1) * BLOCK, :].T
        xt_ref[b] = block
        full_ref[:, b * BLOCK : (b + 1) * BLOCK] = block
    ids = sub_iota(BLOCK, BF)
    for d, out_ref in enumerate(out_refs):
        for g in range(length // BLOCK):
            row = rows_ref[d : d + 1, g * BLOCK : (g + 1) * BLOCK]
            for b in range(blocks):
                hot_ref[b * BLOCK : (b + 1) * BLOCK, g * BLOCK : (g + 1) * BLOCK] = onehot_t(
                    (row - b * BLOCK).astype(F32), ids
                )
        out_ref[...] = mm(full_ref[...], hot_ref[...]).T.astype(BF)


def main_kernel(
    src_ref, core_ref, xt_loc_ref, r0_ref, r1_ref, r2_ref, r3_ref, book_ref, cell_ref, w_ref, dw_ref, cg_ref,
    coarse_ref, pg_ref, wt_ref, keep_ref, give_ref,
    xt_ref, gt_ref, conv_ref, sg_ref, ch_ref, part_ref,
):
    kvol = w_ref.shape[0]
    blocks = xt_loc_ref.shape[0]
    recv_refs = (r0_ref, r1_ref, r2_ref, r3_ref)
    each = r0_ref.shape[0] // BLOCK
    far = 4 * each
    child = dw_ref.shape[0]
    quarter = cg_ref.shape[0] // blocks
    ids = sub_iota(BLOCK, BF)
    ids2 = jnp.concatenate([ids, ids + jnp.asarray(BLOCK, BF)], axis=0)

    for k in range(kvol):
        wt_ref[:, k * BLOCK : (k + 1) * BLOCK] = w_ref[k].T
    for b in range(blocks):
        xt_ref[b] = xt_loc_ref[b]
    for b in range(far):
        one = b % each
        xt_ref[blocks + b] = recv_refs[b // each][one * BLOCK : (one + 1) * BLOCK, :].T
    xt_ref[blocks + far] = jnp.zeros((BLOCK, BLOCK), BF)
    for j in range(child):
        part = mm(cg_ref[...], dw_ref[j], NT).astype(BF)
        for b in range(blocks):
            sg_ref[b, j * quarter : (j + 1) * quarter, :] = part[b * quarter : (b + 1) * quarter, :]
    conv_ref[...] = jnp.zeros_like(conv_ref)

    @pl.loop(0, blocks // 2)
    def _(p):
        for k in range(kvol):
            for h in range(2):
                b = 2 * p + h
                hot = onehot_t(book_ref[k, pl.ds(b, 1), :], ids)
                got = mm(xt_ref[src_ref[k, b]], hot)
                gt_ref[k * BLOCK : (k + 1) * BLOCK, h * BLOCK : (h + 1) * BLOCK] = got.astype(BF)
        pre = mm(wt_ref[...], gt_ref[...])
        hid = jnp.maximum(pre, 0.0).astype(BF)
        halves = []
        for h in range(2):
            b = 2 * p + h
            hot = onehot_t(cell_ref[pl.ds(b, 1), :], ids2)
            kids = mm(hot, hid[:, h * BLOCK : (h + 1) * BLOCK], NT).astype(BF)
            for j in range(child):
                ch_ref[pl.ds(pl.multiple_of(b * quarter, quarter), quarter), j * BLOCK : (j + 1) * BLOCK] = (
                    kids[j * quarter : (j + 1) * quarter, :]
                )
            halves.append(mm(sg_ref[b], hot, TN))
        grad = jnp.concatenate(halves, axis=1)
        pgt = jnp.where(pre > 0, grad, 0.0).astype(BF)
        pg = pgt.T
        pg_ref[p] = pg
        conv_ref[...] += mm(gt_ref[...], pg)

    kids = ch_ref[...]
    coarse_ref[...] = mm(kids, dw_ref[...].reshape(child * BLOCK, BLOCK)).astype(BF)
    rows = kvol * BLOCK
    part_ref[0:rows, :] = conv_ref[...].astype(BF)
    part_ref[rows : rows + child * BLOCK, :] = mm(kids, cg_ref[...], TN).astype(BF)
    rest = part_ref.shape[0] - rows - child * BLOCK
    part_ref[rows + child * BLOCK :, :] = jnp.zeros((rest, BLOCK), BF)
    half = keep_ref.shape[0]
    core = core_ref[0]
    keep_ref[...] = part_ref[pl.ds(pl.multiple_of(core * half, half), half), :]
    give_ref[...] = part_ref[pl.ds(pl.multiple_of((1 - core) * half, half), half), :]


def back_kernel(lo, hi, src_ref, book_ref, wt_ref, pg_ref, *refs):
    if lo == 0:
        table_ref, back_ref = refs
        table_ref[...] = jnp.zeros_like(table_ref)
    else:
        before_ref, table_ref, back_ref = refs
        table_ref[...] = before_ref[...]
    kvol = book_ref.shape[0]
    ids = sub_iota(BLOCK, BF)

    @pl.loop(lo, hi)
    def _(p):
        back_ref[...] = mm(pg_ref[p], wt_ref[...]).astype(BF)
        for k in range(kvol):
            for h in range(2):
                b = 2 * p + h
                hot = onehot_t(book_ref[k, pl.ds(b, 1), :], ids)
                table_ref[src_ref[k, b]] += mm(
                    hot, back_ref[h * BLOCK : (h + 1) * BLOCK, k * BLOCK : (k + 1) * BLOCK]
                )


def add_kernel(table_ref, rows_ref, g0_ref, g1_ref, g2_ref, g3_ref, out_ref, ret_ref):
    blocks = out_ref.shape[0] // BLOCK
    lists, length = rows_ref.shape
    ids = sub_iota(BLOCK, BF)
    for d, got_ref in enumerate((g0_ref, g1_ref, g2_ref, g3_ref)):
        ret_ref[d * length : (d + 1) * length, :] = got_ref[...]
    groups = [
        rows_ref[d : d + 1, g * BLOCK : (g + 1) * BLOCK] for d in range(lists) for g in range(length // BLOCK)
    ]
    for b in range(blocks):
        hot = jnp.concatenate([onehot_t((row - b * BLOCK).astype(F32), ids) for row in groups], axis=1)
        out_ref[b * BLOCK : (b + 1) * BLOCK, :] = table_ref[b] + mm(hot, ret_ref[...])


def spread_kernel(core_ref, own_ref, other_ref, conv_ref, down_ref):
    half = own_ref.shape[0]
    rows = conv_ref.shape[0]

    def put(low_ref, high_ref):
        conv_ref[0:half, :] = low_ref[...].astype(F32)
        conv_ref[half:rows, :] = high_ref[0 : rows - half, :].astype(F32)
        down_ref[...] = high_ref[rows - half : rows - half + down_ref.shape[0], :].astype(F32)

    @pl.when(core_ref[0] == 0)
    def _():
        put(own_ref, other_ref)

    @pl.when(core_ref[0] != 0)
    def _():
        put(other_ref, own_ref)


def call(kernel, outs, ins, scratch=(), aliases=None):
    single = len(outs) == 1
    shapes = tuple(jax.ShapeDtypeStruct(s, d) for s, d in outs)
    return pl.pallas_call(
        kernel,
        out_shape=shapes[0] if single else shapes,
        in_specs=ins,
        out_specs=VM if single else tuple(VM for _ in outs),
        scratch_shapes=list(scratch),
        input_output_aliases=aliases or {},
        compiler_params=pltpu.CompilerParams(vmem_limit_bytes=VMEM_LIMIT),
    )


def wide(v):
    return v.astype(F32)


def tie(*values):
    return lax.optimization_barrier(values)


def body(features, conv_weight, down_weight, coarse_grad, rulebook, boundary_rows, parent_code):
    row_count, chans = features.shape
    coarse_rows, out_chans = coarse_grad.shape
    list_len = boundary_rows.shape[1]
    child = down_weight.shape[0]
    kvol = conv_weight.shape[0]
    blocks = row_count // BLOCK
    pairs = blocks // 2
    far_rows = 4 * list_len
    quarter = coarse_rows // blocks
    slabs, tiles = lax.axis_size("slab"), lax.axis_size("tile")
    place = lax.axis_index("slab") * tiles + lax.axis_index("tile")
    core = place & 1

    *outgoing, xt = call(
        pick_kernel,
        [((list_len, chans), BF)] * 4 + [((blocks, BLOCK, BLOCK), BF)],
        [VM, VM],
        [pltpu.VMEM((BLOCK, row_count), BF), pltpu.VMEM((row_count, list_len), BF)],
    )(features, boundary_rows)
    up = {"slab": [(i, i + 1) for i in range(slabs - 1)], "tile": [(i, i + 1) for i in range(tiles - 1)]}
    down = {a: [(j, i) for i, j in links] for a, links in up.items()}
    received = [
        lax.ppermute(outgoing[0], "slab", up["slab"]),
        lax.ppermute(outgoing[1], "slab", down["slab"]),
        lax.ppermute(outgoing[2], "tile", up["tile"]),
        lax.ppermute(outgoing[3], "tile", down["tile"]),
    ]

    book = rulebook.reshape(kvol, blocks, BLOCK)
    source = jnp.min(book, axis=2) // BLOCK
    inner = (book - source[:, :, None] * BLOCK).astype(F32)
    code = parent_code.reshape(blocks, BLOCK)
    cell = (code % child) * quarter + code // child - jnp.arange(blocks, dtype=jnp.int32)[:, None] * quarter
    cell = jnp.where(code < child * coarse_rows, cell, -1).astype(F32)

    grad_rows = (kvol + child) * BLOCK
    part_rows = -(-grad_rows // 512) * 512
    table = blocks + far_rows // BLOCK + 1
    core_one = core.reshape(1)
    coarse, pg, wt, keep, give = call(
        main_kernel,
        [
            ((coarse_rows, out_chans), BF),
            ((pairs, 2 * BLOCK, BLOCK), BF),
            ((BLOCK, kvol * BLOCK), BF),
            ((part_rows // 2, out_chans), BF),
            ((part_rows // 2, out_chans), BF),
        ],
        [SM, SM] + [VM] * 10,
        [
            pltpu.VMEM((table, BLOCK, BLOCK), BF),
            pltpu.VMEM((kvol * BLOCK, 2 * BLOCK), BF),
            pltpu.VMEM((kvol * BLOCK, BLOCK), F32),
            pltpu.VMEM((blocks, child * quarter, BLOCK), BF),
            pltpu.VMEM((coarse_rows, child * BLOCK), BF),
            pltpu.VMEM((part_rows, BLOCK), BF),
        ],
    )(source, core_one, xt, *received, inner, cell, conv_weight, down_weight, coarse_grad)

    def back_part(acc, lo, hi):
        ins = (source, inner, wt, pg) + (() if acc is None else (acc,))
        return call(
            functools.partial(back_kernel, lo, hi),
            [((table, BLOCK, BLOCK), F32)],
            [SM] + [VM] * (len(ins) - 1),
            [pltpu.VMEM((2 * BLOCK, kvol * BLOCK), BF)],
            aliases={} if acc is None else {4: 0},
        )(*ins)

    stride = {"c": 1, "z": 2, "y": 8, "x": tiles}
    size = {"c": 2, "z": 4, "y": tiles // 8, "x": slabs}

    def send(v, axes, to):
        links = []
        for i in range(slabs * tiles):
            axis = axes[i % 2]
            st, n = stride[axis], size[axis]
            q = (i // st) % n
            links.append((i, i + (to(q) % n - q) * st))
        return lax.ppermute(v, ("slab", "tile"), links)

    def spot(axes):
        first, second = [(place >> (stride[a].bit_length() - 1)) & (size[a] - 1) for a in axes]
        return jnp.where(core == 0, first, second)

    def shifts(axes, pieces):
        return [send(v, axes, lambda q, sh=sh: q + sh) for sh, v in zip((1, 2, 3), pieces)]

    order = ("xy", "yz", "zx", "xy")
    swap = send(give, "cc", lambda q: 1 - q)
    acc = back_part(None, 0, 2)
    swap, acc = tie(swap, acc)
    y = (wide(keep) + wide(swap)).astype(BF)

    i, m = spot(order[0]), y.shape[0] // 4
    mine = lax.dynamic_slice_in_dim(y, i * m, m, 0)
    got = shifts(order[0], [lax.dynamic_slice_in_dim(y, ((i + sh) & 3) * m, m, 0) for sh in (1, 2, 3)])
    acc = back_part(acc, 2, 4)
    *got, acc = tie(*got, acc)
    y = ((wide(mine) + wide(got[1])) + (wide(got[0]) + wide(got[2]))).astype(BF)

    for ph, (lo, hi) in ((1, (4, 6)), (2, (6, 8))):
        y, acc = tie(y, acc)
        got = shifts(order[ph], [y] * 3)
        acc = back_part(acc, lo, hi)
        *got, acc = tie(*got, acc)
        y = ((wide(y) + wide(got[1])) + (wide(got[0]) + wide(got[2]))).astype(BF)

    y, acc = tie(y, acc)
    i = spot(order[3])
    got = shifts(order[3], [y] * 3)
    far = acc[blocks : table - 1].astype(BF).reshape(4, list_len, chans)
    returned = [
        lax.ppermute(far[0], "slab", down["slab"]),
        lax.ppermute(far[1], "slab", up["slab"]),
        lax.ppermute(far[2], "tile", down["tile"]),
        lax.ppermute(far[3], "tile", up["tile"]),
    ]
    full = jnp.zeros((4 * m, out_chans), BF)
    for sh, v in zip((0, 1, 2, 3), [y] + got):
        full = lax.dynamic_update_slice_in_dim(full, v, ((i + 4 - sh) & 3) * m, 0)
    other = send(full, "cc", lambda q: 1 - q)
    input_grad = call(
        add_kernel, [((row_count, chans), F32)], [VM] * 6, [pltpu.VMEM((far_rows, chans), BF)]
    )(acc, boundary_rows, *returned)
    conv_grad, down_grad = call(
        spread_kernel,
        [((kvol * BLOCK, out_chans), F32), ((child * BLOCK, out_chans), F32)],
        [SM, VM, VM],
    )(core_one, full, other)
    return (
        coarse,
        input_grad,
        conv_grad.reshape(kvol, chans, chans),
        down_grad.reshape(child, chans, out_chans),
    )


def solution(mesh):
    return jax.shard_map(
        body,
        mesh=mesh,
        in_specs=(
            P(("slab", "tile"), None),
            P(),
            P(),
            P(("slab", "tile"), None),
            P(None, ("slab", "tile")),
            P(("slab", "tile"), None),
            P(("slab", "tile")),
        ),
        out_specs=(P(("slab", "tile"), None), P(("slab", "tile"), None), P(), P()),
        check_vma=False,
    )
```

time: 160 us -> 116 us (0.72)
  Pallas kernels: 69.7 us -> 52.8 us
  waiting for transfers between devices: 24 us -> 11 us
  starting transfers between devices: 53.7 us -> 43.8 us
  local copies, waits for them, and re-layouts: 6.1 us -> 3.4 us
  other arithmetic: 5.44 us -> 3.16 us
    pallas_call x4 -> x8, Pallas kernels: 69.7 us -> 52.8 us  [the longest x1 21.6 us: body(): call(main_kernel, [((coarse_rows, out_chans), BF), ((pairs, 2 * BLOCK, BL...]
    ppermute x17 -> x14, waiting for transfers between devices: 18.3 us -> 5.3 us  [send(): return lax.ppermute(v, ('slab', 'tile'), links)]
    ppermute x17 -> x14, starting transfers between devices: 27.6 us -> 20 us  [send(): return lax.ppermute(v, ('slab', 'tile'), links)]
    slice x3 -> x1, local copies, waits for them, and re-layouts: 3.23 us -> 0.02 us  [body(): far[3]]
    unnamed x7 -> x27, local copies, waits for them, and re-layouts: 0.06 us -> 3.16 us
    ppermute x1, starting transfers between devices: 5.88 us -> 3.68 us  [body(): lax.ppermute(far[2], 'tile', down['tile'])]
  transfers between devices with their start and end apart: 25 -> 22, of which waited for: 12 -> 3; matrix products, arithmetic and copies ran while one was open for 3% -> 3% of each run, Pallas kernels for 29% -> 22%
where the time goes in v2:
time: 116 us; the launch traced here: 115 us
  Pallas kernels  52.8 us (46%)
  starting transfers between devices  43.8 us (38%)
  waiting for transfers between devices  11 us (9%)
  local copies, waits for them, and re-layouts  3.4 us (3%)
  other arithmetic  3.16 us (3%)
    pallas_call x1, Pallas kernels, body(): call(main_kernel, [((coarse_rows, out_chans), BF), ((pairs, 2 * BLOCK, BL...  21.6 us
    pallas_call x4, Pallas kernels, back_part(): call(functools.partial(back_kernel, lo, hi), [((table, BLOCK, BLOCK), F32...  21.2 us
    ppermute x14, starting transfers between devices, send(): return lax.ppermute(v, ('slab', 'tile'), links)  20 us
    ppermute x1, starting transfers between devices, body(): lax.ppermute(outgoing[3], 'tile', down['tile'])  5.75 us
    ppermute x1, waiting for transfers between devices, body(): lax.ppermute(far[3], 'tile', up['tile'])  5.7 us
    ppermute x14, waiting for transfers between devices, send(): return lax.ppermute(v, ('slab', 'tile'), links)  5.3 us
    ppermute x1, starting transfers between devices, body(): lax.ppermute(far[1], 'slab', up['slab'])  4.55 us
    pallas_call x1, Pallas kernels, body(): call(add_kernel, [((row_count, chans), F32)], [VM] * 6, [pltpu.VMEM((far_...  3.72 us
  transfers between devices with their start and end apart: 22, of which 3 were waited for; matrix products, arithmetic and copies ran while one was open for 3% of the time, Pallas kernels for 22%

profile of v2, /device:TPU:8, one launch (start us, length us, event | category | flops | bytes accessed | tf_op | source)
XLA Modules:
  0.0 115.2 jit_solution(4954853474348407943)
XLA Ops:
  0.6 3.6 %shard_map.102 = (bf16[256,128]{1,0:T(8,128)(2,1)}, bf16[256,128]{1,0:T(8,128)(2,1)}, bf16[256,128]{1,0:T(8,128)(2,1)}, bf16[256,128]{1,0:T(8,128)(2,1)}, bf16[16,128,128]{2,1,0:T(8,128)(2,1)}) custom-call(bf16[2048,128]{1,0:T(8,128)(2,1)} %feat_ref.1, s32[4,256]{1,0:T(4,128)} %rows_ref.3), custom_call_target="tpu_custom_call" | custom-call | tf_op jit(solution)/shard_map/pallas_call | solution.py:213
  4.2 3.4 %collective-permute-start = (bf16[256,128]{1,0:T(8,128)(2,1)}, bf16[256,128]{1,0:T(8,128)(2,1)S(1)}, u32[]{:S(2)}, u32[]{:S(2)}) collective-permute-start(bf16[256,128]{1,0:T(8,128)(2,1)} %get-tuple-element.37), channel_id=1, source_target_pairs={{0,32},{32,64},{64,96},{1,33},{33,65},{65,97},{2,34},{34,66},{66,9... | collective-permute-start | bytes 196616 | tf_op jit(solution)/shard_map/ppermute | solution.py:222
  7.6 1.3 %collective-permute-start.1 = (bf16[256,128]{1,0:T(8,128)(2,1)}, bf16[256,128]{1,0:T(8,128)(2,1)S(1)}, u32[]{:S(2)}, u32[]{:S(2)}) collective-permute-start(bf16[256,128]{1,0:T(8,128)(2,1)} %get-tuple-element.38), channel_id=1, source_target_pairs={{32,0},{64,32},{96,64},{33,1},{65,33},{97,65},{34,2},{66,34},{98,6... | collective-permute-start | bytes 196616 | tf_op jit(solution)/shard_map/ppermute | solution.py:223
  8.9 1.9 %collective-permute-start.2 = (bf16[256,128]{1,0:T(8,128)(2,1)}, bf16[256,128]{1,0:T(8,128)(2,1)S(1)}, u32[]{:S(2)}, u32[]{:S(2)}) collective-permute-start(bf16[256,128]{1,0:T(8,128)(2,1)} %get-tuple-element.39), channel_id=1, source_target_pairs={{0,1},{1,2},{2,3},{3,4},{4,5},{5,6},{6,7},{7,8},{8,9},{9,10},{10,1... | collective-permute-start | bytes 196616 | tf_op jit(solution)/shard_map/ppermute | solution.py:224
  10.8 5.8 %collective-permute-start.3 = (bf16[256,128]{1,0:T(8,128)(2,1)}, bf16[256,128]{1,0:T(8,128)(2,1)S(1)}, u32[]{:S(2)}, u32[]{:S(2)}) collective-permute-start(bf16[256,128]{1,0:T(8,128)(2,1)} %get-tuple-element.40), channel_id=1, source_target_pairs={{1,0},{2,1},{3,2},{4,3},{5,4},{6,5},{7,6},{8,7},{9,8},{10,9},{11,1... | collective-permute-start | bytes 196616 | tf_op jit(solution)/shard_map/ppermute | solution.py:225
  16.6 1.0 copy.14
  18.8 0.8 subtract_convert_fusion.book_ref
  20.9 21.6 %shard_map.103 = (bf16[512,128]{1,0:T(8,128)(2,1)}, bf16[8,256,128]{2,1,0:T(8,128)(2,1)}, bf16[128,3456]{1,0:T(8,128)(2,1)}, bf16[2304,128]{1,0:T(8,128)(2,1)}, bf16[2304,128]{1,0:T(8,128)(2,1)}) custom-call(s32[27,16]{1,0:T(8,128)} %get-tuple-element.76.src_ref, s32[1]{0:T(128)} %bitcast.core_ref, bf16[16,128,128]{2,1,0:T(8,128)(2,1)} %get-tuple-element.36.xt_loc_ref, ...), custom_call_target="tpu_custom_call" | custom-call | tf_op jit(solution)/shard_map/pallas_call | solution.py:239
  42.5 4.9 %shard_map.104.refs_0_ = f32[25,128,128]{2,1,0:T(8,128)} custom-call(s32[27,16]{1,0:T(8,128)} %get-tuple-element.76.src_ref, f32[27,16,128]{2,1,0:T(8,128)} %subtract_convert_fusion.book_ref, bf16[128,3456]{1,0:T(8,128)(2,1)} %get-tuple-element.44.wt_ref, bf16[8,256,128]{2,1,0:T(8,128)(2,1)} %get-tuple-element.45.pg_ref), custom_call_target="tpu_custom_call" | custom-call | tf_op jit(solution)/shard_map/pallas_call | solution.py:261
  47.7 2.6 %collective-permute-start.5 = (bf16[576,128]{1,0:T(8,128)(2,1)S(1)}, bf16[576,128]{1,0:T(8,128)(2,1)S(1)}, u32[]{:S(2)}, u32[]{:S(2)}) collective-permute-start(bf16[576,128]{1,0:T(8,128)(2,1)S(1)} %get-tuple-element.74), channel_id=1, source_target_pairs={{0,32},{1,9},{2,34},{3,11},{4,36},{5,13},{6,38},{7,15},{8,40},{9,1... | collective-permute-start | bytes 442376 | tf_op jit(solution)/shard_map/ppermute | solution.py:279
  50.3 2.8 %collective-permute-start.6 = (bf16[576,128]{1,0:T(8,128)(2,1)S(1)}, bf16[576,128]{1,0:T(8,128)(2,1)S(1)}, u32[]{:S(2)}, u32[]{:S(2)}) collective-permute-start(bf16[576,128]{1,0:T(8,128)(2,1)S(1)} %get-tuple-element.73), channel_id=1, source_target_pairs={{0,64},{1,17},{2,66},{3,19},{4,68},{5,21},{6,70},{7,23},{8,72},{9,... | collective-permute-start | bytes 442376 | tf_op jit(solution)/shard_map/ppermute | solution.py:279
  53.1 1.4 %collective-permute-start.7 = (bf16[576,128]{1,0:T(8,128)(2,1)S(1)}, bf16[576,128]{1,0:T(8,128)(2,1)S(1)}, u32[]{:S(2)}, u32[]{:S(2)}) collective-permute-start(bf16[576,128]{1,0:T(8,128)(2,1)S(1)} %get-tuple-element.72), channel_id=1, source_target_pairs={{0,96},{1,25},{2,98},{3,27},{4,100},{5,29},{6,102},{7,31},{8,104},... | collective-permute-start | bytes 442376 | tf_op jit(solution)/shard_map/ppermute | solution.py:279
  54.5 5.4 %shard_map.105.refs_0_ = f32[25,128,128]{2,1,0:T(8,128)} custom-call(s32[27,16]{1,0:T(8,128)} %get-tuple-element.76.src_ref, f32[27,16,128]{2,1,0:T(8,128)} %subtract_convert_fusion.book_ref, bf16[128,3456]{1,0:T(8,128)(2,1)} %get-tuple-element.44.wt_ref, bf16[8,256,128]{2,1,0:T(8,128)(2,1)} %get-tuple-element.45.pg_ref, ...), custom_call_target="tpu_custom_call", output_to_operand_aliasing={{}: (4, {})} | custom-call | tf_op jit(solution)/shard_map/pallas_call | solution.py:261
  60.1 1.6 %collective-permute-start.8 = (bf16[576,128]{1,0:T(8,128)(2,1)S(1)}, bf16[576,128]{1,0:T(8,128)(2,1)S(1)}, u32[]{:S(2)}, u32[]{:S(2)}) collective-permute-start(bf16[576,128]{1,0:T(8,128)(2,1)S(1)} %add_convert_fusion.3), channel_id=1, source_target_pairs={{0,8},{1,3},{2,10},{3,5},{4,12},{5,7},{6,14},{7,1},{8,16},{9,11},{... | collective-permute-start | bytes 442376 | tf_op jit(solution)/shard_map/ppermute | solution.py:279
  61.7 0.8 collective-permute-start.9
  62.5 2.5 %collective-permute-start.10 = (bf16[576,128]{1,0:T(8,128)(2,1)S(1)}, bf16[576,128]{1,0:T(8,128)(2,1)S(1)}, u32[]{:S(2)}, u32[]{:S(2)}) collective-permute-start(bf16[576,128]{1,0:T(8,128)(2,1)S(1)} %add_convert_fusion.3), channel_id=1, source_target_pairs={{0,24},{1,7},{2,26},{3,1},{4,28},{5,3},{6,30},{7,5},{8,0},{9,15},{... | collective-permute-start | bytes 442376 | tf_op jit(solution)/shard_map/ppermute | solution.py:279
  65.1 5.4 %shard_map.106.refs_0_ = f32[25,128,128]{2,1,0:T(8,128)} custom-call(s32[27,16]{1,0:T(8,128)} %get-tuple-element.76.src_ref, f32[27,16,128]{2,1,0:T(8,128)} %subtract_convert_fusion.book_ref, bf16[128,3456]{1,0:T(8,128)(2,1)} %get-tuple-element.44.wt_ref, bf16[8,256,128]{2,1,0:T(8,128)(2,1)} %get-tuple-element.45.pg_ref, ...), custom_call_target="tpu_custom_call", output_to_operand_aliasing={{}: (4, {})} | custom-call | tf_op jit(solution)/shard_map/pallas_call | solution.py:261
  70.8 3.2 %collective-permute-start.12 = (bf16[576,128]{1,0:T(8,128)(2,1)S(1)}, bf16[576,128]{1,0:T(8,128)(2,1)S(1)}, u32[]{:S(2)}, u32[]{:S(2)}) collective-permute-start(bf16[576,128]{1,0:T(8,128)(2,1)S(1)} %add_convert_fusion.2), channel_id=1, source_target_pairs={{0,4},{1,65},{2,6},{3,67},{4,0},{5,69},{6,2},{7,71},{8,12},{9,73},... | collective-permute-start | bytes 442376 | tf_op jit(solution)/shard_map/ppermute | solution.py:279
  74.0 1.2 %collective-permute-start.13 = (bf16[576,128]{1,0:T(8,128)(2,1)S(1)}, bf16[576,128]{1,0:T(8,128)(2,1)S(1)}, u32[]{:S(2)}, u32[]{:S(2)}) collective-permute-start(bf16[576,128]{1,0:T(8,128)(2,1)S(1)} %add_convert_fusion.2), channel_id=1, source_target_pairs={{0,6},{1,97},{2,0},{3,99},{4,2},{5,101},{6,4},{7,103},{8,14},{9,10... | collective-permute-start | bytes 442376 | tf_op jit(solution)/shard_map/ppermute | solution.py:279
  75.2 5.4 %shard_map.107.table_ref = f32[25,128,128]{2,1,0:T(8,128)} custom-call(s32[27,16]{1,0:T(8,128)} %get-tuple-element.76.src_ref, f32[27,16,128]{2,1,0:T(8,128)} %subtract_convert_fusion.book_ref, bf16[128,3456]{1,0:T(8,128)(2,1)} %get-tuple-element.44.wt_ref, bf16[8,256,128]{2,1,0:T(8,128)(2,1)} %get-tuple-element.45.pg_ref, ...), custom_call_target="tpu_custom_call", output_to_operand_aliasing={{}: (4, {})} | custom-call | tf_op jit(solution)/shard_map/pallas_call | solution.py:261
  81.4 1.8 %collective-permute-start.19 = (bf16[576,128]{1,0:T(8,128)(2,1)S(1)}, bf16[576,128]{1,0:T(8,128)(2,1)S(1)}, u32[]{:S(2)}, u32[]{:S(2)}) collective-permute-start(bf16[576,128]{1,0:T(8,128)(2,1)S(1)} %add_convert_fusion.1), channel_id=1, source_target_pairs={{0,64},{1,17},{2,66},{3,19},{4,68},{5,21},{6,70},{7,23},{8,72},{9,... | collective-permute-start | bytes 442376 | tf_op jit(solution)/shard_map/ppermute | solution.py:279
  83.2 1.0 collective-permute-start.20
  84.3 4.4 %collective-permute-done.18 = bf16[576,128]{1,0:T(8,128)(2,1)S(1)} collective-permute-done((bf16[576,128]{1,0:T(8,128)(2,1)S(1)}, bf16[576,128]{1,0:T(8,128)(2,1)S(1)}, u32[]{:S(2)}, u32[]{:S(2)}) %collective-permute-start.18) | collective-permute-done | bytes 147488 | tf_op jit(solution)/shard_map/ppermute | solution.py:279
  88.8 0.8 collective-permute-done.20
  90.0 1.3 %collective-permute-start.14 = (bf16[256,128]{1,0:T(8,128)(2,1)S(1)}, bf16[256,128]{1,0:T(8,128)(2,1)S(1)}, u32[]{:S(2)}, u32[]{:S(2)}) collective-permute-start(bf16[256,128]{1,0:T(8,128)(2,1)S(1)} %bitcast.39), channel_id=1, source_target_pairs={{32,0},{64,32},{96,64},{33,1},{65,33},{97,65},{34,2},{66,34},{98,6... | collective-permute-start | bytes 196616 | tf_op jit(solution)/shard_map/ppermute | solution.py:313
  91.3 4.5 %collective-permute-start.15 = (bf16[256,128]{1,0:T(8,128)(2,1)S(1)}, bf16[256,128]{1,0:T(8,128)(2,1)S(1)}, u32[]{:S(2)}, u32[]{:S(2)}) collective-permute-start(bf16[256,128]{1,0:T(8,128)(2,1)S(1)} %bitcast.38), channel_id=1, source_target_pairs={{0,32},{32,64},{64,96},{1,33},{33,65},{65,97},{2,34},{34,66},{66,9... | collective-permute-start | bytes 196616 | tf_op jit(solution)/shard_map/ppermute | solution.py:314
  95.8 3.7 %collective-permute-start.16 = (bf16[256,128]{1,0:T(8,128)(2,1)S(1)}, bf16[256,128]{1,0:T(8,128)(2,1)S(1)}, u32[]{:S(2)}, u32[]{:S(2)}) collective-permute-start(bf16[256,128]{1,0:T(8,128)(2,1)S(1)} %bitcast.37), channel_id=1, source_target_pairs={{1,0},{2,1},{3,2},{4,3},{5,4},{6,5},{7,6},{8,7},{9,8},{10,9},{11,1... | collective-permute-start | bytes 196616 | tf_op jit(solution)/shard_map/ppermute | solution.py:315
  99.5 1.9 %collective-permute-start.17 = (bf16[256,128]{1,0:T(8,128)(2,1)S(1)}, bf16[256,128]{1,0:T(8,128)(2,1)S(1)}, u32[]{:S(2)}, u32[]{:S(2)}) collective-permute-start(bf16[256,128]{1,0:T(8,128)(2,1)S(1)} %bitcast.36), channel_id=1, source_target_pairs={{0,1},{1,2},{2,3},{3,4},{4,5},{5,6},{6,7},{7,8},{8,9},{9,10},{10,1... | collective-permute-start | bytes 196616 | tf_op jit(solution)/shard_map/ppermute | solution.py:316
  101.5 5.7 %collective-permute-done.17.g3_ref = bf16[256,128]{1,0:T(8,128)(2,1)S(1)} collective-permute-done((bf16[256,128]{1,0:T(8,128)(2,1)S(1)}, bf16[256,128]{1,0:T(8,128)(2,1)S(1)}, u32[]{:S(2)}, u32[]{:S(2)}) %collective-permute-start.17) | collective-permute-done | bytes 65568 | tf_op jit(solution)/shard_map/ppermute | solution.py:316
  107.9 3.7 %shard_map.108 = f32[2048,128]{1,0:T(8,128)} custom-call(f32[25,128,128]{2,1,0:T(8,128)} %shard_map.107.table_ref, s32[4,256]{1,0:T(4,128)} %rows_ref.3, bf16[256,128]{1,0:T(8,128)(2,1)} %copy-done.8, bf16[256,128]{1,0:T(8,128)(2,1)} %copy-done.9, bf16[256,128]{1,0:T(8,128)(2,1)} %copy-done.10, bf16[256,128]{1,0:T(8,128)(2,1)} %copy-done.11), custom_call_target="tpu_custom_call" | custom-call | tf_op jit(solution)/shard_map/pallas_call | solution.py:322
  111.6 0.9 copy-done.3
  112.5 2.8 %shard_map.109 = (f32[3456,128]{1,0:T(8,128)}, f32[1024,128]{1,0:T(8,128)}) custom-call(s32[1]{0:T(128)} %bitcast.core_ref, bf16[2304,128]{1,0:T(8,128)(2,1)} %copy-done.1, bf16[2304,128]{1,0:T(8,128)(2,1)} %copy-done.3), custom_call_target="tpu_custom_call" | custom-call | tf_op jit(solution)/shard_map/pallas_call | solution.py:325
  (64 shorter events, 4.9 us)
Async XLA Ops:
  0.6 18.9 %copy-start.12 = (s32[2048]{0:T(1024)S(1)}, s32[2048]{0:T(1024)}, u32[]{:S(2)}) copy-start(s32[2048]{0:T(1024)} %param.13) | copy-start | bytes 24580
  4.2 16.0 %collective-permute-start = (bf16[256,128]{1,0:T(8,128)(2,1)}, bf16[256,128]{1,0:T(8,128)(2,1)S(1)}, u32[]{:S(2)}, u32[]{:S(2)}) collective-permute-start(bf16[256,128]{1,0:T(8,128)(2,1)} %get-tuple-element.37), channel_id=1, source_target_pairs={{0,32},{32,64},{64,96},{1,33},{33,65},{65,97},{2,34},{34,66},{66,9... | collective-permute-start | bytes 196616 | tf_op jit(solution)/shard_map/ppermute | solution.py:222
  7.6 12.6 %collective-permute-start.1 = (bf16[256,128]{1,0:T(8,128)(2,1)}, bf16[256,128]{1,0:T(8,128)(2,1)S(1)}, u32[]{:S(2)}, u32[]{:S(2)}) collective-permute-start(bf16[256,128]{1,0:T(8,128)(2,1)} %get-tuple-element.38), channel_id=1, source_target_pairs={{32,0},{64,32},{96,64},{33,1},{65,33},{97,65},{34,2},{66,34},{98,6... | collective-permute-start | bytes 196616 | tf_op jit(solution)/shard_map/ppermute | solution.py:223
  8.9 11.4 %collective-permute-start.2 = (bf16[256,128]{1,0:T(8,128)(2,1)}, bf16[256,128]{1,0:T(8,128)(2,1)S(1)}, u32[]{:S(2)}, u32[]{:S(2)}) collective-permute-start(bf16[256,128]{1,0:T(8,128)(2,1)} %get-tuple-element.39), channel_id=1, source_target_pairs={{0,1},{1,2},{2,3},{3,4},{4,5},{5,6},{6,7},{7,8},{8,9},{9,10},{10,1... | collective-permute-start | bytes 196616 | tf_op jit(solution)/shard_map/ppermute | solution.py:224
  10.8 9.5 %collective-permute-start.3 = (bf16[256,128]{1,0:T(8,128)(2,1)}, bf16[256,128]{1,0:T(8,128)(2,1)S(1)}, u32[]{:S(2)}, u32[]{:S(2)}) collective-permute-start(bf16[256,128]{1,0:T(8,128)(2,1)} %get-tuple-element.40), channel_id=1, source_target_pairs={{1,0},{2,1},{3,2},{4,3},{5,4},{6,5},{7,6},{8,7},{9,8},{10,9},{11,1... | collective-permute-start | bytes 196616 | tf_op jit(solution)/shard_map/ppermute | solution.py:225
  20.2 0.6 copy-start.5
  20.3 0.6 copy-start.6
  42.5 4.9 %collective-permute-start.4 = (bf16[2304,128]{1,0:T(8,128)(2,1)}, bf16[2304,128]{1,0:T(8,128)(2,1)S(1)}, u32[]{:S(2)}, u32[]{:S(2)}) collective-permute-start(bf16[2304,128]{1,0:T(8,128)(2,1)} %get-tuple-element.43), channel_id=1, source_target_pairs={{0,1},{1,0},{2,3},{3,2},{4,5},{5,4},{6,7},{7,6},{8,9},{9,8},{10,11... | collective-permute-start | bytes 1769480 | tf_op jit(solution)/shard_map/ppermute | solution.py:279
  42.5 4.9 %copy-start.2 = (bf16[2304,128]{1,0:T(8,128)(2,1)S(1)}, bf16[2304,128]{1,0:T(8,128)(2,1)}, u32[]{:S(2)}) copy-start(bf16[2304,128]{1,0:T(8,128)(2,1)} %get-tuple-element.42) | copy-start | bytes 1769476
  47.7 12.3 %collective-permute-start.5 = (bf16[576,128]{1,0:T(8,128)(2,1)S(1)}, bf16[576,128]{1,0:T(8,128)(2,1)S(1)}, u32[]{:S(2)}, u32[]{:S(2)}) collective-permute-start(bf16[576,128]{1,0:T(8,128)(2,1)S(1)} %get-tuple-element.74), channel_id=1, source_target_pairs={{0,32},{1,9},{2,34},{3,11},{4,36},{5,13},{6,38},{7,15},{8,40},{9,1... | collective-permute-start | bytes 442376 | tf_op jit(solution)/shard_map/ppermute | solution.py:279
  50.3 9.7 %collective-permute-start.6 = (bf16[576,128]{1,0:T(8,128)(2,1)S(1)}, bf16[576,128]{1,0:T(8,128)(2,1)S(1)}, u32[]{:S(2)}, u32[]{:S(2)}) collective-permute-start(bf16[576,128]{1,0:T(8,128)(2,1)S(1)} %get-tuple-element.73), channel_id=1, source_target_pairs={{0,64},{1,17},{2,66},{3,19},{4,68},{5,21},{6,70},{7,23},{8,72},{9,... | collective-permute-start | bytes 442376 | tf_op jit(solution)/shard_map/ppermute | solution.py:279
  53.1 6.9 %collective-permute-start.7 = (bf16[576,128]{1,0:T(8,128)(2,1)S(1)}, bf16[576,128]{1,0:T(8,128)(2,1)S(1)}, u32[]{:S(2)}, u32[]{:S(2)}) collective-permute-start(bf16[576,128]{1,0:T(8,128)(2,1)S(1)} %get-tuple-element.72), channel_id=1, source_target_pairs={{0,96},{1,25},{2,98},{3,27},{4,100},{5,29},{6,102},{7,31},{8,104},... | collective-permute-start | bytes 442376 | tf_op jit(solution)/shard_map/ppermute | solution.py:279
  60.1 10.4 %collective-permute-start.8 = (bf16[576,128]{1,0:T(8,128)(2,1)S(1)}, bf16[576,128]{1,0:T(8,128)(2,1)S(1)}, u32[]{:S(2)}, u32[]{:S(2)}) collective-permute-start(bf16[576,128]{1,0:T(8,128)(2,1)S(1)} %add_convert_fusion.3), channel_id=1, source_target_pairs={{0,8},{1,3},{2,10},{3,5},{4,12},{5,7},{6,14},{7,1},{8,16},{9,11},{... | collective-permute-start | bytes 442376 | tf_op jit(solution)/shard_map/ppermute | solution.py:279
  61.7 8.8 %collective-permute-start.9 = (bf16[576,128]{1,0:T(8,128)(2,1)S(1)}, bf16[576,128]{1,0:T(8,128)(2,1)S(1)}, u32[]{:S(2)}, u32[]{:S(2)}) collective-permute-start(bf16[576,128]{1,0:T(8,128)(2,1)S(1)} %add_convert_fusion.3), channel_id=1, source_target_pairs={{0,16},{1,5},{2,18},{3,7},{4,20},{5,1},{6,22},{7,3},{8,24},{9,13},... | collective-permute-start | bytes 442376 | tf_op jit(solution)/shard_map/ppermute | solution.py:279
  62.5 8.0 %collective-permute-start.10 = (bf16[576,128]{1,0:T(8,128)(2,1)S(1)}, bf16[576,128]{1,0:T(8,128)(2,1)S(1)}, u32[]{:S(2)}, u32[]{:S(2)}) collective-permute-start(bf16[576,128]{1,0:T(8,128)(2,1)S(1)} %add_convert_fusion.3), channel_id=1, source_target_pairs={{0,24},{1,7},{2,26},{3,1},{4,28},{5,3},{6,30},{7,5},{8,0},{9,15},{... | collective-permute-start | bytes 442376 | tf_op jit(solution)/shard_map/ppermute | solution.py:279
  70.6 10.1 %collective-permute-start.11 = (bf16[576,128]{1,0:T(8,128)(2,1)S(1)}, bf16[576,128]{1,0:T(8,128)(2,1)S(1)}, u32[]{:S(2)}, u32[]{:S(2)}) collective-permute-start(bf16[576,128]{1,0:T(8,128)(2,1)S(1)} %add_convert_fusion.2), channel_id=1, source_target_pairs={{0,2},{1,33},{2,4},{3,35},{4,6},{5,37},{6,0},{7,39},{8,10},{9,41},... | collective-permute-start | bytes 442376 | tf_op jit(solution)/shard_map/ppermute | solution.py:279
  70.8 9.8 %collective-permute-start.12 = (bf16[576,128]{1,0:T(8,128)(2,1)S(1)}, bf16[576,128]{1,0:T(8,128)(2,1)S(1)}, u32[]{:S(2)}, u32[]{:S(2)}) collective-permute-start(bf16[576,128]{1,0:T(8,128)(2,1)S(1)} %add_convert_fusion.2), channel_id=1, source_target_pairs={{0,4},{1,65},{2,6},{3,67},{4,0},{5,69},{6,2},{7,71},{8,12},{9,73},... | collective-permute-start | bytes 442376 | tf_op jit(solution)/shard_map/ppermute | solution.py:279
  74.0 6.6 %collective-permute-start.13 = (bf16[576,128]{1,0:T(8,128)(2,1)S(1)}, bf16[576,128]{1,0:T(8,128)(2,1)S(1)}, u32[]{:S(2)}, u32[]{:S(2)}) collective-permute-start(bf16[576,128]{1,0:T(8,128)(2,1)S(1)} %add_convert_fusion.2), channel_id=1, source_target_pairs={{0,6},{1,97},{2,0},{3,99},{4,2},{5,101},{6,4},{7,103},{8,14},{9,10... | collective-permute-start | bytes 442376 | tf_op jit(solution)/shard_map/ppermute | solution.py:279
  80.6 9.1 %copy-start = (f32[25,128,128]{2,1,0:T(8,128)S(1)}, f32[25,128,128]{2,1,0:T(8,128)}, u32[]{:S(2)}) copy-start(f32[25,128,128]{2,1,0:T(8,128)} %shard_map.107.table_ref) | copy-start | bytes 4915204
  80.8 8.0 %collective-permute-start.18 = (bf16[576,128]{1,0:T(8,128)(2,1)S(1)}, bf16[576,128]{1,0:T(8,128)(2,1)S(1)}, u32[]{:S(2)}, u32[]{:S(2)}) collective-permute-start(bf16[576,128]{1,0:T(8,128)(2,1)S(1)} %add_convert_fusion.1), channel_id=1, source_target_pairs={{0,32},{1,9},{2,34},{3,11},{4,36},{5,13},{6,38},{7,15},{8,40},{9,1... | collective-permute-start | bytes 442376 | tf_op jit(solution)/shard_map/ppermute | solution.py:279
  81.4 7.4 %collective-permute-start.19 = (bf16[576,128]{1,0:T(8,128)(2,1)S(1)}, bf16[576,128]{1,0:T(8,128)(2,1)S(1)}, u32[]{:S(2)}, u32[]{:S(2)}) collective-permute-start(bf16[576,128]{1,0:T(8,128)(2,1)S(1)} %add_convert_fusion.1), channel_id=1, source_target_pairs={{0,64},{1,17},{2,66},{3,19},{4,68},{5,21},{6,70},{7,23},{8,72},{9,... | collective-permute-start | bytes 442376 | tf_op jit(solution)/shard_map/ppermute | solution.py:279
  83.2 6.5 %collective-permute-start.20 = (bf16[576,128]{1,0:T(8,128)(2,1)S(1)}, bf16[576,128]{1,0:T(8,128)(2,1)S(1)}, u32[]{:S(2)}, u32[]{:S(2)}) collective-permute-start(bf16[576,128]{1,0:T(8,128)(2,1)S(1)} %add_convert_fusion.1), channel_id=1, source_target_pairs={{0,96},{1,25},{2,98},{3,27},{4,100},{5,29},{6,102},{7,31},{8,104},... | collective-permute-start | bytes 442376 | tf_op jit(solution)/shard_map/ppermute | solution.py:279
  89.7 21.9 %copy-start.1 = (bf16[2304,128]{1,0:T(8,128)(2,1)}, bf16[2304,128]{1,0:T(8,128)(2,1)S(1)}, u32[]{:S(2)}) copy-start(bf16[2304,128]{1,0:T(8,128)(2,1)S(1)} %constant_dynamic-update-slice_fusion.own_ref) | copy-start | bytes 1769476
  89.7 21.9 %collective-permute-start.21 = (bf16[2304,128]{1,0:T(8,128)(2,1)S(1)}, bf16[2304,128]{1,0:T(8,128)(2,1)S(1)}, u32[]{:S(2)}, u32[]{:S(2)}) collective-permute-start(bf16[2304,128]{1,0:T(8,128)(2,1)S(1)} %constant_dynamic-update-slice_fusion.own_ref), channel_id=1, source_target_pairs={{0,1},{1,0},{2,3},{3,2},{4,5},{5,4},{6,7},{7,6},{8,9},{9,8},{10,11... | collective-permute-start | bytes 1769480 | tf_op jit(solution)/shard_map/ppermute | solution.py:279
  90.0 11.5 %collective-permute-start.14 = (bf16[256,128]{1,0:T(8,128)(2,1)S(1)}, bf16[256,128]{1,0:T(8,128)(2,1)S(1)}, u32[]{:S(2)}, u32[]{:S(2)}) collective-permute-start(bf16[256,128]{1,0:T(8,128)(2,1)S(1)} %bitcast.39), channel_id=1, source_target_pairs={{32,0},{64,32},{96,64},{33,1},{65,33},{97,65},{34,2},{66,34},{98,6... | collective-permute-start | bytes 196616 | tf_op jit(solution)/shard_map/ppermute | solution.py:313
  91.3 10.2 %collective-permute-start.15 = (bf16[256,128]{1,0:T(8,128)(2,1)S(1)}, bf16[256,128]{1,0:T(8,128)(2,1)S(1)}, u32[]{:S(2)}, u32[]{:S(2)}) collective-permute-start(bf16[256,128]{1,0:T(8,128)(2,1)S(1)} %bitcast.38), channel_id=1, source_target_pairs={{0,32},{32,64},{64,96},{1,33},{33,65},{65,97},{2,34},{34,66},{66,9... | collective-permute-start | bytes 196616 | tf_op jit(solution)/shard_map/ppermute | solution.py:314
  95.8 5.7 %collective-permute-start.16 = (bf16[256,128]{1,0:T(8,128)(2,1)S(1)}, bf16[256,128]{1,0:T(8,128)(2,1)S(1)}, u32[]{:S(2)}, u32[]{:S(2)}) collective-permute-start(bf16[256,128]{1,0:T(8,128)(2,1)S(1)} %bitcast.37), channel_id=1, source_target_pairs={{1,0},{2,1},{3,2},{4,3},{5,4},{6,5},{7,6},{8,7},{9,8},{10,9},{11,1... | collective-permute-start | bytes 196616 | tf_op jit(solution)/shard_map/ppermute | solution.py:315
  99.5 7.7 %collective-permute-start.17 = (bf16[256,128]{1,0:T(8,128)(2,1)S(1)}, bf16[256,128]{1,0:T(8,128)(2,1)S(1)}, u32[]{:S(2)}, u32[]{:S(2)}) collective-permute-start(bf16[256,128]{1,0:T(8,128)(2,1)S(1)} %bitcast.36), channel_id=1, source_target_pairs={{0,1},{1,2},{2,3},{3,4},{4,5},{5,6},{6,7},{7,8},{8,9},{9,10},{10,1... | collective-permute-start | bytes 196616 | tf_op jit(solution)/shard_map/ppermute | solution.py:316
  101.5 5.8 %copy-start.8 = (bf16[256,128]{1,0:T(8,128)(2,1)}, bf16[256,128]{1,0:T(8,128)(2,1)S(1)}, u32[]{:S(2)}) copy-start(bf16[256,128]{1,0:T(8,128)(2,1)S(1)} %collective-permute-done.14.g0_ref) | copy-start | bytes 196612
  101.5 5.7 %copy-start.9 = (bf16[256,128]{1,0:T(8,128)(2,1)}, bf16[256,128]{1,0:T(8,128)(2,1)S(1)}, u32[]{:S(2)}) copy-start(bf16[256,128]{1,0:T(8,128)(2,1)S(1)} %collective-permute-done.15.g1_ref) | copy-start | bytes 196612
  101.5 5.7 %copy-start.10 = (bf16[256,128]{1,0:T(8,128)(2,1)}, bf16[256,128]{1,0:T(8,128)(2,1)S(1)}, u32[]{:S(2)}) copy-start(bf16[256,128]{1,0:T(8,128)(2,1)S(1)} %collective-permute-done.16.g2_ref) | copy-start | bytes 196612
  111.6 0.9 copy-start.3
  (3 other events, 1.9 us)

commit v3 on v2

--- a/solution.py
+++ b/solution.py
@@ -33,7 +33,32 @@
     return jnp.where(ids == wide, jnp.ones((), BF), jnp.zeros((), BF))
 
 
-def pick_kernel(feat_ref, rows_ref, *refs):
+def list_order(core, rows_ref):
+    rows = [rows_ref[d : d + 1, :] for d in range(4)]
+    return (rows[0], rows[1], jnp.where(core == 0, rows[2], rows[3]), jnp.where(core == 0, rows[3], rows[2]))
+
+
+def slot_order(core):
+    return (0, 1, 3 - core, 2 + core)
+
+
+def index_kernel(book_ref, code_ref, src_ref, inner_ref, cell_ref):
+    kvol = book_ref.shape[0]
+    blocks, child, quarter = cell_ref.shape[0], 8, BLOCK // 4
+    lane = lax.broadcasted_iota(jnp.int32, (kvol, BLOCK), 1)
+    found = jnp.zeros((kvol, BLOCK), jnp.int32)
+    for b in range(blocks):
+        book = book_ref[:, b * BLOCK : (b + 1) * BLOCK]
+        block = jnp.min(book, axis=1, keepdims=True) // BLOCK
+        inner_ref[b] = (book - block * BLOCK).astype(F32)
+        found = jnp.where(lane == b, block, found)
+        code = code_ref[:, b * BLOCK : (b + 1) * BLOCK]
+        cell = (code % child) * quarter + code // child - b * quarter
+        cell_ref[b : b + 1, :] = jnp.where(code < child * quarter * blocks, cell, -1).astype(F32)
+    src_ref[...] = found
+
+
+def pick_kernel(core_ref, feat_ref, rows_ref, *refs):
     out_refs, xt_ref, full_ref, hot_ref = refs[:-3], refs[-3], refs[-2], refs[-1]
     blocks = feat_ref.shape[0] // BLOCK
     length = rows_ref.shape[1]
@@ -42,9 +67,9 @@
         xt_ref[b] = block
         full_ref[:, b * BLOCK : (b + 1) * BLOCK] = block
     ids = sub_iota(BLOCK, BF)
-    for d, out_ref in enumerate(out_refs):
+    for rows, out_ref in zip(list_order(core_ref[0], rows_ref), out_refs):
         for g in range(length // BLOCK):
-            row = rows_ref[d : d + 1, g * BLOCK : (g + 1) * BLOCK]
+            row = rows[:, g * BLOCK : (g + 1) * BLOCK]
             for b in range(blocks):
                 hot_ref[b * BLOCK : (b + 1) * BLOCK, g * BLOCK : (g + 1) * BLOCK] = onehot_t(
                     (row - b * BLOCK).astype(F32), ids
@@ -73,7 +98,8 @@
         xt_ref[b] = xt_loc_ref[b]
     for b in range(far):
         one = b % each
-        xt_ref[blocks + b] = recv_refs[b // each][one * BLOCK : (one + 1) * BLOCK, :].T
+        slot = slot_order(core_ref[0])[b // each]
+        xt_ref[blocks + each * slot + one] = recv_refs[b // each][one * BLOCK : (one + 1) * BLOCK, :].T
     xt_ref[blocks + far] = jnp.zeros((BLOCK, BLOCK), BF)
     for j in range(child):
         part = mm(cg_ref[...], dw_ref[j], NT).astype(BF)
@@ -86,7 +112,7 @@
         for k in range(kvol):
             for h in range(2):
                 b = 2 * p + h
-                hot = onehot_t(book_ref[k, pl.ds(b, 1), :], ids)
+                hot = onehot_t(book_ref[b, k : k + 1, :], ids)
                 got = mm(xt_ref[src_ref[k, b]], hot)
                 gt_ref[k * BLOCK : (k + 1) * BLOCK, h * BLOCK : (h + 1) * BLOCK] = got.astype(BF)
         pre = mm(wt_ref[...], gt_ref[...])
@@ -120,14 +146,16 @@
     give_ref[...] = part_ref[pl.ds(pl.multiple_of((1 - core) * half, half), half), :]
 
 
-def back_kernel(lo, hi, src_ref, book_ref, wt_ref, pg_ref, *refs):
-    if lo == 0:
-        table_ref, back_ref = refs
-        table_ref[...] = jnp.zeros_like(table_ref)
+def back_kernel(lo, hi, pairs, src_ref, core_ref, book_ref, wt_ref, pg_ref, *refs):
+    refs, back_ref = refs[:-1], refs[-1]
+    if lo > 0:
+        before_ref, refs = refs[0], refs[1:]
+    if hi < pairs:
+        (table_ref,) = refs
     else:
-        before_ref, table_ref, back_ref = refs
-        table_ref[...] = before_ref[...]
-    kvol = book_ref.shape[0]
+        local_ref, *far_refs, table_ref = refs
+    table_ref[...] = jnp.zeros_like(table_ref) if lo == 0 else before_ref[...]
+    kvol = book_ref.shape[1]
     ids = sub_iota(BLOCK, BF)
 
     @pl.loop(lo, hi)
@@ -136,24 +164,40 @@
         for k in range(kvol):
             for h in range(2):
                 b = 2 * p + h
-                hot = onehot_t(book_ref[k, pl.ds(b, 1), :], ids)
+                hot = onehot_t(book_ref[b, k : k + 1, :], ids)
                 table_ref[src_ref[k, b]] += mm(
                     hot, back_ref[h * BLOCK : (h + 1) * BLOCK, k * BLOCK : (k + 1) * BLOCK]
                 )
 
-
-def add_kernel(table_ref, rows_ref, g0_ref, g1_ref, g2_ref, g3_ref, out_ref, ret_ref):
+    if hi == pairs:
+        blocks = local_ref.shape[0] // BLOCK
+        for b in range(blocks):
+            local_ref[b * BLOCK : (b + 1) * BLOCK, :] = table_ref[b]
+        for slot, far_ref in zip(slot_order(core_ref[0]), far_refs):
+            each = far_ref.shape[0] // BLOCK
+            for one in range(each):
+                far_ref[one * BLOCK : (one + 1) * BLOCK, :] = table_ref[blocks + each * slot + one].astype(BF)
+
+
+def add_kernel(info_ref, local_ref, rows_ref, g0_ref, g1_ref, g2_ref, g3_ref, out_ref, ret_ref):
     blocks = out_ref.shape[0] // BLOCK
-    lists, length = rows_ref.shape
+    length = rows_ref.shape[1]
     ids = sub_iota(BLOCK, BF)
-    for d, got_ref in enumerate((g0_ref, g1_ref, g2_ref, g3_ref)):
-        ret_ref[d * length : (d + 1) * length, :] = got_ref[...]
+    nothing = jnp.zeros((length, BLOCK), BF)
+    slab = info_ref[1]
+    ret_ref[0:length, :] = jnp.where(slab < info_ref[2] - 1, g0_ref[...], nothing)
+    ret_ref[length : 2 * length, :] = jnp.where(slab > 0, g1_ref[...], nothing)
+    ret_ref[2 * length : 3 * length, :] = g2_ref[...]
+    ret_ref[3 * length :, :] = g3_ref[...]
     groups = [
-        rows_ref[d : d + 1, g * BLOCK : (g + 1) * BLOCK] for d in range(lists) for g in range(length // BLOCK)
+        rows[:, g * BLOCK : (g + 1) * BLOCK]
+        for rows in list_order(info_ref[0], rows_ref)
+        for g in range(length // BLOCK)
     ]
     for b in range(blocks):
         hot = jnp.concatenate([onehot_t((row - b * BLOCK).astype(F32), ids) for row in groups], axis=1)
-        out_ref[b * BLOCK : (b + 1) * BLOCK, :] = table_ref[b] + mm(hot, ret_ref[...])
+        spot = slice(b * BLOCK, (b + 1) * BLOCK)
+        out_ref[spot, :] = local_ref[spot, :] + mm(hot, ret_ref[...])
 
 
 def spread_kernel(core_ref, own_ref, other_ref, conv_ref, down_ref):
@@ -174,9 +218,13 @@
         put(other_ref, own_ref)
 
 
+def here(x):
+    return pltpu.with_memory_space_constraint(x, pltpu.VMEM)
+
+
 def call(kernel, outs, ins, scratch=(), aliases=None):
     single = len(outs) == 1
-    shapes = tuple(jax.ShapeDtypeStruct(s, d) for s, d in outs)
+    shapes = tuple((jax.ShapeDtypeStruct if not near else pltpu.VMEM)(s, d) for s, d, *near in outs)
     return pl.pallas_call(
         kernel,
         out_shape=shapes[0] if single else shapes,
@@ -209,41 +257,42 @@
     slabs, tiles = lax.axis_size("slab"), lax.axis_size("tile")
     place = lax.axis_index("slab") * tiles + lax.axis_index("tile")
     core = place & 1
-
+    info = jnp.stack([core, lax.axis_index("slab"), jnp.int32(slabs)])
+
+    near = True
     *outgoing, xt = call(
         pick_kernel,
-        [((list_len, chans), BF)] * 4 + [((blocks, BLOCK, BLOCK), BF)],
+        [((list_len, chans), BF, near)] * 4 + [((blocks, BLOCK, BLOCK), BF, near)],
+        [SM, VM, VM],
+        [pltpu.VMEM((BLOCK, row_count), BF), pltpu.VMEM((row_count, list_len), BF)],
+    )(info, features, boundary_rows)
+    up = [(i, i + 1) for i in range(slabs - 1)]
+    down = [(i + 1, i) for i in range(slabs - 1)]
+    chip = [(i, i ^ 1) for i in range(tiles)]
+    beside = [(i, i + 2 * (i % 2) - 1) for i in range(1, tiles - 1)]
+    received = [
+        lax.ppermute(outgoing[0], "slab", up),
+        lax.ppermute(outgoing[1], "slab", down),
+        lax.ppermute(outgoing[2], "tile", chip),
+        lax.ppermute(outgoing[3], "tile", beside),
+    ]
+    source, inner, cell = call(
+        index_kernel,
+        [((kvol, BLOCK), jnp.int32), ((blocks, kvol, BLOCK), F32, near), ((blocks, BLOCK), F32, near)],
         [VM, VM],
-        [pltpu.VMEM((BLOCK, row_count), BF), pltpu.VMEM((row_count, list_len), BF)],
-    )(features, boundary_rows)
-    up = {"slab": [(i, i + 1) for i in range(slabs - 1)], "tile": [(i, i + 1) for i in range(tiles - 1)]}
-    down = {a: [(j, i) for i, j in links] for a, links in up.items()}
-    received = [
-        lax.ppermute(outgoing[0], "slab", up["slab"]),
-        lax.ppermute(outgoing[1], "slab", down["slab"]),
-        lax.ppermute(outgoing[2], "tile", up["tile"]),
-        lax.ppermute(outgoing[3], "tile", down["tile"]),
-    ]
-
-    book = rulebook.reshape(kvol, blocks, BLOCK)
-    source = jnp.min(book, axis=2) // BLOCK
-    inner = (book - source[:, :, None] * BLOCK).astype(F32)
-    code = parent_code.reshape(blocks, BLOCK)
-    cell = (code % child) * quarter + code // child - jnp.arange(blocks, dtype=jnp.int32)[:, None] * quarter
-    cell = jnp.where(code < child * coarse_rows, cell, -1).astype(F32)
+    )(rulebook, parent_code.reshape(1, row_count))
 
     grad_rows = (kvol + child) * BLOCK
     part_rows = -(-grad_rows // 512) * 512
     table = blocks + far_rows // BLOCK + 1
-    core_one = core.reshape(1)
     coarse, pg, wt, keep, give = call(
         main_kernel,
         [
             ((coarse_rows, out_chans), BF),
-            ((pairs, 2 * BLOCK, BLOCK), BF),
-            ((BLOCK, kvol * BLOCK), BF),
-            ((part_rows // 2, out_chans), BF),
-            ((part_rows // 2, out_chans), BF),
+            ((pairs, 2 * BLOCK, BLOCK), BF, near),
+            ((BLOCK, kvol * BLOCK), BF, near),
+            ((part_rows // 2, out_chans), BF, near),
+            ((part_rows // 2, out_chans), BF, near),
         ],
         [SM, SM] + [VM] * 10,
         [
@@ -254,16 +303,19 @@
             pltpu.VMEM((coarse_rows, child * BLOCK), BF),
             pltpu.VMEM((part_rows, BLOCK), BF),
         ],
-    )(source, core_one, xt, *received, inner, cell, conv_weight, down_weight, coarse_grad)
+    )(source, info, here(xt), *map(here, received), here(inner), here(cell), conv_weight, down_weight, coarse_grad)
 
     def back_part(acc, lo, hi):
-        ins = (source, inner, wt, pg) + (() if acc is None else (acc,))
+        ins = (source, info, here(inner), here(wt), here(pg)) + (() if acc is None else (here(acc),))
+        whole = ((table, BLOCK, BLOCK), F32, near)
+        scratch = [pltpu.VMEM((2 * BLOCK, kvol * BLOCK), BF)]
+        if hi < pairs:
+            outs = [whole]
+        else:
+            outs = [((row_count, chans), F32, near)] + [((list_len, chans), BF, near)] * 4
+            scratch = [pltpu.VMEM(*whole[:2])] + scratch
         return call(
-            functools.partial(back_kernel, lo, hi),
-            [((table, BLOCK, BLOCK), F32)],
-            [SM] + [VM] * (len(ins) - 1),
-            [pltpu.VMEM((2 * BLOCK, kvol * BLOCK), BF)],
-            aliases={} if acc is None else {4: 0},
+            functools.partial(back_kernel, lo, hi, pairs), outs, [SM, SM] + [VM] * (len(ins) - 2), scratch
         )(*ins)
 
     stride = {"c": 1, "z": 2, "y": 8, "x": tiles}
@@ -285,7 +337,7 @@
     def shifts(axes, pieces):
         return [send(v, axes, lambda q, sh=sh: q + sh) for sh, v in zip((1, 2, 3), pieces)]
 
-    order = ("xy", "yz", "zx", "xy")
+    order = ("xx", "yz", "zy", "xx")
     swap = send(give, "cc", lambda q: 1 - q)
     acc = back_part(None, 0, 2)
     swap, acc = tie(swap, acc)
@@ -301,32 +353,35 @@
     for ph, (lo, hi) in ((1, (4, 6)), (2, (6, 8))):
         y, acc = tie(y, acc)
         got = shifts(order[ph], [y] * 3)
-        acc = back_part(acc, lo, hi)
-        *got, acc = tie(*got, acc)
+        result = back_part(acc, lo, hi)
+        if hi < pairs:
+            acc = result
+            *got, acc = tie(*got, acc)
+        else:
+            *got, local, far0, far1, far2, far3 = tie(*got, *result)
         y = ((wide(y) + wide(got[1])) + (wide(got[0]) + wide(got[2]))).astype(BF)
 
-    y, acc = tie(y, acc)
     i = spot(order[3])
-    got = shifts(order[3], [y] * 3)
-    far = acc[blocks : table - 1].astype(BF).reshape(4, list_len, chans)
+    got = shifts(order[3], [jnp.concatenate([y, far1]), y, jnp.concatenate([y, far0])])
     returned = [
-        lax.ppermute(far[0], "slab", down["slab"]),
-        lax.ppermute(far[1], "slab", up["slab"]),
-        lax.ppermute(far[2], "tile", down["tile"]),
-        lax.ppermute(far[3], "tile", up["tile"]),
+        got[2][m:],
+        got[0][m:],
+        lax.ppermute(far2, "tile", chip),
+        lax.ppermute(far3, "tile", beside),
     ]
+    got = [got[0][:m], got[1], got[2][:m]]
     full = jnp.zeros((4 * m, out_chans), BF)
     for sh, v in zip((0, 1, 2, 3), [y] + got):
         full = lax.dynamic_update_slice_in_dim(full, v, ((i + 4 - sh) & 3) * m, 0)
     other = send(full, "cc", lambda q: 1 - q)
     input_grad = call(
-        add_kernel, [((row_count, chans), F32)], [VM] * 6, [pltpu.VMEM((far_rows, chans), BF)]
-    )(acc, boundary_rows, *returned)
+        add_kernel, [((row_count, chans), F32)], [SM] + [VM] * 6, [pltpu.VMEM((far_rows, chans), BF)]
+    )(info, here(local), boundary_rows, *map(here, returned))
     conv_grad, down_grad = call(
         spread_kernel,
         [((kvol * BLOCK, out_chans), F32), ((child * BLOCK, out_chans), F32)],
         [SM, VM, VM],
-    )(core_one, full, other)
+    )(info, here(full), here(other))
     return (
         coarse,
         input_grad,

time: 116 us -> 104 us (0.90)
  Pallas kernels: 52.8 us -> 43.7 us
  starting transfers between devices: 43.8 us -> 37.1 us
  waiting for transfers between devices: 11 us -> 14.5 us
    ppermute x8 -> x6, starting transfers between devices: 23.8 us -> 14.4 us  [the longest x1 5.92 us: body(): lax.ppermute(outgoing[3], 'tile', beside)]
    pallas_call x6 -> x7, Pallas kernels: 28.5 us -> 20.6 us  [the longest x4 13.1 us: back_part(): call(functools.partial(back_kernel, lo, hi, pairs), outs, [SM, SM] + [VM]...]
    ppermute x14, waiting for transfers between devices: 5.3 us -> 10.1 us  [send(): return lax.ppermute(v, ('slab', 'tile'), links)]
    ppermute x14, starting transfers between devices: 20 us -> 22.7 us  [send(): return lax.ppermute(v, ('slab', 'tile'), links)]
    unnamed x27 -> x6, local copies, waits for them, and re-layouts: 3.16 us -> 1.63 us
    convert_element_type x2 -> x0, other arithmetic: 1.47 us -> none  [the longest x1 0.8 us: body(): inner = (book - source[:, :, None] * BLOCK).astype(F32)]
    ppermute x8 -> x6, waiting for transfers between devices: 5.72 us -> 4.41 us  [the longest x1 4.39 us: body(): lax.ppermute(far3, 'tile', beside)]
    dynamic_update_slice x0 -> x1, other arithmetic: none -> 1.17 us  [body(): full = lax.dynamic_update_slice_in_dim(full, v, (i + 4 - sh & 3) * m, 0)]
  transfers between devices with their start and end apart: 22 -> 20, of which waited for: 3 -> 8; matrix products, arithmetic and copies ran while one was open for 3% -> 0% of each run, Pallas kernels for 22% -> 18%
where the time goes in v3:
time: 104 us; the launch traced here: 103 us
  Pallas kernels  43.7 us (42%)
  starting transfers between devices  37.1 us (36%)
  waiting for transfers between devices  14.5 us (14%)
  other arithmetic  4.19 us (4%)
  local copies, waits for them, and re-layouts  2.54 us (2%)
    ppermute x14, starting transfers between devices, send(): return lax.ppermute(v, ('slab', 'tile'), links)  22.7 us
    pallas_call x1, Pallas kernels, body(): call(main_kernel, [((coarse_rows, out_chans), BF), ((pairs, 2 * BLOCK, BL...  20.9 us
    pallas_call x4, Pallas kernels, back_part(): call(functools.partial(back_kernel, lo, hi, pairs), outs, [SM, SM] + [VM]...  13.1 us
    ppermute x14, waiting for transfers between devices, send(): return lax.ppermute(v, ('slab', 'tile'), links)  10.1 us
    ppermute x1, starting transfers between devices, body(): lax.ppermute(outgoing[3], 'tile', beside)  5.92 us
    ppermute x1, waiting for transfers between devices, body(): lax.ppermute(far3, 'tile', beside)  4.39 us
    ppermute x1, starting transfers between devices, body(): lax.ppermute(outgoing[0], 'slab', up)  3.4 us
    ppermute x1, starting transfers between devices, body(): lax.ppermute(far3, 'tile', beside)  3.24 us
  transfers between devices with their start and end apart: 20, of which 8 were waited for; matrix products, arithmetic and copies ran while one was open for 0% of the time, Pallas kernels for 18%

profile of v3, /device:TPU:8, one launch (start us, length us, event | category | flops | bytes accessed | tf_op | source)
XLA Modules:
  0.0 102.9 jit_solution(7185108984724908688)
XLA Ops:
  1.2 2.5 %shard_map.103 = (bf16[256,128]{1,0:T(8,128)(2,1)S(1)}, bf16[256,128]{1,0:T(8,128)(2,1)S(1)}, bf16[256,128]{1,0:T(8,128)(2,1)S(1)}, bf16[256,128]{1,0:T(8,128)(2,1)S(1)}, bf16[16,128,128]{2,1,0:T(8,128)(2,1)S(1)}) custom-call(s32[3]{0:T(128)} %pad_add_fusion.core_ref.info_ref, bf16[2048,128]{1,0:T(8,128)(2,1)} %feat_ref.1, s32[4,256]{1,0:T(4,128)} %rows_ref.3), custom_call_target="tpu_custom_call" | custom-call | tf_op jit(solution)/shard_map/pallas_call | solution.py:263
  3.8 3.4 %collective-permute-start = (bf16[256,128]{1,0:T(8,128)(2,1)S(1)}, bf16[256,128]{1,0:T(8,128)(2,1)S(1)}, u32[]{:S(2)}, u32[]{:S(2)}) collective-permute-start(bf16[256,128]{1,0:T(8,128)(2,1)S(1)} %get-tuple-element.48), channel_id=1, source_target_pairs={{0,32},{32,64},{64,96},{1,33},{33,65},{65,97},{2,34},{34,66},{66,9... | collective-permute-start | bytes 196616 | tf_op jit(solution)/shard_map/ppermute | solution.py:274
  7.2 1.3 %collective-permute-start.1 = (bf16[256,128]{1,0:T(8,128)(2,1)S(1)}, bf16[256,128]{1,0:T(8,128)(2,1)S(1)}, u32[]{:S(2)}, u32[]{:S(2)}) collective-permute-start(bf16[256,128]{1,0:T(8,128)(2,1)S(1)} %get-tuple-element.49), channel_id=1, source_target_pairs={{32,0},{64,32},{96,64},{33,1},{65,33},{97,65},{34,2},{66,34},{98,6... | collective-permute-start | bytes 196616 | tf_op jit(solution)/shard_map/ppermute | solution.py:275
  8.6 5.9 %collective-permute-start.3 = (bf16[256,128]{1,0:T(8,128)(2,1)S(1)}, bf16[256,128]{1,0:T(8,128)(2,1)S(1)}, u32[]{:S(2)}, u32[]{:S(2)}) collective-permute-start(bf16[256,128]{1,0:T(8,128)(2,1)S(1)} %get-tuple-element.51), channel_id=1, source_target_pairs={{1,2},{2,1},{3,4},{4,3},{5,6},{6,5},{7,8},{8,7},{9,10},{10,9},{11,... | collective-permute-start | bytes 196616 | tf_op jit(solution)/shard_map/ppermute | solution.py:277
  14.5 2.0 %shard_map.102 = (s32[27,128]{1,0:T(8,128)}, f32[16,27,128]{2,1,0:T(8,128)S(1)}, f32[16,128]{1,0:T(8,128)S(1)}) custom-call(s32[27,2048]{1,0:T(8,128)} %book_ref.1, s32[1,2048]{1,0:T(1,128)} %bitcast.5), custom_call_target="tpu_custom_call" | custom-call | tf_op jit(solution)/shard_map/pallas_call | solution.py:279
  16.5 20.9 %shard_map.104 = (bf16[512,128]{1,0:T(8,128)(2,1)}, bf16[8,256,128]{2,1,0:T(8,128)(2,1)S(1)}, bf16[128,3456]{1,0:T(8,128)(2,1)S(1)}, bf16[2304,128]{1,0:T(8,128)(2,1)S(1)}, bf16[2304,128]{1,0:T(8,128)(2,1)}) custom-call(s32[27,128]{1,0:T(8,128)} %get-tuple-element.46.src_ref, s32[3]{0:T(128)} %pad_add_fusion.core_ref.info_ref, ...), custom_call_target="tpu_custom_call" | custom-call | tf_op jit(solution)/shard_map/pallas_call | solution.py:288
  38.2 3.4 %shard_map.105.refs_0_ = f32[25,128,128]{2,1,0:T(8,128)S(1)} custom-call(s32[27,128]{1,0:T(8,128)} %get-tuple-element.46.src_ref, s32[3]{0:T(128)} %pad_add_fusion.core_ref.info_ref, f32[16,27,128]{2,1,0:T(8,128)S(1)} %get-tuple-element.52.book_ref, bf16[128,3456]{1,0:T(8,128)(2,1)S(1)} %get-tuple-element.57.wt_ref, ...), custom_call_target="tpu_custom_call" | custom-call | tf_op jit(solution)/shard_map/pallas_call | solution.py:317
  41.6 1.2 %add_convert_fusion = bf16[2304,128]{1,0:T(8,128)(2,1)S(1)} fusion(bf16[2304,128]{1,0:T(8,128)(2,1)} %collective-permute-done.4, bf16[2304,128]{1,0:T(8,128)(2,1)S(1)} %copy-done.1), kind=kLoop, calls=%fused_computation | loop fusion | flops 1179648 | bytes 1769472 | tf_op jit(solution)/shard_map/convert_element_type | solution.py:344
  44.4 2.6 %collective-permute-start.5 = (bf16[576,128]{1,0:T(8,128)(2,1)}, bf16[576,128]{1,0:T(8,128)(2,1)S(1)}, u32[]{:S(2)}, u32[]{:S(2)}) collective-permute-start(bf16[576,128]{1,0:T(8,128)(2,1)} %get-tuple-element.92), channel_id=1, source_target_pairs={{0,32},{1,33},{2,34},{3,35},{4,36},{5,37},{6,38},{7,39},{8,40},{9,... | collective-permute-start | bytes 442376 | tf_op jit(solution)/shard_map/ppermute | solution.py:331
  47.0 2.7 %collective-permute-start.6 = (bf16[576,128]{1,0:T(8,128)(2,1)}, bf16[576,128]{1,0:T(8,128)(2,1)}, u32[]{:S(2)}, u32[]{:S(2)}) collective-permute-start(bf16[576,128]{1,0:T(8,128)(2,1)} %get-tuple-element.91), channel_id=1, source_target_pairs={{0,64},{1,65},{2,66},{3,67},{4,68},{5,69},{6,70},{7,71},{8,72},{9,... | collective-permute-start | bytes 442376 | tf_op jit(solution)/shard_map/ppermute | solution.py:331
  49.8 1.4 %collective-permute-start.7 = (bf16[576,128]{1,0:T(8,128)(2,1)}, bf16[576,128]{1,0:T(8,128)(2,1)}, u32[]{:S(2)}, u32[]{:S(2)}) collective-permute-start(bf16[576,128]{1,0:T(8,128)(2,1)} %get-tuple-element.90), channel_id=1, source_target_pairs={{0,96},{1,97},{2,98},{3,99},{4,100},{5,101},{6,102},{7,103},{8,104... | collective-permute-start | bytes 442376 | tf_op jit(solution)/shard_map/ppermute | solution.py:331
  51.2 3.2 %shard_map.106.refs_0_ = f32[25,128,128]{2,1,0:T(8,128)S(1)} custom-call(s32[27,128]{1,0:T(8,128)} %get-tuple-element.46.src_ref, s32[3]{0:T(128)} %pad_add_fusion.core_ref.info_ref, f32[16,27,128]{2,1,0:T(8,128)S(1)} %get-tuple-element.52.book_ref, bf16[128,3456]{1,0:T(8,128)(2,1)S(1)} %get-tuple-element.57.wt_ref, ...), custom_call_target="tpu_custom_call" | custom-call | tf_op jit(solution)/shard_map/pallas_call | solution.py:317
  54.4 3.0 %collective-permute-done.6 = bf16[576,128]{1,0:T(8,128)(2,1)} collective-permute-done((bf16[576,128]{1,0:T(8,128)(2,1)}, bf16[576,128]{1,0:T(8,128)(2,1)}, u32[]{:S(2)}, u32[]{:S(2)}) %collective-permute-start.6) | collective-permute-done | bytes 147488 | tf_op jit(solution)/shard_map/ppermute | solution.py:331
  57.5 1.1 %add_convert_fusion.3 = bf16[576,128]{1,0:T(8,128)(2,1)S(1)} fusion(bf16[576,128]{1,0:T(8,128)(2,1)} %collective-permute-done.7, bf16[576,128]{1,0:T(8,128)(2,1)S(1)} %collective-permute-done.5, bf16[576,128]{1,0:T(8,128)(2,1)} %collective-permute-done.6, bf16[2304,128]{1,0:T(8,128)(2,1)} %copy-done.2, s32[]{:T(128)S(6)} %select_n.21), kind=kLoop, calls=%fused_computation.3 | loop fusion | flops 589824 | bytes 737284 | tf_op jit(solution)/shard_map/convert_element_type | solution.py:351
  58.6 1.6 %collective-permute-start.8 = (bf16[576,128]{1,0:T(8,128)(2,1)S(1)}, bf16[576,128]{1,0:T(8,128)(2,1)S(1)}, u32[]{:S(2)}, u32[]{:S(2)}) collective-permute-start(bf16[576,128]{1,0:T(8,128)(2,1)S(1)} %add_convert_fusion.3), channel_id=1, source_target_pairs={{0,8},{1,3},{2,10},{3,5},{4,12},{5,7},{6,14},{7,1},{8,16},{9,11},{... | collective-permute-start | bytes 442376 | tf_op jit(solution)/shard_map/ppermute | solution.py:331
  60.2 1.1 %collective-permute-start.9 = (bf16[576,128]{1,0:T(8,128)(2,1)S(1)}, bf16[576,128]{1,0:T(8,128)(2,1)S(1)}, u32[]{:S(2)}, u32[]{:S(2)}) collective-permute-start(bf16[576,128]{1,0:T(8,128)(2,1)S(1)} %add_convert_fusion.3), channel_id=1, source_target_pairs={{0,16},{1,5},{2,18},{3,7},{4,20},{5,1},{6,22},{7,3},{8,24},{9,13},... | collective-permute-start | bytes 442376 | tf_op jit(solution)/shard_map/ppermute | solution.py:331
  61.4 2.5 %collective-permute-start.10 = (bf16[576,128]{1,0:T(8,128)(2,1)S(1)}, bf16[576,128]{1,0:T(8,128)(2,1)S(1)}, u32[]{:S(2)}, u32[]{:S(2)}) collective-permute-start(bf16[576,128]{1,0:T(8,128)(2,1)S(1)} %add_convert_fusion.3), channel_id=1, source_target_pairs={{0,24},{1,7},{2,26},{3,1},{4,28},{5,3},{6,30},{7,5},{8,0},{9,15},{... | collective-permute-start | bytes 442376 | tf_op jit(solution)/shard_map/ppermute | solution.py:331
  63.9 3.2 %shard_map.107.refs_0_ = f32[25,128,128]{2,1,0:T(8,128)S(1)} custom-call(s32[27,128]{1,0:T(8,128)} %get-tuple-element.46.src_ref, s32[3]{0:T(128)} %pad_add_fusion.core_ref.info_ref, f32[16,27,128]{2,1,0:T(8,128)S(1)} %get-tuple-element.52.book_ref, bf16[128,3456]{1,0:T(8,128)(2,1)S(1)} %get-tuple-element.57.wt_ref, ...), custom_call_target="tpu_custom_call" | custom-call | tf_op jit(solution)/shard_map/pallas_call | solution.py:317
  67.2 0.9 collective-permute-done.10
  68.3 5.1 %collective-permute-start.12 = (bf16[576,128]{1,0:T(8,128)(2,1)S(1)}, bf16[576,128]{1,0:T(8,128)(2,1)}, u32[]{:S(2)}, u32[]{:S(2)}) collective-permute-start(bf16[576,128]{1,0:T(8,128)(2,1)S(1)} %add_convert_fusion.2), channel_id=1, source_target_pairs={{0,4},{1,17},{2,6},{3,19},{4,0},{5,21},{6,2},{7,23},{8,12},{9,25},... | collective-permute-start | bytes 442376 | tf_op jit(solution)/shard_map/ppermute | solution.py:331
  73.3 3.3 %shard_map.108 = (f32[2048,128]{1,0:T(8,128)S(1)}, bf16[256,128]{1,0:T(8,128)(2,1)S(1)}, bf16[256,128]{1,0:T(8,128)(2,1)S(1)}, bf16[256,128]{1,0:T(8,128)(2,1)S(1)}, bf16[256,128]{1,0:T(8,128)(2,1)S(1)}) custom-call(s32[27,128]{1,0:T(8,128)} %get-tuple-element.46.src_ref, s32[3]{0:T(128)} %pad_add_fusion.core_ref.info_ref, ...), custom_call_target="tpu_custom_call" | custom-call | tf_op jit(solution)/shard_map/pallas_call | solution.py:317
  76.7 1.5 %collective-permute-done.12 = bf16[576,128]{1,0:T(8,128)(2,1)} collective-permute-done((bf16[576,128]{1,0:T(8,128)(2,1)S(1)}, bf16[576,128]{1,0:T(8,128)(2,1)}, u32[]{:S(2)}, u32[]{:S(2)}) %collective-permute-start.12) | collective-permute-done | bytes 147488 | tf_op jit(solution)/shard_map/ppermute | solution.py:331
  78.6 1.2 %constant_dynamic-update-slice_fusion.1 = (bf16[2304,128]{1,0:T(8,128)(2,1)S(1)}, bf16[576,128]{1,0:T(8,128)(2,1)S(1)}) fusion(bf16[2304,128]{1,0:T(8,128)(2,1)S(1)} %broadcast_in_dim.3, s32[]{:T(128)S(6)} %select_n.25, bf16[576,128]{1,0:T(8,128)(2,1)} %collective-permute-done.13, bf16[576,128]{1,0:T(8,128)(2,1)} %collective-permute-done.11, ...), kind=kLoop, calls=%fused_computation.9 | loop fusion | flops 589824 | bytes 884740 | tf_op jit(solution)/shard_map/dynamic_update_slice | solution.py:375
  79.9 1.2 %collective-permute-start.15 = (bf16[832,128]{1,0:T(8,128)(2,1)S(1)}, bf16[832,128]{1,0:T(8,128)(2,1)S(1)}, u32[]{:S(2)}, u32[]{:S(2)}) collective-permute-start(bf16[832,128]{1,0:T(8,128)(2,1)S(1)} %get-tuple-element.93), channel_id=1, source_target_pairs={{0,32},{1,33},{2,34},{3,35},{4,36},{5,37},{6,38},{7,39},{8,40},{9,... | collective-permute-start | bytes 638984 | tf_op jit(solution)/shard_map/ppermute | solution.py:331
  81.1 2.4 %collective-permute-start.18 = (bf16[576,128]{1,0:T(8,128)(2,1)S(1)}, bf16[576,128]{1,0:T(8,128)(2,1)S(1)}, u32[]{:S(2)}, u32[]{:S(2)}) collective-permute-start(bf16[576,128]{1,0:T(8,128)(2,1)S(1)} %get-tuple-element.89), channel_id=1, source_target_pairs={{0,64},{1,65},{2,66},{3,67},{4,68},{5,69},{6,70},{7,71},{8,72},{9,... | collective-permute-start | bytes 442376 | tf_op jit(solution)/shard_map/ppermute | solution.py:331
  83.5 1.8 %collective-permute-start.14 = (bf16[832,128]{1,0:T(8,128)(2,1)S(1)}, bf16[832,128]{1,0:T(8,128)(2,1)S(1)}, u32[]{:S(2)}, u32[]{:S(2)}) collective-permute-start(bf16[832,128]{1,0:T(8,128)(2,1)S(1)} %get-tuple-element.94), channel_id=1, source_target_pairs={{0,96},{1,97},{2,98},{3,99},{4,100},{5,101},{6,102},{7,103},{8,104... | collective-permute-start | bytes 638984 | tf_op jit(solution)/shard_map/ppermute | solution.py:331
  85.2 1.8 %collective-permute-done.15 = bf16[832,128]{1,0:T(8,128)(2,1)S(1)} collective-permute-done((bf16[832,128]{1,0:T(8,128)(2,1)S(1)}, bf16[832,128]{1,0:T(8,128)(2,1)S(1)}, u32[]{:S(2)}, u32[]{:S(2)}) %collective-permute-start.15) | collective-permute-done | bytes 213024 | tf_op jit(solution)/shard_map/ppermute | solution.py:331
  87.0 1.8 %collective-permute-done.18 = bf16[576,128]{1,0:T(8,128)(2,1)S(1)} collective-permute-done((bf16[576,128]{1,0:T(8,128)(2,1)S(1)}, bf16[576,128]{1,0:T(8,128)(2,1)S(1)}, u32[]{:S(2)}, u32[]{:S(2)}) %collective-permute-start.18) | collective-permute-done | bytes 147488 | tf_op jit(solution)/shard_map/ppermute | solution.py:331
  90.0 3.2 %collective-permute-start.17 = (bf16[256,128]{1,0:T(8,128)(2,1)S(1)}, bf16[256,128]{1,0:T(8,128)(2,1)S(1)}, u32[]{:S(2)}, u32[]{:S(2)}) collective-permute-start(bf16[256,128]{1,0:T(8,128)(2,1)S(1)} %get-tuple-element.85), channel_id=1, source_target_pairs={{1,2},{2,1},{3,4},{4,3},{5,6},{6,5},{7,8},{8,7},{9,10},{10,9},{11,... | collective-permute-start | bytes 196616 | tf_op jit(solution)/shard_map/ppermute | solution.py:370
  93.3 4.4 %collective-permute-done.17.g3_ref = bf16[256,128]{1,0:T(8,128)(2,1)S(1)} collective-permute-done((bf16[256,128]{1,0:T(8,128)(2,1)S(1)}, bf16[256,128]{1,0:T(8,128)(2,1)S(1)}, u32[]{:S(2)}, u32[]{:S(2)}) %collective-permute-start.17) | collective-permute-done | bytes 65568 | tf_op jit(solution)/shard_map/ppermute | solution.py:370
  97.7 2.9 %shard_map.109 = f32[2048,128]{1,0:T(8,128)} custom-call(s32[3]{0:T(128)} %pad_add_fusion.core_ref.info_ref, f32[2048,128]{1,0:T(8,128)S(1)} %get-tuple-element.78.local_ref, s32[4,256]{1,0:T(4,128)} %rows_ref.3, bf16[256,128]{1,0:T(8,128)(2,1)S(1)} %slice.16.g0_ref, bf16[256,128]{1,0:T(8,128)(2,1)S(1)} %slice.17.g1_ref, ...), custom_call_target="tpu_custom_call" | custom-call | tf_op jit(solution)/shard_map/pallas_call | solution.py:377
  100.7 2.2 %shard_map.110 = (f32[3456,128]{1,0:T(8,128)}, f32[1024,128]{1,0:T(8,128)}) custom-call(s32[3]{0:T(128)} %pad_add_fusion.core_ref.info_ref, bf16[2304,128]{1,0:T(8,128)(2,1)S(1)} %slice_dynamic-update-slice_fusion.own_ref, bf16[2304,128]{1,0:T(8,128)(2,1)S(1)} %collective-permute-done.19.other_ref), custom_call_target="tpu_custom_call" | custom-call | tf_op jit(solution)/shard_map/pallas_call | solution.py:380
  (36 shorter events, 5.0 us)
Async XLA Ops:
  3.8 12.7 %collective-permute-start = (bf16[256,128]{1,0:T(8,128)(2,1)S(1)}, bf16[256,128]{1,0:T(8,128)(2,1)S(1)}, u32[]{:S(2)}, u32[]{:S(2)}) collective-permute-start(bf16[256,128]{1,0:T(8,128)(2,1)S(1)} %get-tuple-element.48), channel_id=1, source_target_pairs={{0,32},{32,64},{64,96},{1,33},{33,65},{65,97},{2,34},{34,66},{66,9... | collective-permute-start | bytes 196616 | tf_op jit(solution)/shard_map/ppermute | solution.py:274
  7.2 9.3 %collective-permute-start.1 = (bf16[256,128]{1,0:T(8,128)(2,1)S(1)}, bf16[256,128]{1,0:T(8,128)(2,1)S(1)}, u32[]{:S(2)}, u32[]{:S(2)}) collective-permute-start(bf16[256,128]{1,0:T(8,128)(2,1)S(1)} %get-tuple-element.49), channel_id=1, source_target_pairs={{32,0},{64,32},{96,64},{33,1},{65,33},{97,65},{34,2},{66,34},{98,6... | collective-permute-start | bytes 196616 | tf_op jit(solution)/shard_map/ppermute | solution.py:275
  8.5 8.0 %collective-permute-start.2 = (bf16[256,128]{1,0:T(8,128)(2,1)S(1)}, bf16[256,128]{1,0:T(8,128)(2,1)S(1)}, u32[]{:S(2)}, u32[]{:S(2)}) collective-permute-start(bf16[256,128]{1,0:T(8,128)(2,1)S(1)} %get-tuple-element.50), channel_id=1, source_target_pairs={{0,1},{1,0},{2,3},{3,2},{4,5},{5,4},{6,7},{7,6},{8,9},{9,8},{10,11... | collective-permute-start | bytes 196616 | tf_op jit(solution)/shard_map/ppermute | solution.py:276
  8.6 7.9 %collective-permute-start.3 = (bf16[256,128]{1,0:T(8,128)(2,1)S(1)}, bf16[256,128]{1,0:T(8,128)(2,1)S(1)}, u32[]{:S(2)}, u32[]{:S(2)}) collective-permute-start(bf16[256,128]{1,0:T(8,128)(2,1)S(1)} %get-tuple-element.51), channel_id=1, source_target_pairs={{1,2},{2,1},{3,4},{4,3},{5,6},{6,5},{7,8},{8,7},{9,10},{10,9},{11,... | collective-permute-start | bytes 196616 | tf_op jit(solution)/shard_map/ppermute | solution.py:277
  37.4 0.8 copy-start
  38.2 3.4 %collective-permute-start.4 = (bf16[2304,128]{1,0:T(8,128)(2,1)}, bf16[2304,128]{1,0:T(8,128)(2,1)}, u32[]{:S(2)}, u32[]{:S(2)}) collective-permute-start(bf16[2304,128]{1,0:T(8,128)(2,1)} %get-tuple-element.56), channel_id=1, source_target_pairs={{0,1},{1,0},{2,3},{3,2},{4,5},{5,4},{6,7},{7,6},{8,9},{9,8},{10,11... | collective-permute-start | bytes 1769480 | tf_op jit(solution)/shard_map/ppermute | solution.py:331
  38.2 3.4 %copy-start.1 = (bf16[2304,128]{1,0:T(8,128)(2,1)S(1)}, bf16[2304,128]{1,0:T(8,128)(2,1)}, u32[]{:S(2)}) copy-start(bf16[2304,128]{1,0:T(8,128)(2,1)} %copy-done) | copy-start | bytes 1769476
  42.8 0.8 copy-start.2
  44.4 10.0 %collective-permute-start.5 = (bf16[576,128]{1,0:T(8,128)(2,1)}, bf16[576,128]{1,0:T(8,128)(2,1)S(1)}, u32[]{:S(2)}, u32[]{:S(2)}) collective-permute-start(bf16[576,128]{1,0:T(8,128)(2,1)} %get-tuple-element.92), channel_id=1, source_target_pairs={{0,32},{1,33},{2,34},{3,35},{4,36},{5,37},{6,38},{7,39},{8,40},{9,... | collective-permute-start | bytes 442376 | tf_op jit(solution)/shard_map/ppermute | solution.py:331
  47.0 10.4 %collective-permute-start.6 = (bf16[576,128]{1,0:T(8,128)(2,1)}, bf16[576,128]{1,0:T(8,128)(2,1)}, u32[]{:S(2)}, u32[]{:S(2)}) collective-permute-start(bf16[576,128]{1,0:T(8,128)(2,1)} %get-tuple-element.91), channel_id=1, source_target_pairs={{0,64},{1,65},{2,66},{3,67},{4,68},{5,69},{6,70},{7,71},{8,72},{9,... | collective-permute-start | bytes 442376 | tf_op jit(solution)/shard_map/ppermute | solution.py:331
  49.8 7.7 %collective-permute-start.7 = (bf16[576,128]{1,0:T(8,128)(2,1)}, bf16[576,128]{1,0:T(8,128)(2,1)}, u32[]{:S(2)}, u32[]{:S(2)}) collective-permute-start(bf16[576,128]{1,0:T(8,128)(2,1)} %get-tuple-element.90), channel_id=1, source_target_pairs={{0,96},{1,97},{2,98},{3,99},{4,100},{5,101},{6,102},{7,103},{8,104... | collective-permute-start | bytes 442376 | tf_op jit(solution)/shard_map/ppermute | solution.py:331
  58.6 8.5 %collective-permute-start.8 = (bf16[576,128]{1,0:T(8,128)(2,1)S(1)}, bf16[576,128]{1,0:T(8,128)(2,1)S(1)}, u32[]{:S(2)}, u32[]{:S(2)}) collective-permute-start(bf16[576,128]{1,0:T(8,128)(2,1)S(1)} %add_convert_fusion.3), channel_id=1, source_target_pairs={{0,8},{1,3},{2,10},{3,5},{4,12},{5,7},{6,14},{7,1},{8,16},{9,11},{... | collective-permute-start | bytes 442376 | tf_op jit(solution)/shard_map/ppermute | solution.py:331
  60.2 6.9 %collective-permute-start.9 = (bf16[576,128]{1,0:T(8,128)(2,1)S(1)}, bf16[576,128]{1,0:T(8,128)(2,1)S(1)}, u32[]{:S(2)}, u32[]{:S(2)}) collective-permute-start(bf16[576,128]{1,0:T(8,128)(2,1)S(1)} %add_convert_fusion.3), channel_id=1, source_target_pairs={{0,16},{1,5},{2,18},{3,7},{4,20},{5,1},{6,22},{7,3},{8,24},{9,13},... | collective-permute-start | bytes 442376 | tf_op jit(solution)/shard_map/ppermute | solution.py:331
  61.4 6.7 %collective-permute-start.10 = (bf16[576,128]{1,0:T(8,128)(2,1)S(1)}, bf16[576,128]{1,0:T(8,128)(2,1)S(1)}, u32[]{:S(2)}, u32[]{:S(2)}) collective-permute-start(bf16[576,128]{1,0:T(8,128)(2,1)S(1)} %add_convert_fusion.3), channel_id=1, source_target_pairs={{0,24},{1,7},{2,26},{3,1},{4,28},{5,3},{6,30},{7,5},{8,0},{9,15},{... | collective-permute-start | bytes 442376 | tf_op jit(solution)/shard_map/ppermute | solution.py:331
  68.2 8.5 %collective-permute-start.11 = (bf16[576,128]{1,0:T(8,128)(2,1)S(1)}, bf16[576,128]{1,0:T(8,128)(2,1)}, u32[]{:S(2)}, u32[]{:S(2)}) collective-permute-start(bf16[576,128]{1,0:T(8,128)(2,1)S(1)} %add_convert_fusion.2), channel_id=1, source_target_pairs={{0,2},{1,9},{2,4},{3,11},{4,6},{5,13},{6,0},{7,15},{8,10},{9,17},{... | collective-permute-start | bytes 442376 | tf_op jit(solution)/shard_map/ppermute | solution.py:331
  68.3 9.9 %collective-permute-start.12 = (bf16[576,128]{1,0:T(8,128)(2,1)S(1)}, bf16[576,128]{1,0:T(8,128)(2,1)}, u32[]{:S(2)}, u32[]{:S(2)}) collective-permute-start(bf16[576,128]{1,0:T(8,128)(2,1)S(1)} %add_convert_fusion.2), channel_id=1, source_target_pairs={{0,4},{1,17},{2,6},{3,19},{4,0},{5,21},{6,2},{7,23},{8,12},{9,25},... | collective-permute-start | bytes 442376 | tf_op jit(solution)/shard_map/ppermute | solution.py:331
  73.3 5.2 %collective-permute-start.13 = (bf16[576,128]{1,0:T(8,128)(2,1)S(1)}, bf16[576,128]{1,0:T(8,128)(2,1)}, u32[]{:S(2)}, u32[]{:S(2)}) collective-permute-start(bf16[576,128]{1,0:T(8,128)(2,1)S(1)} %add_convert_fusion.2), channel_id=1, source_target_pairs={{0,6},{1,25},{2,0},{3,27},{4,2},{5,29},{6,4},{7,31},{8,14},{9,1},{... | collective-permute-start | bytes 442376 | tf_op jit(solution)/shard_map/ppermute | solution.py:331
  79.9 7.1 %collective-permute-start.15 = (bf16[832,128]{1,0:T(8,128)(2,1)S(1)}, bf16[832,128]{1,0:T(8,128)(2,1)S(1)}, u32[]{:S(2)}, u32[]{:S(2)}) collective-permute-start(bf16[832,128]{1,0:T(8,128)(2,1)S(1)} %get-tuple-element.93), channel_id=1, source_target_pairs={{0,32},{1,33},{2,34},{3,35},{4,36},{5,37},{6,38},{7,39},{8,40},{9,... | collective-permute-start | bytes 638984 | tf_op jit(solution)/shard_map/ppermute | solution.py:331
  81.1 7.8 %collective-permute-start.18 = (bf16[576,128]{1,0:T(8,128)(2,1)S(1)}, bf16[576,128]{1,0:T(8,128)(2,1)S(1)}, u32[]{:S(2)}, u32[]{:S(2)}) collective-permute-start(bf16[576,128]{1,0:T(8,128)(2,1)S(1)} %get-tuple-element.89), channel_id=1, source_target_pairs={{0,64},{1,65},{2,66},{3,67},{4,68},{5,69},{6,70},{7,71},{8,72},{9,... | collective-permute-start | bytes 442376 | tf_op jit(solution)/shard_map/ppermute | solution.py:331
  83.5 6.0 %collective-permute-start.14 = (bf16[832,128]{1,0:T(8,128)(2,1)S(1)}, bf16[832,128]{1,0:T(8,128)(2,1)S(1)}, u32[]{:S(2)}, u32[]{:S(2)}) collective-permute-start(bf16[832,128]{1,0:T(8,128)(2,1)S(1)} %get-tuple-element.94), channel_id=1, source_target_pairs={{0,96},{1,97},{2,98},{3,99},{4,100},{5,101},{6,102},{7,103},{8,104... | collective-permute-start | bytes 638984 | tf_op jit(solution)/shard_map/ppermute | solution.py:331
  89.4 11.2 %collective-permute-start.19 = (bf16[2304,128]{1,0:T(8,128)(2,1)S(1)}, bf16[2304,128]{1,0:T(8,128)(2,1)S(1)}, u32[]{:S(2)}, u32[]{:S(2)}) collective-permute-start(bf16[2304,128]{1,0:T(8,128)(2,1)S(1)} %slice_dynamic-update-slice_fusion.own_ref), channel_id=1, source_target_pairs={{0,1},{1,0},{2,3},{3,2},{4,5},{5,4},{6,7},{7,6},{8,9},{9,8},{10,11... | collective-permute-start | bytes 1769480 | tf_op jit(solution)/shard_map/ppermute | solution.py:331
  89.5 3.8 %collective-permute-start.16 = (bf16[256,128]{1,0:T(8,128)(2,1)S(1)}, bf16[256,128]{1,0:T(8,128)(2,1)S(1)}, u32[]{:S(2)}, u32[]{:S(2)}) collective-permute-start(bf16[256,128]{1,0:T(8,128)(2,1)S(1)} %get-tuple-element.84), channel_id=1, source_target_pairs={{0,1},{1,0},{2,3},{3,2},{4,5},{5,4},{6,7},{7,6},{8,9},{9,8},{10,11... | collective-permute-start | bytes 196616 | tf_op jit(solution)/shard_map/ppermute | solution.py:369
  90.0 7.7 %collective-permute-start.17 = (bf16[256,128]{1,0:T(8,128)(2,1)S(1)}, bf16[256,128]{1,0:T(8,128)(2,1)S(1)}, u32[]{:S(2)}, u32[]{:S(2)}) collective-permute-start(bf16[256,128]{1,0:T(8,128)(2,1)S(1)} %get-tuple-element.85), channel_id=1, source_target_pairs={{1,2},{2,1},{3,4},{4,3},{5,6},{6,5},{7,8},{8,7},{9,10},{10,9},{11,... | collective-permute-start | bytes 196616 | tf_op jit(solution)/shard_map/ppermute | solution.py:370

commit v4 on v3

v4 whole, which is shorter than its diff:
```python
import functools

import jax
import jax.numpy as jnp
from jax import lax
from jax.experimental import pallas as pl
from jax.experimental.pallas import tpu as pltpu
from jax.sharding import PartitionSpec as P

BLOCK = 128
BF = jnp.bfloat16
F32 = jnp.float32
VM = pl.BlockSpec(memory_space=pltpu.VMEM)
SM = pl.BlockSpec(memory_space=pltpu.SMEM)

NN = (((1,), (0,)), ((), ()))
NT = (((1,), (1,)), ((), ()))
TN = (((0,), (0,)), ((), ()))


def mm(a, b, dims=NN):
    return lax.dot_general(a, b, dims, preferred_element_type=F32)


def sub_iota(rows, dtype=F32):
    return lax.broadcasted_iota(jnp.int32, (rows, BLOCK), 0).astype(F32).astype(dtype)


def onehot_t(row, ids):
    wide = jnp.broadcast_to(row, (16, BLOCK)).astype(BF)
    wide = jnp.concatenate([wide] * (ids.shape[0] // 16), axis=0)
    return jnp.where(ids == wide, jnp.ones((), BF), jnp.zeros((), BF))


def core_id():
    return lax.axis_index("tile") & 1


def list_order(core, rows_ref):
    rows = [rows_ref[d : d + 1, :] for d in range(4)]
    return (rows[0], rows[1], jnp.where(core == 0, rows[2], rows[3]), jnp.where(core == 0, rows[3], rows[2]))


def slot_order(core):
    return (0, 1, 3 - core, 2 + core)


def index_kernel(book_ref, code_ref, w_ref, dw_ref, cg_ref, src_ref, inner_ref, cell_ref, wt_ref, sg_ref):
    kvol = book_ref.shape[0]
    blocks, child, quarter = cell_ref.shape[0], 8, BLOCK // 4
    lane = lax.broadcasted_iota(jnp.int32, (kvol, BLOCK), 1)
    found = jnp.zeros((kvol, BLOCK), jnp.int32)
    for b in range(blocks):
        book = book_ref[:, b * BLOCK : (b + 1) * BLOCK]
        block = jnp.min(book, axis=1, keepdims=True) // BLOCK
        inner_ref[b] = (book - block * BLOCK).astype(F32)
        found = jnp.where(lane == b, block, found)
        code = code_ref[:, b * BLOCK : (b + 1) * BLOCK]
        cell = (code % child) * quarter + code // child - b * quarter
        cell_ref[b : b + 1, :] = jnp.where(code < child * quarter * blocks, cell, -1).astype(F32)
    src_ref[...] = found
    for k in range(kvol):
        wt_ref[:, k * BLOCK : (k + 1) * BLOCK] = w_ref[k].T
    for j in range(child):
        part = mm(cg_ref[...], dw_ref[j], NT).astype(BF)
        for b in range(blocks):
            sg_ref[b, j * quarter : (j + 1) * quarter, :] = part[b * quarter : (b + 1) * quarter, :]


def pick_kernel(feat_ref, rows_ref, *refs):
    out_refs, xt_ref, full_ref, hot_ref = refs[:-3], refs[-3], refs[-2], refs[-1]
    blocks = feat_ref.shape[0] // BLOCK
    length = rows_ref.shape[1]
    for b in range(blocks):
        block = feat_ref[b * BLOCK : (b + 1) * BLOCK, :].T
        xt_ref[b] = block
        full_ref[:, b * BLOCK : (b + 1) * BLOCK] = block
    ids = sub_iota(BLOCK, BF)
    for rows, out_ref in zip(list_order(core_id(), rows_ref), out_refs):
        for g in range(length // BLOCK):
            row = rows[:, g * BLOCK : (g + 1) * BLOCK]
            for b in range(blocks):
                hot_ref[b * BLOCK : (b + 1) * BLOCK, g * BLOCK : (g + 1) * BLOCK] = onehot_t(
                    (row - b * BLOCK).astype(F32), ids
                )
        out_ref[...] = mm(full_ref[...], hot_ref[...]).T.astype(BF)


def main_kernel(
    src_ref, xt_loc_ref, r0_ref, r1_ref, r2_ref, r3_ref, book_ref, cell_ref, wt_ref, sg_ref, dw_ref, cg_ref,
    coarse_ref, pg_ref, keep_ref, give_ref,
    xt_ref, gt_ref, ch_ref, part_ref,
):
    kvol = book_ref.shape[1]
    blocks = xt_loc_ref.shape[0]
    recv_refs = (r0_ref, r1_ref, r2_ref, r3_ref)
    each = r0_ref.shape[0] // BLOCK
    far = 4 * each
    child = dw_ref.shape[0]
    quarter = cg_ref.shape[0] // blocks
    ids = sub_iota(BLOCK, BF)
    ids2 = jnp.concatenate([ids, ids + jnp.asarray(BLOCK, BF)], axis=0)

    for b in range(blocks):
        xt_ref[b] = xt_loc_ref[b]
    for b in range(far):
        one = b % each
        slot = slot_order(core_id())[b // each]
        xt_ref[blocks + each * slot + one] = recv_refs[b // each][one * BLOCK : (one + 1) * BLOCK, :].T
    xt_ref[blocks + far] = jnp.zeros((BLOCK, BLOCK), BF)
    ch_ref[(blocks - 1) * quarter :, :] = jnp.zeros((quarter, child * BLOCK), BF)
    pg_ref[blocks // 2 - 1, BLOCK:, :] = jnp.zeros((BLOCK, BLOCK), BF)

    def some(p, count):
        for k in range(kvol):
            for h in range(count):
                b = 2 * p + h
                hot = onehot_t(book_ref[b, k : k + 1, :], ids)
                got = mm(xt_ref[src_ref[k, b]], hot)
                at = pl.multiple_of(p * 2 * BLOCK + h * BLOCK, BLOCK)
                gt_ref[k * BLOCK : (k + 1) * BLOCK, pl.ds(at, BLOCK)] = got.astype(BF)
        width = count * BLOCK
        pre = mm(wt_ref[...], gt_ref[:, pl.ds(pl.multiple_of(p * 2 * BLOCK, 2 * BLOCK), width)])
        hid = jnp.maximum(pre, 0.0).astype(BF)
        halves = []
        for h in range(count):
            b = 2 * p + h
            hot = onehot_t(cell_ref[pl.ds(b, 1), :], ids2)
            kids = mm(hot, hid[:, h * BLOCK : (h + 1) * BLOCK], NT).astype(BF)
            for j in range(child):
                ch_ref[pl.ds(pl.multiple_of(b * quarter, quarter), quarter), j * BLOCK : (j + 1) * BLOCK] = (
                    kids[j * quarter : (j + 1) * quarter, :]
                )
            halves.append(mm(sg_ref[b], hot, TN))
        grad = jnp.concatenate(halves, axis=1)
        pgt = jnp.where(pre > 0, grad, 0.0).astype(BF)
        pg_ref[p, 0:width, :] = pgt.T

    @pl.loop(0, blocks // 2 - 1)
    def _(p):
        some(p, 2)

    some(blocks // 2 - 1, 1)
    live = (blocks - 1) * BLOCK
    conv = mm(gt_ref[:, 0:live], pg_ref[...].reshape(blocks * BLOCK, BLOCK)[0:live, :])

    kids = ch_ref[...]
    coarse_ref[...] = mm(kids, dw_ref[...].reshape(child * BLOCK, BLOCK)).astype(BF)
    rows = kvol * BLOCK
    part_ref[0:rows, :] = conv.astype(BF)
    part_ref[rows : rows + child * BLOCK, :] = mm(kids, cg_ref[...], TN).astype(BF)
    rest = part_ref.shape[0] - rows - child * BLOCK
    part_ref[rows + child * BLOCK :, :] = jnp.zeros((rest, BLOCK), BF)
    half = keep_ref.shape[0]
    core = core_id()
    keep_ref[...] = part_ref[pl.ds(pl.multiple_of(core * half, half), half), :]
    give_ref[...] = part_ref[pl.ds(pl.multiple_of((1 - core) * half, half), half), :]


def back_kernel(lo, hi, pairs, src_ref, book_ref, wt_ref, pg_ref, *refs):
    refs, back_ref = refs[:-1], refs[-1]
    if lo > 0:
        before_ref, refs = refs[0], refs[1:]
    if hi < pairs:
        (table_ref,) = refs
    else:
        local_ref, *far_refs, table_ref = refs
    table_ref[...] = jnp.zeros_like(table_ref) if lo == 0 else before_ref[...]
    kvol = book_ref.shape[1]
    ids = sub_iota(BLOCK, BF)

    def some(p, count):
        back_ref[0 : count * BLOCK, :] = mm(pg_ref[p, 0 : count * BLOCK, :], wt_ref[...]).astype(BF)
        for k in range(kvol):
            for h in range(count):
                b = 2 * p + h
                hot = onehot_t(book_ref[b, k : k + 1, :], ids)
                table_ref[src_ref[k, b]] += mm(
                    hot, back_ref[h * BLOCK : (h + 1) * BLOCK, k * BLOCK : (k + 1) * BLOCK]
                )

    @pl.loop(lo, min(hi, pairs - 1))
    def _(p):
        some(p, 2)

    if hi == pairs:
        some(pairs - 1, 1)
        blocks = local_ref.shape[0] // BLOCK
        for b in range(blocks):
            local_ref[b * BLOCK : (b + 1) * BLOCK, :] = table_ref[b]
        for slot, far_ref in zip(slot_order(core_id()), far_refs):
            each = far_ref.shape[0] // BLOCK
            for one in range(each):
                far_ref[one * BLOCK : (one + 1) * BLOCK, :] = table_ref[blocks + each * slot + one].astype(BF)


def add_kernel(local_ref, rows_ref, g0_ref, g1_ref, g2_ref, g3_ref, out_ref, ret_ref):
    blocks = out_ref.shape[0] // BLOCK
    length = rows_ref.shape[1]
    ids = sub_iota(BLOCK, BF)
    nothing = jnp.zeros((length, BLOCK), BF)
    slab = lax.axis_index("slab")
    ret_ref[0:length, :] = jnp.where(slab < lax.axis_size("slab") - 1, g0_ref[g0_ref.shape[0] - length :, :], nothing)
    ret_ref[length : 2 * length, :] = jnp.where(slab > 0, g1_ref[g1_ref.shape[0] - length :, :], nothing)
    ret_ref[2 * length : 3 * length, :] = g2_ref[...]
    ret_ref[3 * length :, :] = g3_ref[...]
    groups = [
        rows[:, g * BLOCK : (g + 1) * BLOCK]
        for rows in list_order(core_id(), rows_ref)
        for g in range(length // BLOCK)
    ]
    for b in range(blocks):
        hot = jnp.concatenate([onehot_t((row - b * BLOCK).astype(F32), ids) for row in groups], axis=1)
        spot = slice(b * BLOCK, (b + 1) * BLOCK)
        out_ref[spot, :] = local_ref[spot, :] + mm(hot, ret_ref[...])


def wide(v):
    return v.astype(F32)


def quarter_at(n, m):
    return pl.ds(pl.multiple_of((n & 3) * m, m), m)


def pair_kernel(keep_ref, swap_ref, mine_ref, *piece_refs):
    m = mine_ref.shape[0]
    slab = lax.axis_index("slab")
    for sh, out_ref in enumerate((mine_ref, *piece_refs)):
        at = quarter_at(slab + sh, m)
        out_ref[...] = (wide(keep_ref[at, :]) + wide(swap_ref[at, :])).astype(BF)


def four_kernel(own_ref, g1_ref, g2_ref, g3_ref, *refs):
    outs = refs[0:1] if len(refs) == 1 else refs[2:]
    total = (wide(own_ref[...]) + wide(g2_ref[...])) + (wide(g1_ref[...]) + wide(g3_ref[...]))
    m = own_ref.shape[0]
    for out_ref in outs:
        out_ref[0:m, :] = total.astype(BF)
    if len(outs) > 1:
        outs[1][m:, :] = refs[0][...]
        outs[2][m:, :] = refs[1][...]


def join_kernel(own_ref, g1_ref, g2_ref, g3_ref, full_ref):
    m = own_ref.shape[0]
    slab = lax.axis_index("slab") + 4
    for sh, ref in enumerate((own_ref, g1_ref, g2_ref, g3_ref)):
        full_ref[quarter_at(slab - sh, m), :] = ref[0:m, :]


def spread_kernel(own_ref, other_ref, conv_ref, down_ref):
    half = own_ref.shape[0]
    rows = conv_ref.shape[0]

    def put(low_ref, high_ref):
        conv_ref[0:half, :] = low_ref[...].astype(F32)
        conv_ref[half:rows, :] = high_ref[0 : rows - half, :].astype(F32)
        down_ref[...] = high_ref[rows - half : rows - half + down_ref.shape[0], :].astype(F32)

    @pl.when(core_id() == 0)
    def _():
        put(own_ref, other_ref)

    @pl.when(core_id() != 0)
    def _():
        put(other_ref, own_ref)


def here(x):
    return pltpu.with_memory_space_constraint(x, pltpu.VMEM)


def afar(x):
    return pltpu.with_memory_space_constraint(x, pltpu.HBM)


def call(mib, kernel, outs, ins, scratch=()):
    single = len(outs) == 1
    shapes = tuple((jax.ShapeDtypeStruct if not near else pltpu.VMEM)(s, d) for s, d, *near in outs)
    return pl.pallas_call(
        kernel,
        out_shape=shapes[0] if single else shapes,
        in_specs=ins,
        out_specs=VM if single else tuple(VM for _ in outs),
        scratch_shapes=list(scratch),
        compiler_params=pltpu.CompilerParams(vmem_limit_bytes=mib * 1024 * 1024),
    )


def tie(*values):
    return lax.optimization_barrier(values)


def body(features, conv_weight, down_weight, coarse_grad, rulebook, boundary_rows, parent_code):
    row_count, chans = features.shape
    coarse_rows, out_chans = coarse_grad.shape
    list_len = boundary_rows.shape[1]
    child = down_weight.shape[0]
    kvol = conv_weight.shape[0]
    blocks = row_count // BLOCK
    pairs = blocks // 2
    far_rows = 4 * list_len
    quarter = coarse_rows // blocks
    slabs, tiles = lax.axis_size("slab"), lax.axis_size("tile")
    place = lax.axis_index("slab") * tiles + lax.axis_index("tile")
    core = place & 1

    near = True
    *outgoing, xt = call(
        12,
        pick_kernel,
        [((list_len, chans), BF, near)] * 4 + [((blocks, BLOCK, BLOCK), BF, near)],
        [VM, VM],
        [pltpu.VMEM((BLOCK, row_count), BF), pltpu.VMEM((row_count, list_len), BF)],
    )(afar(features), afar(boundary_rows))
    up = [(i, i + 1) for i in range(slabs - 1)]
    down = [(i + 1, i) for i in range(slabs - 1)]
    chip = [(i, i ^ 1) for i in range(tiles)]
    beside = [(i, i + 2 * (i % 2) - 1) for i in range(1, tiles - 1)]
    received = [
        lax.ppermute(outgoing[0], "slab", up),
        lax.ppermute(outgoing[1], "slab", down),
        lax.ppermute(outgoing[2], "tile", chip),
        lax.ppermute(outgoing[3], "tile", beside),
    ]
    source, inner, cell, wt, sg = call(
        12,
        index_kernel,
        [
            ((kvol, BLOCK), jnp.int32),
            ((blocks, kvol, BLOCK), F32, near),
            ((blocks, BLOCK), F32, near),
            ((BLOCK, kvol * BLOCK), BF, near),
            ((blocks, child * quarter, BLOCK), BF, near),
        ],
        [VM] * 5,
    )(*map(afar, (rulebook, parent_code.reshape(1, row_count), conv_weight, down_weight, coarse_grad)))

    grad_rows = (kvol + child) * BLOCK
    part_rows = -(-grad_rows // 512) * 512
    table = blocks + far_rows // BLOCK + 1
    coarse, pg, keep, give = call(
        32,
        main_kernel,
        [
            ((coarse_rows, out_chans), BF),
            ((pairs, 2 * BLOCK, BLOCK), BF, near),
            ((part_rows // 2, out_chans), BF, near),
            ((part_rows // 2, out_chans), BF, near),
        ],
        [SM] + [VM] * 11,
        [
            pltpu.VMEM((table, BLOCK, BLOCK), BF),
            pltpu.VMEM((kvol * BLOCK, row_count), BF),
            pltpu.VMEM((coarse_rows, child * BLOCK), BF),
            pltpu.VMEM((part_rows, BLOCK), BF),
        ],
    )(source, *map(here, (xt, *received, inner, cell, wt, sg)), afar(down_weight), afar(coarse_grad))

    def back_part(acc, lo, hi):
        ins = (source, here(inner), here(wt), here(pg)) + (() if acc is None else (here(acc),))
        whole = ((table, BLOCK, BLOCK), F32, near)
        scratch = [pltpu.VMEM((2 * BLOCK, kvol * BLOCK), BF)]
        if hi < pairs:
            outs = [whole]
        else:
            outs = [((row_count, chans), F32, near)] + [((list_len, chans), BF, near)] * 4
            scratch = [pltpu.VMEM(*whole[:2])] + scratch
        return call(
            12, functools.partial(back_kernel, lo, hi, pairs), outs, [SM] + [VM] * (len(ins) - 1), scratch
        )(*ins)

    stride = {"c": 1, "z": 2, "y": 8, "x": tiles}
    size = {"c": 2, "z": 4, "y": tiles // 8, "x": slabs}

    def send(v, axes, to):
        links = []
        for i in range(slabs * tiles):
            axis = axes[i % 2]
            st, n = stride[axis], size[axis]
            q = (i // st) % n
            links.append((i, i + (to(q) % n - q) * st))
        return lax.ppermute(v, ("slab", "tile"), links)

    def shifts(axes, pieces):
        return [send(v, axes, lambda q, sh=sh: q + sh) for sh, v in zip((1, 2, 3), pieces)]

    order = ("xx", "yz", "zy", "xx")
    swap = send(give, "cc", lambda q: 1 - q)
    acc = back_part(None, 0, 2)
    swap, acc = tie(swap, acc)
    m = part_rows // 8
    near_piece = ((m, out_chans), BF, near)
    long_piece = ((m + list_len, out_chans), BF, near)
    y, *pieces = call(8, pair_kernel, [near_piece] * 4, [VM] * 2)(here(keep), here(swap))

    for ph, (lo, hi) in enumerate(((2, 4), (4, 6), (6, 8))):
        y, acc = tie(y, acc)
        got = shifts(order[ph], pieces)
        result = back_part(acc, lo, hi)
        if hi < pairs:
            acc = result
            *got, acc = tie(*got, acc)
            y = call(8, four_kernel, [near_piece], [VM] * 4)(*map(here, (y, *got)))
            pieces = [y] * 3
        else:
            *got, local, far0, far1, far2, far3 = tie(*got, *result)
            y, low, high = call(8, four_kernel, [near_piece, long_piece, long_piece], [VM] * 6)(
                *map(here, (y, *got, far0, far1))
            )

    got = shifts(order[3], [high, y, low])
    returned = [
        got[2],
        got[0],
        lax.ppermute(far2, "tile", chip),
        lax.ppermute(far3, "tile", beside),
    ]
    full = call(8, join_kernel, [((4 * m, out_chans), BF, near)], [VM] * 4)(*map(here, (y, *got)))
    other = send(full, "cc", lambda q: 1 - q)
    input_grad = call(
        12, add_kernel, [((row_count, chans), F32)], [VM] * 6, [pltpu.VMEM((far_rows, chans), BF)]
    )(here(local), afar(boundary_rows), *map(here, returned))
    conv_grad, down_grad = call(
        12,
        spread_kernel,
        [((kvol * BLOCK, out_chans), F32), ((child * BLOCK, out_chans), F32)],
        [VM, VM],
    )(here(full), here(other))
    return (
        coarse,
        input_grad,
        conv_grad.reshape(kvol, chans, chans),
        down_grad.reshape(child, chans, out_chans),
    )


def solution(mesh):
    return jax.shard_map(
        body,
        mesh=mesh,
        in_specs=(
            P(("slab", "tile"), None),
            P(),
            P(),
            P(("slab", "tile"), None),
            P(None, ("slab", "tile")),
            P(("slab", "tile"), None),
            P(("slab", "tile")),
        ),
        out_specs=(P(("slab", "tile"), None), P(("slab", "tile"), None), P(), P()),
        check_vma=False,
    )
```

time: 104 us -> 93.9 us (0.903)
  Pallas kernels: 43.7 us -> 38.1 us
  other arithmetic: 4.19 us -> 0 us
  waiting for transfers between devices: 14.5 us -> 18 us
  local copies, waits for them, and re-layouts: 2.54 us -> 0 us
    pallas_call x9 -> x14, Pallas kernels: 43.7 us -> 38.1 us  [the longest x1 16.8 us: body(): call(32, main_kernel, [((coarse_rows, out_chans), BF), ((pairs, 2 * BLOCK...]
    ppermute x14, waiting for transfers between devices: 10.1 us -> 13.9 us  [send(): return lax.ppermute(v, ('slab', 'tile'), links)]
    convert_element_type x3 -> x0, other arithmetic: 2.43 us -> none  [the longest x1 1.22 us: body(): y = (wide(keep) + wide(swap)).astype(BF)]
    unnamed x6 -> x0, local copies, waits for them, and re-layouts: 1.63 us -> none
    dynamic_update_slice x1 -> x0, other arithmetic: 1.17 us -> none  [body(): full = lax.dynamic_update_slice_in_dim(full, v, (i + 4 - sh & 3) * m, 0)]
where the time goes in v4:
time: 93.9 us; the launch traced here: 93.5 us
  Pallas kernels  38.1 us (41%)
  starting transfers between devices  36.6 us (39%)
  waiting for transfers between devices  18 us (19%)
    ppermute x14, starting transfers between devices, send(): return lax.ppermute(v, ('slab', 'tile'), links)  21.8 us
    pallas_call x1, Pallas kernels, body(): call(32, main_kernel, [((coarse_rows, out_chans), BF), ((pairs, 2 * BLOCK...  16.8 us
    ppermute x14, waiting for transfers between devices, send(): return lax.ppermute(v, ('slab', 'tile'), links)  13.9 us
    pallas_call x4, Pallas kernels, back_part(): call(12, functools.partial(back_kernel, lo, hi, pairs), outs, [SM] + [VM]...  11.8 us
    ppermute x1, starting transfers between devices, body(): lax.ppermute(outgoing[3], 'tile', beside)  5.92 us
    ppermute x1, waiting for transfers between devices, body(): lax.ppermute(far3, 'tile', beside)  4.12 us
    ppermute x1, starting transfers between devices, body(): lax.ppermute(far3, 'tile', beside)  3.54 us
    ppermute x1, starting transfers between devices, body(): lax.ppermute(outgoing[0], 'slab', up)  3.4 us
  transfers between devices with their start and end apart: 20, of which 8 were waited for; matrix products, arithmetic and copies ran while one was open for 0% of the time, Pallas kernels for 18%

profile of v4, /device:TPU:8, one launch (start us, length us, event | category | flops | bytes accessed | tf_op | source)
XLA Modules:
  0.0 93.5 jit_solution(11394206468350681955)
XLA Ops:
  0.6 2.6 %shard_map.103 = (bf16[256,128]{1,0:T(8,128)(2,1)S(1)}, bf16[256,128]{1,0:T(8,128)(2,1)S(1)}, bf16[256,128]{1,0:T(8,128)(2,1)S(1)}, bf16[256,128]{1,0:T(8,128)(2,1)S(1)}, bf16[16,128,128]{2,1,0:T(8,128)(2,1)S(1)}) custom-call(bf16[2048,128]{1,0:T(8,128)(2,1)} %feat_ref.1, s32[4,256]{1,0:T(4,128)} %rows_ref.3), custom_call_target="tpu_custom_call" | custom-call | tf_op jit(solution)/shard_map/pallas_call | solution.py:310
  3.2 3.4 %collective-permute-start = (bf16[256,128]{1,0:T(8,128)(2,1)S(1)}, bf16[256,128]{1,0:T(8,128)(2,1)S(1)}, u32[]{:S(2)}, u32[]{:S(2)}) collective-permute-start(bf16[256,128]{1,0:T(8,128)(2,1)S(1)} %get-tuple-element.58), channel_id=1, source_target_pairs={{0,32},{32,64},{64,96},{1,33},{33,65},{65,97},{2,34},{34,66},{66,9... | collective-permute-start | bytes 196616 | tf_op jit(solution)/shard_map/ppermute | solution.py:322
  6.6 1.3 %collective-permute-start.1 = (bf16[256,128]{1,0:T(8,128)(2,1)S(1)}, bf16[256,128]{1,0:T(8,128)(2,1)S(1)}, u32[]{:S(2)}, u32[]{:S(2)}) collective-permute-start(bf16[256,128]{1,0:T(8,128)(2,1)S(1)} %get-tuple-element.59), channel_id=1, source_target_pairs={{32,0},{64,32},{96,64},{33,1},{65,33},{97,65},{34,2},{66,34},{98,6... | collective-permute-start | bytes 196616 | tf_op jit(solution)/shard_map/ppermute | solution.py:323
  8.0 5.9 %collective-permute-start.3 = (bf16[256,128]{1,0:T(8,128)(2,1)S(1)}, bf16[256,128]{1,0:T(8,128)(2,1)S(1)}, u32[]{:S(2)}, u32[]{:S(2)}) collective-permute-start(bf16[256,128]{1,0:T(8,128)(2,1)S(1)} %get-tuple-element.61), channel_id=1, source_target_pairs={{1,2},{2,1},{3,4},{4,3},{5,6},{6,5},{7,8},{8,7},{9,10},{10,9},{11,... | collective-permute-start | bytes 196616 | tf_op jit(solution)/shard_map/ppermute | solution.py:325
  13.9 2.0 %shard_map.102 = (s32[27,128]{1,0:T(8,128)S(1)}, f32[16,27,128]{2,1,0:T(8,128)S(1)}, f32[16,128]{1,0:T(8,128)S(1)}, bf16[128,3456]{1,0:T(8,128)(2,1)S(1)}, bf16[16,256,128]{2,1,0:T(8,128)(2,1)S(1)}) custom-call(s32[27,2048]{1,0:T(8,128)} %book_ref.1, s32[1,2048]{1,0:T(1,128)} %bitcast.3, bf16[27,128,128]{2,1,0:T(8,128)(2,1)} %w_ref.1, ...), custom_call_target="tpu_custom_call" | custom-call | tf_op jit(solution)/shard_map/pallas_call | solution.py:327
  16.0 16.8 %shard_map.104 = (bf16[512,128]{1,0:T(8,128)(2,1)}, bf16[8,256,128]{2,1,0:T(8,128)(2,1)S(1)}, bf16[2304,128]{1,0:T(8,128)(2,1)S(1)}, bf16[2304,128]{1,0:T(8,128)(2,1)S(1)}) custom-call(s32[27,128]{1,0:T(8,128)S(1)} %get-tuple-element.56.src_ref, bf16[16,128,128]{2,1,0:T(8,128)(2,1)S(1)} %get-tuple-element.57.xt_loc_ref, ...), custom_call_target="tpu_custom_call" | custom-call | tf_op jit(solution)/shard_map/pallas_call | solution.py:343
  32.9 3.1 %shard_map.105.refs_0_ = f32[25,128,128]{2,1,0:T(8,128)S(1)} custom-call(s32[27,128]{1,0:T(8,128)S(1)} %get-tuple-element.56.src_ref, f32[16,27,128]{2,1,0:T(8,128)S(1)} %get-tuple-element.62.book_ref, bf16[128,3456]{1,0:T(8,128)(2,1)S(1)} %get-tuple-element.64.wt_ref, bf16[8,256,128]{2,1,0:T(8,128)(2,1)S(1)} %get-tuple-element.69.pg_ref), custom_call_target="tpu_custom_call" | custom-call | tf_op jit(solution)/shard_map/pallas_call | solution.py:370
  36.0 0.2 shard_map.106
  36.1 2.7 %collective-permute-start.5 = (bf16[576,128]{1,0:T(8,128)(2,1)S(1)}, bf16[576,128]{1,0:T(8,128)(2,1)S(1)}, u32[]{:S(2)}, u32[]{:S(2)}) collective-permute-start(bf16[576,128]{1,0:T(8,128)(2,1)S(1)} %get-tuple-element.74), channel_id=1, source_target_pairs={{0,32},{1,33},{2,34},{3,35},{4,36},{5,37},{6,38},{7,39},{8,40},{9,... | collective-permute-start | bytes 442376 | tf_op jit(solution)/shard_map/ppermute | solution.py:384
  38.8 2.7 %collective-permute-start.6 = (bf16[576,128]{1,0:T(8,128)(2,1)S(1)}, bf16[576,128]{1,0:T(8,128)(2,1)S(1)}, u32[]{:S(2)}, u32[]{:S(2)}) collective-permute-start(bf16[576,128]{1,0:T(8,128)(2,1)S(1)} %get-tuple-element.75), channel_id=1, source_target_pairs={{0,64},{1,65},{2,66},{3,67},{4,68},{5,69},{6,70},{7,71},{8,72},{9,... | collective-permute-start | bytes 442376 | tf_op jit(solution)/shard_map/ppermute | solution.py:384
  41.6 1.4 %collective-permute-start.7 = (bf16[576,128]{1,0:T(8,128)(2,1)S(1)}, bf16[576,128]{1,0:T(8,128)(2,1)S(1)}, u32[]{:S(2)}, u32[]{:S(2)}) collective-permute-start(bf16[576,128]{1,0:T(8,128)(2,1)S(1)} %get-tuple-element.76), channel_id=1, source_target_pairs={{0,96},{1,97},{2,98},{3,99},{4,100},{5,101},{6,102},{7,103},{8,104... | collective-permute-start | bytes 442376 | tf_op jit(solution)/shard_map/ppermute | solution.py:384
  43.0 3.1 %shard_map.107.refs_0_ = f32[25,128,128]{2,1,0:T(8,128)S(1)} custom-call(s32[27,128]{1,0:T(8,128)S(1)} %get-tuple-element.56.src_ref, f32[16,27,128]{2,1,0:T(8,128)S(1)} %get-tuple-element.62.book_ref, bf16[128,3456]{1,0:T(8,128)(2,1)S(1)} %get-tuple-element.64.wt_ref, bf16[8,256,128]{2,1,0:T(8,128)(2,1)S(1)} %get-tuple-element.69.pg_ref, ...), custom_call_target="tpu_custom_call" | custom-call | tf_op jit(solution)/shard_map/pallas_call | solution.py:370
  46.2 2.8 %collective-permute-done.6.g2_ref = bf16[576,128]{1,0:T(8,128)(2,1)S(1)} collective-permute-done((bf16[576,128]{1,0:T(8,128)(2,1)S(1)}, bf16[576,128]{1,0:T(8,128)(2,1)S(1)}, u32[]{:S(2)}, u32[]{:S(2)}) %collective-permute-start.6) | collective-permute-done | bytes 147488 | tf_op jit(solution)/shard_map/ppermute | solution.py:384
  49.1 3.0 %collective-permute-start.9 = (bf16[576,128]{1,0:T(8,128)(2,1)S(1)}, bf16[576,128]{1,0:T(8,128)(2,1)S(1)}, u32[]{:S(2)}, u32[]{:S(2)}) collective-permute-start(bf16[576,128]{1,0:T(8,128)(2,1)S(1)} %shard_map.108.own_ref), channel_id=1, source_target_pairs={{0,16},{1,5},{2,18},{3,7},{4,20},{5,1},{6,22},{7,3},{8,24},{9,13},... | collective-permute-start | bytes 442376 | tf_op jit(solution)/shard_map/ppermute | solution.py:384
  52.1 2.2 %collective-permute-start.8 = (bf16[576,128]{1,0:T(8,128)(2,1)S(1)}, bf16[576,128]{1,0:T(8,128)(2,1)S(1)}, u32[]{:S(2)}, u32[]{:S(2)}) collective-permute-start(bf16[576,128]{1,0:T(8,128)(2,1)S(1)} %shard_map.108.own_ref), channel_id=1, source_target_pairs={{0,8},{1,3},{2,10},{3,5},{4,12},{5,7},{6,14},{7,1},{8,16},{9,11},{... | collective-permute-start | bytes 442376 | tf_op jit(solution)/shard_map/ppermute | solution.py:384
  54.3 3.1 %shard_map.109.refs_0_ = f32[25,128,128]{2,1,0:T(8,128)S(1)} custom-call(s32[27,128]{1,0:T(8,128)S(1)} %get-tuple-element.56.src_ref, f32[16,27,128]{2,1,0:T(8,128)S(1)} %get-tuple-element.62.book_ref, bf16[128,3456]{1,0:T(8,128)(2,1)S(1)} %get-tuple-element.64.wt_ref, bf16[8,256,128]{2,1,0:T(8,128)(2,1)S(1)} %get-tuple-element.69.pg_ref, ...), custom_call_target="tpu_custom_call" | custom-call | tf_op jit(solution)/shard_map/pallas_call | solution.py:370
  57.5 0.5 collective-permute-done.8.g1_ref
  58.0 3.8 %collective-permute-start.13 = (bf16[576,128]{1,0:T(8,128)(2,1)S(1)}, bf16[576,128]{1,0:T(8,128)(2,1)S(1)}, u32[]{:S(2)}, u32[]{:S(2)}) collective-permute-start(bf16[576,128]{1,0:T(8,128)(2,1)S(1)} %shard_map.110.own_ref), channel_id=1, source_target_pairs={{0,6},{1,25},{2,0},{3,27},{4,2},{5,29},{6,4},{7,31},{8,14},{9,1},{... | collective-permute-start | bytes 442376 | tf_op jit(solution)/shard_map/ppermute | solution.py:384
  61.8 0.9 %collective-permute-start.11 = (bf16[576,128]{1,0:T(8,128)(2,1)S(1)}, bf16[576,128]{1,0:T(8,128)(2,1)S(1)}, u32[]{:S(2)}, u32[]{:S(2)}) collective-permute-start(bf16[576,128]{1,0:T(8,128)(2,1)S(1)} %shard_map.110.own_ref), channel_id=1, source_target_pairs={{0,2},{1,9},{2,4},{3,11},{4,6},{5,13},{6,0},{7,15},{8,10},{9,17},{... | collective-permute-start | bytes 442376 | tf_op jit(solution)/shard_map/ppermute | solution.py:384
  62.8 2.5 %shard_map.111 = (f32[2048,128]{1,0:T(8,128)S(1)}, bf16[256,128]{1,0:T(8,128)(2,1)S(1)}, bf16[256,128]{1,0:T(8,128)(2,1)S(1)}, bf16[256,128]{1,0:T(8,128)(2,1)S(1)}, bf16[256,128]{1,0:T(8,128)(2,1)S(1)}) custom-call(s32[27,128]{1,0:T(8,128)S(1)} %get-tuple-element.56.src_ref, f32[16,27,128]{2,1,0:T(8,128)S(1)} %get-tuple-element.62.book_ref, ...), custom_call_target="tpu_custom_call" | custom-call | tf_op jit(solution)/shard_map/pallas_call | solution.py:370
  65.3 0.8 collective-permute-done.13.g3_ref
  66.1 2.5 %collective-permute-done.12.g2_ref = bf16[576,128]{1,0:T(8,128)(2,1)S(1)} collective-permute-done((bf16[576,128]{1,0:T(8,128)(2,1)S(1)}, bf16[576,128]{1,0:T(8,128)(2,1)S(1)}, u32[]{:S(2)}, u32[]{:S(2)}) %collective-permute-start.12) | collective-permute-done | bytes 147488 | tf_op jit(solution)/shard_map/ppermute | solution.py:384
  68.6 1.2 %collective-permute-done.11.g1_ref = bf16[576,128]{1,0:T(8,128)(2,1)S(1)} collective-permute-done((bf16[576,128]{1,0:T(8,128)(2,1)S(1)}, bf16[576,128]{1,0:T(8,128)(2,1)S(1)}, u32[]{:S(2)}, u32[]{:S(2)}) %collective-permute-start.11) | collective-permute-done | bytes 147488 | tf_op jit(solution)/shard_map/ppermute | solution.py:384
  69.8 2.2 %collective-permute-start.14 = (bf16[832,128]{1,0:T(8,128)(2,1)S(1)}, bf16[832,128]{1,0:T(8,128)(2,1)S(1)}, u32[]{:S(2)}, u32[]{:S(2)}) collective-permute-start(bf16[832,128]{1,0:T(8,128)(2,1)S(1)} %get-tuple-element.101), channel_id=1, source_target_pairs={{0,96},{1,97},{2,98},{3,99},{4,100},{5,101},{6,102},{7,103},{8,104... | collective-permute-start | bytes 638984 | tf_op jit(solution)/shard_map/ppermute | solution.py:384
  72.1 2.5 %collective-permute-start.18 = (bf16[576,128]{1,0:T(8,128)(2,1)S(1)}, bf16[576,128]{1,0:T(8,128)(2,1)S(1)}, u32[]{:S(2)}, u32[]{:S(2)}) collective-permute-start(bf16[576,128]{1,0:T(8,128)(2,1)S(1)} %get-tuple-element.105.own_ref), channel_id=1, source_target_pairs={{0,64},{1,65},{2,66},{3,67},{4,68},{5,69},{6,70},{7,71},{8,72},{9,... | collective-permute-start | bytes 442376 | tf_op jit(solution)/shard_map/ppermute | solution.py:384
  74.6 5.5 %collective-permute-done.18.g2_ref = bf16[576,128]{1,0:T(8,128)(2,1)S(1)} collective-permute-done((bf16[576,128]{1,0:T(8,128)(2,1)S(1)}, bf16[576,128]{1,0:T(8,128)(2,1)S(1)}, u32[]{:S(2)}, u32[]{:S(2)}) %collective-permute-start.18) | collective-permute-done | bytes 147488 | tf_op jit(solution)/shard_map/ppermute | solution.py:384
  80.1 0.6 collective-permute-done.15.g1_ref
  80.9 0.5 collective-permute-start.16
  81.4 3.5 %collective-permute-start.17 = (bf16[256,128]{1,0:T(8,128)(2,1)S(1)}, bf16[256,128]{1,0:T(8,128)(2,1)S(1)}, u32[]{:S(2)}, u32[]{:S(2)}) collective-permute-start(bf16[256,128]{1,0:T(8,128)(2,1)S(1)} %get-tuple-element.104), channel_id=1, source_target_pairs={{1,2},{2,1},{3,4},{4,3},{5,6},{6,5},{7,8},{8,7},{9,10},{10,9},{11,... | collective-permute-start | bytes 196616 | tf_op jit(solution)/shard_map/ppermute | solution.py:418
  84.9 4.1 %collective-permute-done.17.g3_ref = bf16[256,128]{1,0:T(8,128)(2,1)S(1)} collective-permute-done((bf16[256,128]{1,0:T(8,128)(2,1)S(1)}, bf16[256,128]{1,0:T(8,128)(2,1)S(1)}, u32[]{:S(2)}, u32[]{:S(2)}) %collective-permute-start.17) | collective-permute-done | bytes 65568 | tf_op jit(solution)/shard_map/ppermute | solution.py:418
  89.0 3.0 %shard_map.113 = f32[2048,128]{1,0:T(8,128)} custom-call(f32[2048,128]{1,0:T(8,128)S(1)} %get-tuple-element.94.local_ref, s32[4,256]{1,0:T(4,128)} %rows_ref.3, bf16[832,128]{1,0:T(8,128)(2,1)S(1)} %collective-permute-done.14.g0_ref.g3_ref, bf16[832,128]{1,0:T(8,128)(2,1)S(1)} %collective-permute-done.15.g1_ref, ...), custom_call_target="tpu_custom_call" | custom-call | tf_op jit(solution)/shard_map/pallas_call | solution.py:422
  92.0 1.5 %shard_map.115 = (f32[3456,128]{1,0:T(8,128)}, f32[1024,128]{1,0:T(8,128)}) custom-call(bf16[2304,128]{1,0:T(8,128)(2,1)S(1)} %shard_map.114.own_ref, bf16[2304,128]{1,0:T(8,128)(2,1)S(1)} %collective-permute-done.19.other_ref), custom_call_target="tpu_custom_call" | custom-call | tf_op jit(solution)/shard_map/pallas_call | solution.py:425
  (22 shorter events, 0.6 us)
Async XLA Ops:
  3.2 12.8 %collective-permute-start = (bf16[256,128]{1,0:T(8,128)(2,1)S(1)}, bf16[256,128]{1,0:T(8,128)(2,1)S(1)}, u32[]{:S(2)}, u32[]{:S(2)}) collective-permute-start(bf16[256,128]{1,0:T(8,128)(2,1)S(1)} %get-tuple-element.58), channel_id=1, source_target_pairs={{0,32},{32,64},{64,96},{1,33},{33,65},{65,97},{2,34},{34,66},{66,9... | collective-permute-start | bytes 196616 | tf_op jit(solution)/shard_map/ppermute | solution.py:322
  6.6 9.4 %collective-permute-start.1 = (bf16[256,128]{1,0:T(8,128)(2,1)S(1)}, bf16[256,128]{1,0:T(8,128)(2,1)S(1)}, u32[]{:S(2)}, u32[]{:S(2)}) collective-permute-start(bf16[256,128]{1,0:T(8,128)(2,1)S(1)} %get-tuple-element.59), channel_id=1, source_target_pairs={{32,0},{64,32},{96,64},{33,1},{65,33},{97,65},{34,2},{66,34},{98,6... | collective-permute-start | bytes 196616 | tf_op jit(solution)/shard_map/ppermute | solution.py:323
  7.9 8.1 %collective-permute-start.2 = (bf16[256,128]{1,0:T(8,128)(2,1)S(1)}, bf16[256,128]{1,0:T(8,128)(2,1)S(1)}, u32[]{:S(2)}, u32[]{:S(2)}) collective-permute-start(bf16[256,128]{1,0:T(8,128)(2,1)S(1)} %get-tuple-element.60), channel_id=1, source_target_pairs={{0,1},{1,0},{2,3},{3,2},{4,5},{5,4},{6,7},{7,6},{8,9},{9,8},{10,11... | collective-permute-start | bytes 196616 | tf_op jit(solution)/shard_map/ppermute | solution.py:324
  8.0 8.0 %collective-permute-start.3 = (bf16[256,128]{1,0:T(8,128)(2,1)S(1)}, bf16[256,128]{1,0:T(8,128)(2,1)S(1)}, u32[]{:S(2)}, u32[]{:S(2)}) collective-permute-start(bf16[256,128]{1,0:T(8,128)(2,1)S(1)} %get-tuple-element.61), channel_id=1, source_target_pairs={{1,2},{2,1},{3,4},{4,3},{5,6},{6,5},{7,8},{8,7},{9,10},{10,9},{11,... | collective-permute-start | bytes 196616 | tf_op jit(solution)/shard_map/ppermute | solution.py:325
  32.8 3.2 %collective-permute-start.4 = (bf16[2304,128]{1,0:T(8,128)(2,1)S(1)}, bf16[2304,128]{1,0:T(8,128)(2,1)S(1)}, u32[]{:S(2)}, u32[]{:S(2)}) collective-permute-start(bf16[2304,128]{1,0:T(8,128)(2,1)S(1)} %get-tuple-element.68), channel_id=1, source_target_pairs={{0,1},{1,0},{2,3},{3,2},{4,5},{5,4},{6,7},{7,6},{8,9},{9,8},{10,11... | collective-permute-start | bytes 1769480 | tf_op jit(solution)/shard_map/ppermute | solution.py:384
  36.1 10.0 %collective-permute-start.5 = (bf16[576,128]{1,0:T(8,128)(2,1)S(1)}, bf16[576,128]{1,0:T(8,128)(2,1)S(1)}, u32[]{:S(2)}, u32[]{:S(2)}) collective-permute-start(bf16[576,128]{1,0:T(8,128)(2,1)S(1)} %get-tuple-element.74), channel_id=1, source_target_pairs={{0,32},{1,33},{2,34},{3,35},{4,36},{5,37},{6,38},{7,39},{8,40},{9,... | collective-permute-start | bytes 442376 | tf_op jit(solution)/shard_map/ppermute | solution.py:384
  38.8 10.1 %collective-permute-start.6 = (bf16[576,128]{1,0:T(8,128)(2,1)S(1)}, bf16[576,128]{1,0:T(8,128)(2,1)S(1)}, u32[]{:S(2)}, u32[]{:S(2)}) collective-permute-start(bf16[576,128]{1,0:T(8,128)(2,1)S(1)} %get-tuple-element.75), channel_id=1, source_target_pairs={{0,64},{1,65},{2,66},{3,67},{4,68},{5,69},{6,70},{7,71},{8,72},{9,... | collective-permute-start | bytes 442376 | tf_op jit(solution)/shard_map/ppermute | solution.py:384
  41.6 7.4 %collective-permute-start.7 = (bf16[576,128]{1,0:T(8,128)(2,1)S(1)}, bf16[576,128]{1,0:T(8,128)(2,1)S(1)}, u32[]{:S(2)}, u32[]{:S(2)}) collective-permute-start(bf16[576,128]{1,0:T(8,128)(2,1)S(1)} %get-tuple-element.76), channel_id=1, source_target_pairs={{0,96},{1,97},{2,98},{3,99},{4,100},{5,101},{6,102},{7,103},{8,104... | collective-permute-start | bytes 442376 | tf_op jit(solution)/shard_map/ppermute | solution.py:384
  49.1 8.4 %collective-permute-start.10 = (bf16[576,128]{1,0:T(8,128)(2,1)S(1)}, bf16[576,128]{1,0:T(8,128)(2,1)S(1)}, u32[]{:S(2)}, u32[]{:S(2)}) collective-permute-start(bf16[576,128]{1,0:T(8,128)(2,1)S(1)} %shard_map.108.own_ref), channel_id=1, source_target_pairs={{0,24},{1,7},{2,26},{3,1},{4,28},{5,3},{6,30},{7,5},{8,0},{9,15},{... | collective-permute-start | bytes 442376 | tf_op jit(solution)/shard_map/ppermute | solution.py:384
  49.1 8.3 %collective-permute-start.9 = (bf16[576,128]{1,0:T(8,128)(2,1)S(1)}, bf16[576,128]{1,0:T(8,128)(2,1)S(1)}, u32[]{:S(2)}, u32[]{:S(2)}) collective-permute-start(bf16[576,128]{1,0:T(8,128)(2,1)S(1)} %shard_map.108.own_ref), channel_id=1, source_target_pairs={{0,16},{1,5},{2,18},{3,7},{4,20},{5,1},{6,22},{7,3},{8,24},{9,13},... | collective-permute-start | bytes 442376 | tf_op jit(solution)/shard_map/ppermute | solution.py:384
  52.1 5.8 %collective-permute-start.8 = (bf16[576,128]{1,0:T(8,128)(2,1)S(1)}, bf16[576,128]{1,0:T(8,128)(2,1)S(1)}, u32[]{:S(2)}, u32[]{:S(2)}) collective-permute-start(bf16[576,128]{1,0:T(8,128)(2,1)S(1)} %shard_map.108.own_ref), channel_id=1, source_target_pairs={{0,8},{1,3},{2,10},{3,5},{4,12},{5,7},{6,14},{7,1},{8,16},{9,11},{... | collective-permute-start | bytes 442376 | tf_op jit(solution)/shard_map/ppermute | solution.py:384
  58.0 8.1 %collective-permute-start.13 = (bf16[576,128]{1,0:T(8,128)(2,1)S(1)}, bf16[576,128]{1,0:T(8,128)(2,1)S(1)}, u32[]{:S(2)}, u32[]{:S(2)}) collective-permute-start(bf16[576,128]{1,0:T(8,128)(2,1)S(1)} %shard_map.110.own_ref), channel_id=1, source_target_pairs={{0,6},{1,25},{2,0},{3,27},{4,2},{5,29},{6,4},{7,31},{8,14},{9,1},{... | collective-permute-start | bytes 442376 | tf_op jit(solution)/shard_map/ppermute | solution.py:384
  61.8 6.8 %collective-permute-start.12 = (bf16[576,128]{1,0:T(8,128)(2,1)S(1)}, bf16[576,128]{1,0:T(8,128)(2,1)S(1)}, u32[]{:S(2)}, u32[]{:S(2)}) collective-permute-start(bf16[576,128]{1,0:T(8,128)(2,1)S(1)} %shard_map.110.own_ref), channel_id=1, source_target_pairs={{0,4},{1,17},{2,6},{3,19},{4,0},{5,21},{6,2},{7,23},{8,12},{9,25},... | collective-permute-start | bytes 442376 | tf_op jit(solution)/shard_map/ppermute | solution.py:384
  61.8 7.9 %collective-permute-start.11 = (bf16[576,128]{1,0:T(8,128)(2,1)S(1)}, bf16[576,128]{1,0:T(8,128)(2,1)S(1)}, u32[]{:S(2)}, u32[]{:S(2)}) collective-permute-start(bf16[576,128]{1,0:T(8,128)(2,1)S(1)} %shard_map.110.own_ref), channel_id=1, source_target_pairs={{0,2},{1,9},{2,4},{3,11},{4,6},{5,13},{6,0},{7,15},{8,10},{9,17},{... | collective-permute-start | bytes 442376 | tf_op jit(solution)/shard_map/ppermute | solution.py:384
  69.8 10.3 %collective-permute-start.14 = (bf16[832,128]{1,0:T(8,128)(2,1)S(1)}, bf16[832,128]{1,0:T(8,128)(2,1)S(1)}, u32[]{:S(2)}, u32[]{:S(2)}) collective-permute-start(bf16[832,128]{1,0:T(8,128)(2,1)S(1)} %get-tuple-element.101), channel_id=1, source_target_pairs={{0,96},{1,97},{2,98},{3,99},{4,100},{5,101},{6,102},{7,103},{8,104... | collective-permute-start | bytes 638984 | tf_op jit(solution)/shard_map/ppermute | solution.py:384
  72.1 8.6 %collective-permute-start.15 = (bf16[832,128]{1,0:T(8,128)(2,1)S(1)}, bf16[832,128]{1,0:T(8,128)(2,1)S(1)}, u32[]{:S(2)}, u32[]{:S(2)}) collective-permute-start(bf16[832,128]{1,0:T(8,128)(2,1)S(1)} %get-tuple-element.102), channel_id=1, source_target_pairs={{0,32},{1,33},{2,34},{3,35},{4,36},{5,37},{6,38},{7,39},{8,40},{9,... | collective-permute-start | bytes 638984 | tf_op jit(solution)/shard_map/ppermute | solution.py:384
  72.1 8.0 %collective-permute-start.18 = (bf16[576,128]{1,0:T(8,128)(2,1)S(1)}, bf16[576,128]{1,0:T(8,128)(2,1)S(1)}, u32[]{:S(2)}, u32[]{:S(2)}) collective-permute-start(bf16[576,128]{1,0:T(8,128)(2,1)S(1)} %get-tuple-element.105.own_ref), channel_id=1, source_target_pairs={{0,64},{1,65},{2,66},{3,67},{4,68},{5,69},{6,70},{7,71},{8,72},{9,... | collective-permute-start | bytes 442376 | tf_op jit(solution)/shard_map/ppermute | solution.py:384
  80.8 11.2 %collective-permute-start.19 = (bf16[2304,128]{1,0:T(8,128)(2,1)S(1)}, bf16[2304,128]{1,0:T(8,128)(2,1)S(1)}, u32[]{:S(2)}, u32[]{:S(2)}) collective-permute-start(bf16[2304,128]{1,0:T(8,128)(2,1)S(1)} %shard_map.114.own_ref), channel_id=1, source_target_pairs={{0,1},{1,0},{2,3},{3,2},{4,5},{5,4},{6,7},{7,6},{8,9},{9,8},{10,11... | collective-permute-start | bytes 1769480 | tf_op jit(solution)/shard_map/ppermute | solution.py:384
  80.9 4.0 %collective-permute-start.16 = (bf16[256,128]{1,0:T(8,128)(2,1)S(1)}, bf16[256,128]{1,0:T(8,128)(2,1)S(1)}, u32[]{:S(2)}, u32[]{:S(2)}) collective-permute-start(bf16[256,128]{1,0:T(8,128)(2,1)S(1)} %get-tuple-element.103), channel_id=1, source_target_pairs={{0,1},{1,0},{2,3},{3,2},{4,5},{5,4},{6,7},{7,6},{8,9},{9,8},{10,11... | collective-permute-start | bytes 196616 | tf_op jit(solution)/shard_map/ppermute | solution.py:417
  81.4 7.7 %collective-permute-start.17 = (bf16[256,128]{1,0:T(8,128)(2,1)S(1)}, bf16[256,128]{1,0:T(8,128)(2,1)S(1)}, u32[]{:S(2)}, u32[]{:S(2)}) collective-permute-start(bf16[256,128]{1,0:T(8,128)(2,1)S(1)} %get-tuple-element.104), channel_id=1, source_target_pairs={{1,2},{2,1},{3,4},{4,3},{5,6},{6,5},{7,8},{8,7},{9,10},{10,9},{11,... | collective-permute-start | bytes 196616 | tf_op jit(solution)/shard_map/ppermute | solution.py:418

commit v5 on v4

--- a/solution.py
+++ b/solution.py
@@ -158,14 +158,8 @@
 
 
 def back_kernel(lo, hi, pairs, src_ref, book_ref, wt_ref, pg_ref, *refs):
-    refs, back_ref = refs[:-1], refs[-1]
-    if lo > 0:
-        before_ref, refs = refs[0], refs[1:]
-    if hi < pairs:
-        (table_ref,) = refs
-    else:
-        local_ref, *far_refs, table_ref = refs
-    table_ref[...] = jnp.zeros_like(table_ref) if lo == 0 else before_ref[...]
+    *before_refs, table_ref, back_ref = refs
+    table_ref[...] = jnp.zeros_like(table_ref) if lo == 0 else before_refs[0][...]
     kvol = book_ref.shape[1]
     ids = sub_iota(BLOCK, BF)
 
@@ -185,16 +179,17 @@
 
     if hi == pairs:
         some(pairs - 1, 1)
-        blocks = local_ref.shape[0] // BLOCK
-        for b in range(blocks):
-            local_ref[b * BLOCK : (b + 1) * BLOCK, :] = table_ref[b]
-        for slot, far_ref in zip(slot_order(core_id()), far_refs):
-            each = far_ref.shape[0] // BLOCK
-            for one in range(each):
-                far_ref[one * BLOCK : (one + 1) * BLOCK, :] = table_ref[blocks + each * slot + one].astype(BF)
-
-
-def add_kernel(local_ref, rows_ref, g0_ref, g1_ref, g2_ref, g3_ref, out_ref, ret_ref):
+
+
+def far_kernel(table_ref, *far_refs):
+    each = far_refs[0].shape[0] // BLOCK
+    blocks = table_ref.shape[0] - 1 - 4 * each
+    for slot, far_ref in zip(slot_order(core_id()), far_refs):
+        for one in range(each):
+            far_ref[one * BLOCK : (one + 1) * BLOCK, :] = table_ref[blocks + each * slot + one].astype(BF)
+
+
+def add_kernel(table_ref, rows_ref, g0_ref, g1_ref, g2_ref, g3_ref, out_ref, ret_ref):
     blocks = out_ref.shape[0] // BLOCK
     length = rows_ref.shape[1]
     ids = sub_iota(BLOCK, BF)
@@ -212,41 +207,39 @@
     for b in range(blocks):
         hot = jnp.concatenate([onehot_t((row - b * BLOCK).astype(F32), ids) for row in groups], axis=1)
         spot = slice(b * BLOCK, (b + 1) * BLOCK)
-        out_ref[spot, :] = local_ref[spot, :] + mm(hot, ret_ref[...])
+        out_ref[spot, :] = table_ref[b] + mm(hot, ret_ref[...])
 
 
 def wide(v):
     return v.astype(F32)
 
 
+def first_axis():
+    return jnp.where(core_id() == 0, lax.axis_index("slab"), lax.axis_index("tile") >> 3)
+
+
 def quarter_at(n, m):
     return pl.ds(pl.multiple_of((n & 3) * m, m), m)
 
 
 def pair_kernel(keep_ref, swap_ref, mine_ref, *piece_refs):
     m = mine_ref.shape[0]
-    slab = lax.axis_index("slab")
+    place = first_axis()
     for sh, out_ref in enumerate((mine_ref, *piece_refs)):
-        at = quarter_at(slab + sh, m)
+        at = quarter_at(place + sh, m)
         out_ref[...] = (wide(keep_ref[at, :]) + wide(swap_ref[at, :])).astype(BF)
 
 
-def four_kernel(own_ref, g1_ref, g2_ref, g3_ref, *refs):
-    outs = refs[0:1] if len(refs) == 1 else refs[2:]
+def four_kernel(own_ref, g1_ref, g2_ref, g3_ref, out_ref):
     total = (wide(own_ref[...]) + wide(g2_ref[...])) + (wide(g1_ref[...]) + wide(g3_ref[...]))
-    m = own_ref.shape[0]
-    for out_ref in outs:
-        out_ref[0:m, :] = total.astype(BF)
-    if len(outs) > 1:
-        outs[1][m:, :] = refs[0][...]
-        outs[2][m:, :] = refs[1][...]
+    out_ref[...] = total.astype(BF)
 
 
 def join_kernel(own_ref, g1_ref, g2_ref, g3_ref, full_ref):
     m = own_ref.shape[0]
-    slab = lax.axis_index("slab") + 4
+    place = first_axis() + 4
     for sh, ref in enumerate((own_ref, g1_ref, g2_ref, g3_ref)):
-        full_ref[quarter_at(slab - sh, m), :] = ref[0:m, :]
+        full_ref[quarter_at(place - sh, m), :] = ref[...]
 
 
 def spread_kernel(own_ref, other_ref, conv_ref, down_ref):
@@ -360,15 +353,12 @@
 
     def back_part(acc, lo, hi):
         ins = (source, here(inner), here(wt), here(pg)) + (() if acc is None else (here(acc),))
-        whole = ((table, BLOCK, BLOCK), F32, near)
-        scratch = [pltpu.VMEM((2 * BLOCK, kvol * BLOCK), BF)]
-        if hi < pairs:
-            outs = [whole]
-        else:
-            outs = [((row_count, chans), F32, near)] + [((list_len, chans), BF, near)] * 4
-            scratch = [pltpu.VMEM(*whole[:2])] + scratch
         return call(
-            12, functools.partial(back_kernel, lo, hi, pairs), outs, [SM] + [VM] * (len(ins) - 1), scratch
+            12,
+            functools.partial(back_kernel, lo, hi, pairs),
+            [((table, BLOCK, BLOCK), F32, near)],
+            [SM] + [VM] * (len(ins) - 1),
+            [pltpu.VMEM((2 * BLOCK, kvol * BLOCK), BF)],
         )(*ins)
 
     stride = {"c": 1, "z": 2, "y": 8, "x": tiles}
@@ -384,44 +374,45 @@
         return lax.ppermute(v, ("slab", "tile"), links)
 
     def shifts(axes, pieces):
-        return [send(v, axes, lambda q, sh=sh: q + sh) for sh, v in zip((1, 2, 3), pieces)]
-
-    order = ("xx", "yz", "zy", "xx")
+        sent = {}
+        for sh in (1, 3, 2) if pieces[0] is not pieces[1] else (2, 1, 3):
+            sent[sh] = send(pieces[sh - 1], axes, lambda q, sh=sh: q + sh)
+        return [sent[sh] for sh in (1, 2, 3)]
+
+    order = ("xy", "yz", "zx", "xy")
     swap = send(give, "cc", lambda q: 1 - q)
-    acc = back_part(None, 0, 2)
+    acc = back_part(None, 0, 1)
     swap, acc = tie(swap, acc)
     m = part_rows // 8
     near_piece = ((m, out_chans), BF, near)
-    long_piece = ((m + list_len, out_chans), BF, near)
     y, *pieces = call(8, pair_kernel, [near_piece] * 4, [VM] * 2)(here(keep), here(swap))
 
-    for ph, (lo, hi) in enumerate(((2, 4), (4, 6), (6, 8))):
+    for ph, (lo, hi) in enumerate(((1, 4), (4, pairs), (pairs, pairs))):
         y, acc = tie(y, acc)
         got = shifts(order[ph], pieces)
-        result = back_part(acc, lo, hi)
-        if hi < pairs:
-            acc = result
+        if lo < hi:
+            acc = back_part(acc, lo, hi)
             *got, acc = tie(*got, acc)
-            y = call(8, four_kernel, [near_piece], [VM] * 4)(*map(here, (y, *got)))
-            pieces = [y] * 3
         else:
-            *got, local, far0, far1, far2, far3 = tie(*got, *result)
-            y, low, high = call(8, four_kernel, [near_piece, long_piece, long_piece], [VM] * 6)(
-                *map(here, (y, *got, far0, far1))
-            )
-
-    got = shifts(order[3], [high, y, low])
-    returned = [
-        got[2],
-        got[0],
-        lax.ppermute(far2, "tile", chip),
-        lax.ppermute(far3, "tile", beside),
-    ]
+            far = call(8, far_kernel, [((list_len, chans), BF, near)] * 4, [VM])(here(acc))
+            returned = [
+                lax.ppermute(far[0], "slab", down),
+                lax.ppermute(far[1], "slab", up),
+                lax.ppermute(far[2], "tile", chip),
+                lax.ppermute(far[3], "tile", beside),
+            ]
+            g1, g2, g3, *returned = tie(*got, *returned)
+            got = [g1, g2, g3]
+        y = call(8, four_kernel, [near_piece], [VM] * 4)(*map(here, (y, *got)))
+        pieces = [y] * 3
+
+    got = shifts(order[3], [y] * 3)
+    input_grad = call(
+        12, add_kernel, [((row_count, chans), F32)], [VM] * 6, [pltpu.VMEM((far_rows, chans), BF)]
+    )(here(acc), afar(boundary_rows), *map(here, returned))
+    *got, input_grad = tie(*got, input_grad)
     full = call(8, join_kernel, [((4 * m, out_chans), BF, near)], [VM] * 4)(*map(here, (y, *got)))
     other = send(full, "cc", lambda q: 1 - q)
-    input_grad = call(
-        12, add_kernel, [((row_count, chans), F32)], [VM] * 6, [pltpu.VMEM((far_rows, chans), BF)]
-    )(here(local), afar(boundary_rows), *map(here, returned))
     conv_grad, down_grad = call(
         12,
         spread_kernel,

time: 93.9 us -> 91.5 us (0.974)
  waiting for transfers between devices: 18 us -> 11.5 us
  starting transfers between devices: 36.6 us -> 41.1 us
    ppermute x14, waiting for transfers between devices: 13.9 us -> 5.75 us  [send(): return lax.ppermute(v, ('slab', 'tile'), links)]
    ppermute x2 -> x4, starting transfers between devices: 4.04 us -> 9.61 us  [the longest x1 4.55 us: body(): lax.ppermute(far[1], 'slab', up)]
    ppermute x2 -> x4, waiting for transfers between devices: 4.13 us -> 5.78 us  [the longest x1 3.89 us: body(): lax.ppermute(far[3], 'tile', beside)]
    ppermute x14, starting transfers between devices: 21.8 us -> 20.8 us  [send(): return lax.ppermute(v, ('slab', 'tile'), links)]
    pallas_call x5 -> x4, Pallas kernels: 11.9 us -> 11 us  [the longest x3 11 us: back_part(): call(12, functools.partial(back_kernel, lo, hi, pairs), [((table, BLOCK,...]
  transfers between devices with their start and end apart: 20 -> 22, of which waited for: 8 -> 6; matrix products, arithmetic and copies ran while one was open for 0% -> 0% of each run, Pallas kernels for 18% -> 18%
where the time goes in v5:
time: 91.5 us; the launch traced here: 90.8 us
  starting transfers between devices  41.1 us (45%)
  Pallas kernels  37.3 us (41%)
  waiting for transfers between devices  11.5 us (13%)
    ppermute x14, starting transfers between devices, send(): return lax.ppermute(v, ('slab', 'tile'), links)  20.8 us
    pallas_call x1, Pallas kernels, body(): call(32, main_kernel, [((coarse_rows, out_chans), BF), ((pairs, 2 * BLOCK...  16.8 us
    pallas_call x3, Pallas kernels, back_part(): call(12, functools.partial(back_kernel, lo, hi, pairs), [((table, BLOCK,...  11 us
    ppermute x1, starting transfers between devices, body(): lax.ppermute(outgoing[3], 'tile', beside)  5.92 us
    ppermute x14, waiting for transfers between devices, send(): return lax.ppermute(v, ('slab', 'tile'), links)  5.75 us
    ppermute x1, starting transfers between devices, body(): lax.ppermute(far[1], 'slab', up)  4.55 us
    ppermute x1, waiting for transfers between devices, body(): lax.ppermute(far[3], 'tile', beside)  3.89 us
    ppermute x1, starting transfers between devices, body(): lax.ppermute(far[3], 'tile', beside)  3.77 us
  transfers between devices with their start and end apart: 22, of which 6 were waited for; matrix products, arithmetic and copies ran while one was open for 0% of the time, Pallas kernels for 18%

profile of v5, /device:TPU:8, one launch (start us, length us, event | category | flops | bytes accessed | tf_op | source)
XLA Modules:
  0.0 90.8 jit_solution(5959597663039481270)
XLA Ops:
  0.6 2.6 %shard_map.103 = (bf16[256,128]{1,0:T(8,128)(2,1)S(1)}, bf16[256,128]{1,0:T(8,128)(2,1)S(1)}, bf16[256,128]{1,0:T(8,128)(2,1)S(1)}, bf16[256,128]{1,0:T(8,128)(2,1)S(1)}, bf16[16,128,128]{2,1,0:T(8,128)(2,1)S(1)}) custom-call(bf16[2048,128]{1,0:T(8,128)(2,1)} %feat_ref.1, s32[4,256]{1,0:T(4,128)} %rows_ref.3), custom_call_target="tpu_custom_call" | custom-call | tf_op jit(solution)/shard_map/pallas_call | solution.py:303
  3.2 3.4 %collective-permute-start = (bf16[256,128]{1,0:T(8,128)(2,1)S(1)}, bf16[256,128]{1,0:T(8,128)(2,1)S(1)}, u32[]{:S(2)}, u32[]{:S(2)}) collective-permute-start(bf16[256,128]{1,0:T(8,128)(2,1)S(1)} %get-tuple-element.57), channel_id=1, source_target_pairs={{0,32},{32,64},{64,96},{1,33},{33,65},{65,97},{2,34},{34,66},{66,9... | collective-permute-start | bytes 196616 | tf_op jit(solution)/shard_map/ppermute | solution.py:315
  6.6 1.3 %collective-permute-start.1 = (bf16[256,128]{1,0:T(8,128)(2,1)S(1)}, bf16[256,128]{1,0:T(8,128)(2,1)S(1)}, u32[]{:S(2)}, u32[]{:S(2)}) collective-permute-start(bf16[256,128]{1,0:T(8,128)(2,1)S(1)} %get-tuple-element.58), channel_id=1, source_target_pairs={{32,0},{64,32},{96,64},{33,1},{65,33},{97,65},{34,2},{66,34},{98,6... | collective-permute-start | bytes 196616 | tf_op jit(solution)/shard_map/ppermute | solution.py:316
  7.9 0.1 collective-permute-start.2
  8.0 5.9 %collective-permute-start.3 = (bf16[256,128]{1,0:T(8,128)(2,1)S(1)}, bf16[256,128]{1,0:T(8,128)(2,1)S(1)}, u32[]{:S(2)}, u32[]{:S(2)}) collective-permute-start(bf16[256,128]{1,0:T(8,128)(2,1)S(1)} %get-tuple-element.60), channel_id=1, source_target_pairs={{1,2},{2,1},{3,4},{4,3},{5,6},{6,5},{7,8},{8,7},{9,10},{10,9},{11,... | collective-permute-start | bytes 196616 | tf_op jit(solution)/shard_map/ppermute | solution.py:318
  13.9 2.0 %shard_map.102 = (s32[27,128]{1,0:T(8,128)S(1)}, f32[16,27,128]{2,1,0:T(8,128)S(1)}, f32[16,128]{1,0:T(8,128)S(1)}, bf16[128,3456]{1,0:T(8,128)(2,1)S(1)}, bf16[16,256,128]{2,1,0:T(8,128)(2,1)S(1)}) custom-call(s32[27,2048]{1,0:T(8,128)} %book_ref.1, s32[1,2048]{1,0:T(1,128)} %bitcast.3, bf16[27,128,128]{2,1,0:T(8,128)(2,1)} %w_ref.1, ...), custom_call_target="tpu_custom_call" | custom-call | tf_op jit(solution)/shard_map/pallas_call | solution.py:320
  16.0 16.8 %shard_map.104 = (bf16[512,128]{1,0:T(8,128)(2,1)}, bf16[8,256,128]{2,1,0:T(8,128)(2,1)S(1)}, bf16[2304,128]{1,0:T(8,128)(2,1)S(1)}, bf16[2304,128]{1,0:T(8,128)(2,1)S(1)}) custom-call(s32[27,128]{1,0:T(8,128)S(1)} %get-tuple-element.55.src_ref, bf16[16,128,128]{2,1,0:T(8,128)(2,1)S(1)} %get-tuple-element.56.xt_loc_ref, ...), custom_call_target="tpu_custom_call" | custom-call | tf_op jit(solution)/shard_map/pallas_call | solution.py:336
  32.9 2.0 %shard_map.105.refs_0_ = f32[25,128,128]{2,1,0:T(8,128)S(1)} custom-call(s32[27,128]{1,0:T(8,128)S(1)} %get-tuple-element.55.src_ref, f32[16,27,128]{2,1,0:T(8,128)S(1)} %get-tuple-element.61.book_ref, bf16[128,3456]{1,0:T(8,128)(2,1)S(1)} %get-tuple-element.63.wt_ref, bf16[8,256,128]{2,1,0:T(8,128)(2,1)S(1)} %get-tuple-element.68.pg_ref), custom_call_target="tpu_custom_call" | custom-call | tf_op jit(solution)/shard_map/pallas_call | solution.py:356
  34.9 0.2 shard_map.106
  35.1 2.7 %collective-permute-start.5 = (bf16[576,128]{1,0:T(8,128)(2,1)S(1)}, bf16[576,128]{1,0:T(8,128)(2,1)S(1)}, u32[]{:S(2)}, u32[]{:S(2)}) collective-permute-start(bf16[576,128]{1,0:T(8,128)(2,1)S(1)} %get-tuple-element.73), channel_id=1, source_target_pairs={{0,32},{1,9},{2,34},{3,11},{4,36},{5,13},{6,38},{7,15},{8,40},{9,1... | collective-permute-start | bytes 442376 | tf_op jit(solution)/shard_map/ppermute | solution.py:374
  37.8 2.7 %collective-permute-start.6 = (bf16[576,128]{1,0:T(8,128)(2,1)S(1)}, bf16[576,128]{1,0:T(8,128)(2,1)S(1)}, u32[]{:S(2)}, u32[]{:S(2)}) collective-permute-start(bf16[576,128]{1,0:T(8,128)(2,1)S(1)} %get-tuple-element.74), channel_id=1, source_target_pairs={{0,64},{1,17},{2,66},{3,19},{4,68},{5,21},{6,70},{7,23},{8,72},{9,... | collective-permute-start | bytes 442376 | tf_op jit(solution)/shard_map/ppermute | solution.py:374
  40.5 1.4 %collective-permute-start.7 = (bf16[576,128]{1,0:T(8,128)(2,1)S(1)}, bf16[576,128]{1,0:T(8,128)(2,1)S(1)}, u32[]{:S(2)}, u32[]{:S(2)}) collective-permute-start(bf16[576,128]{1,0:T(8,128)(2,1)S(1)} %get-tuple-element.75), channel_id=1, source_target_pairs={{0,96},{1,25},{2,98},{3,27},{4,100},{5,29},{6,102},{7,31},{8,104},... | collective-permute-start | bytes 442376 | tf_op jit(solution)/shard_map/ppermute | solution.py:374
  41.9 4.2 %shard_map.107.refs_0_ = f32[25,128,128]{2,1,0:T(8,128)S(1)} custom-call(s32[27,128]{1,0:T(8,128)S(1)} %get-tuple-element.55.src_ref, f32[16,27,128]{2,1,0:T(8,128)S(1)} %get-tuple-element.61.book_ref, bf16[128,3456]{1,0:T(8,128)(2,1)S(1)} %get-tuple-element.63.wt_ref, bf16[8,256,128]{2,1,0:T(8,128)(2,1)S(1)} %get-tuple-element.68.pg_ref, ...), custom_call_target="tpu_custom_call" | custom-call | tf_op jit(solution)/shard_map/pallas_call | solution.py:356
  46.3 3.0 %collective-permute-start.9 = (bf16[576,128]{1,0:T(8,128)(2,1)S(1)}, bf16[576,128]{1,0:T(8,128)(2,1)S(1)}, u32[]{:S(2)}, u32[]{:S(2)}) collective-permute-start(bf16[576,128]{1,0:T(8,128)(2,1)S(1)} %shard_map.108.own_ref), channel_id=1, source_target_pairs={{0,16},{1,5},{2,18},{3,7},{4,20},{5,1},{6,22},{7,3},{8,24},{9,13},... | collective-permute-start | bytes 442376 | tf_op jit(solution)/shard_map/ppermute | solution.py:374
  49.4 2.2 %collective-permute-start.8 = (bf16[576,128]{1,0:T(8,128)(2,1)S(1)}, bf16[576,128]{1,0:T(8,128)(2,1)S(1)}, u32[]{:S(2)}, u32[]{:S(2)}) collective-permute-start(bf16[576,128]{1,0:T(8,128)(2,1)S(1)} %shard_map.108.own_ref), channel_id=1, source_target_pairs={{0,8},{1,3},{2,10},{3,5},{4,12},{5,7},{6,14},{7,1},{8,16},{9,11},{... | collective-permute-start | bytes 442376 | tf_op jit(solution)/shard_map/ppermute | solution.py:374
  51.5 4.8 %shard_map.109.table_ref = f32[25,128,128]{2,1,0:T(8,128)S(1)} custom-call(s32[27,128]{1,0:T(8,128)S(1)} %get-tuple-element.55.src_ref, f32[16,27,128]{2,1,0:T(8,128)S(1)} %get-tuple-element.61.book_ref, bf16[128,3456]{1,0:T(8,128)(2,1)S(1)} %get-tuple-element.63.wt_ref, bf16[8,256,128]{2,1,0:T(8,128)(2,1)S(1)} %get-tuple-element.68.pg_ref, ...), custom_call_target="tpu_custom_call" | custom-call | tf_op jit(solution)/shard_map/pallas_call | solution.py:356
  56.5 3.0 %collective-permute-start.13 = (bf16[576,128]{1,0:T(8,128)(2,1)S(1)}, bf16[576,128]{1,0:T(8,128)(2,1)S(1)}, u32[]{:S(2)}, u32[]{:S(2)}) collective-permute-start(bf16[576,128]{1,0:T(8,128)(2,1)S(1)} %shard_map.110.own_ref), channel_id=1, source_target_pairs={{0,6},{1,97},{2,0},{3,99},{4,2},{5,101},{6,4},{7,103},{8,14},{9,10... | collective-permute-start | bytes 442376 | tf_op jit(solution)/shard_map/ppermute | solution.py:374
  59.5 0.9 %collective-permute-start.11 = (bf16[576,128]{1,0:T(8,128)(2,1)S(1)}, bf16[576,128]{1,0:T(8,128)(2,1)S(1)}, u32[]{:S(2)}, u32[]{:S(2)}) collective-permute-start(bf16[576,128]{1,0:T(8,128)(2,1)S(1)} %shard_map.110.own_ref), channel_id=1, source_target_pairs={{0,2},{1,33},{2,4},{3,35},{4,6},{5,37},{6,0},{7,39},{8,10},{9,41},... | collective-permute-start | bytes 442376 | tf_op jit(solution)/shard_map/ppermute | solution.py:374
  60.5 1.3 %collective-permute-start.14 = (bf16[256,128]{1,0:T(8,128)(2,1)S(1)}, bf16[256,128]{1,0:T(8,128)(2,1)S(1)}, u32[]{:S(2)}, u32[]{:S(2)}) collective-permute-start(bf16[256,128]{1,0:T(8,128)(2,1)S(1)} %get-tuple-element.89), channel_id=1, source_target_pairs={{32,0},{64,32},{96,64},{33,1},{65,33},{97,65},{34,2},{66,34},{98,6... | collective-permute-start | bytes 196616 | tf_op jit(solution)/shard_map/ppermute | solution.py:399
  61.8 4.5 %collective-permute-start.15 = (bf16[256,128]{1,0:T(8,128)(2,1)S(1)}, bf16[256,128]{1,0:T(8,128)(2,1)S(1)}, u32[]{:S(2)}, u32[]{:S(2)}) collective-permute-start(bf16[256,128]{1,0:T(8,128)(2,1)S(1)} %get-tuple-element.90), channel_id=1, source_target_pairs={{0,32},{32,64},{64,96},{1,33},{33,65},{65,97},{2,34},{34,66},{66,9... | collective-permute-start | bytes 196616 | tf_op jit(solution)/shard_map/ppermute | solution.py:400
  66.3 0.3 collective-permute-done.14.g0_ref
  66.6 1.6 %collective-permute-done.15.g1_ref = bf16[256,128]{1,0:T(8,128)(2,1)S(1)} collective-permute-done((bf16[256,128]{1,0:T(8,128)(2,1)S(1)}, bf16[256,128]{1,0:T(8,128)(2,1)S(1)}, u32[]{:S(2)}, u32[]{:S(2)}) %collective-permute-start.15) | collective-permute-done | bytes 65568 | tf_op jit(solution)/shard_map/ppermute | solution.py:400
  68.2 3.8 %collective-permute-start.17 = (bf16[256,128]{1,0:T(8,128)(2,1)S(1)}, bf16[256,128]{1,0:T(8,128)(2,1)S(1)}, u32[]{:S(2)}, u32[]{:S(2)}) collective-permute-start(bf16[256,128]{1,0:T(8,128)(2,1)S(1)} %get-tuple-element.92), channel_id=1, source_target_pairs={{1,2},{2,1},{3,4},{4,3},{5,6},{6,5},{7,8},{8,7},{9,10},{10,9},{11,... | collective-permute-start | bytes 196616 | tf_op jit(solution)/shard_map/ppermute | solution.py:402
  72.0 3.9 %collective-permute-done.17.g3_ref = bf16[256,128]{1,0:T(8,128)(2,1)S(1)} collective-permute-done((bf16[256,128]{1,0:T(8,128)(2,1)S(1)}, bf16[256,128]{1,0:T(8,128)(2,1)S(1)}, u32[]{:S(2)}, u32[]{:S(2)}) %collective-permute-start.17) | collective-permute-done | bytes 65568 | tf_op jit(solution)/shard_map/ppermute | solution.py:402
  76.0 2.9 %collective-permute-start.20 = (bf16[576,128]{1,0:T(8,128)(2,1)S(1)}, bf16[576,128]{1,0:T(8,128)(2,1)S(1)}, u32[]{:S(2)}, u32[]{:S(2)}) collective-permute-start(bf16[576,128]{1,0:T(8,128)(2,1)S(1)} %shard_map.112.own_ref), channel_id=1, source_target_pairs={{0,96},{1,25},{2,98},{3,27},{4,100},{5,29},{6,102},{7,31},{8,104},... | collective-permute-start | bytes 442376 | tf_op jit(solution)/shard_map/ppermute | solution.py:374
  78.9 1.6 %collective-permute-start.19 = (bf16[576,128]{1,0:T(8,128)(2,1)S(1)}, bf16[576,128]{1,0:T(8,128)(2,1)S(1)}, u32[]{:S(2)}, u32[]{:S(2)}) collective-permute-start(bf16[576,128]{1,0:T(8,128)(2,1)S(1)} %shard_map.112.own_ref), channel_id=1, source_target_pairs={{0,64},{1,17},{2,66},{3,19},{4,68},{5,21},{6,70},{7,23},{8,72},{9,... | collective-permute-start | bytes 442376 | tf_op jit(solution)/shard_map/ppermute | solution.py:374
  80.5 2.9 %shard_map.113 = f32[2048,128]{1,0:T(8,128)} custom-call(f32[25,128,128]{2,1,0:T(8,128)S(1)} %shard_map.109.table_ref, s32[4,256]{1,0:T(4,128)} %rows_ref.3, bf16[256,128]{1,0:T(8,128)(2,1)S(1)} %collective-permute-done.14.g0_ref, bf16[256,128]{1,0:T(8,128)(2,1)S(1)} %collective-permute-done.15.g1_ref, bf16[256,128]{1,0:T(8,128)(2,1)S(1)} %collective-permute-done.16.g2_ref, ...), custom_call_target="tpu_custom_call" | custom-call | tf_op jit(solution)/shard_map/pallas_call | solution.py:410
  83.4 2.2 %collective-permute-done.19.g2_ref = bf16[576,128]{1,0:T(8,128)(2,1)S(1)} collective-permute-done((bf16[576,128]{1,0:T(8,128)(2,1)S(1)}, bf16[576,128]{1,0:T(8,128)(2,1)S(1)}, u32[]{:S(2)}, u32[]{:S(2)}) %collective-permute-start.19) | collective-permute-done | bytes 147488 | tf_op jit(solution)/shard_map/ppermute | solution.py:374
  85.6 1.5 %collective-permute-done.18.g1_ref = bf16[576,128]{1,0:T(8,128)(2,1)S(1)} collective-permute-done((bf16[576,128]{1,0:T(8,128)(2,1)S(1)}, bf16[576,128]{1,0:T(8,128)(2,1)S(1)}, u32[]{:S(2)}, u32[]{:S(2)}) %collective-permute-start.18) | collective-permute-done | bytes 147488 | tf_op jit(solution)/shard_map/ppermute | solution.py:374
  87.2 0.1 collective-permute-start.21
  87.3 2.0 %collective-permute-done.21.other_ref = bf16[2304,128]{1,0:T(8,128)(2,1)S(1)} collective-permute-done((bf16[2304,128]{1,0:T(8,128)(2,1)S(1)}, bf16[2304,128]{1,0:T(8,128)(2,1)S(1)}, u32[]{:S(2)}, u32[]{:S(2)}) %collective-permute-start.21) | collective-permute-done | bytes 589856 | tf_op jit(solution)/shard_map/ppermute | solution.py:374
  89.3 1.5 %shard_map.115 = (f32[3456,128]{1,0:T(8,128)}, f32[1024,128]{1,0:T(8,128)}) custom-call(bf16[2304,128]{1,0:T(8,128)(2,1)S(1)} %shard_map.114.own_ref, bf16[2304,128]{1,0:T(8,128)(2,1)S(1)} %collective-permute-done.21.other_ref), custom_call_target="tpu_custom_call" | custom-call | tf_op jit(solution)/shard_map/pallas_call | solution.py:416
  (26 shorter events, 0.5 us)
Async XLA Ops:
  3.2 12.8 %collective-permute-start = (bf16[256,128]{1,0:T(8,128)(2,1)S(1)}, bf16[256,128]{1,0:T(8,128)(2,1)S(1)}, u32[]{:S(2)}, u32[]{:S(2)}) collective-permute-start(bf16[256,128]{1,0:T(8,128)(2,1)S(1)} %get-tuple-element.57), channel_id=1, source_target_pairs={{0,32},{32,64},{64,96},{1,33},{33,65},{65,97},{2,34},{34,66},{66,9... | collective-permute-start | bytes 196616 | tf_op jit(solution)/shard_map/ppermute | solution.py:315
  6.6 9.4 %collective-permute-start.1 = (bf16[256,128]{1,0:T(8,128)(2,1)S(1)}, bf16[256,128]{1,0:T(8,128)(2,1)S(1)}, u32[]{:S(2)}, u32[]{:S(2)}) collective-permute-start(bf16[256,128]{1,0:T(8,128)(2,1)S(1)} %get-tuple-element.58), channel_id=1, source_target_pairs={{32,0},{64,32},{96,64},{33,1},{65,33},{97,65},{34,2},{66,34},{98,6... | collective-permute-start | bytes 196616 | tf_op jit(solution)/shard_map/ppermute | solution.py:316
  7.9 8.1 %collective-permute-start.2 = (bf16[256,128]{1,0:T(8,128)(2,1)S(1)}, bf16[256,128]{1,0:T(8,128)(2,1)S(1)}, u32[]{:S(2)}, u32[]{:S(2)}) collective-permute-start(bf16[256,128]{1,0:T(8,128)(2,1)S(1)} %get-tuple-element.59), channel_id=1, source_target_pairs={{0,1},{1,0},{2,3},{3,2},{4,5},{5,4},{6,7},{7,6},{8,9},{9,8},{10,11... | collective-permute-start | bytes 196616 | tf_op jit(solution)/shard_map/ppermute | solution.py:317
  8.0 8.0 %collective-permute-start.3 = (bf16[256,128]{1,0:T(8,128)(2,1)S(1)}, bf16[256,128]{1,0:T(8,128)(2,1)S(1)}, u32[]{:S(2)}, u32[]{:S(2)}) collective-permute-start(bf16[256,128]{1,0:T(8,128)(2,1)S(1)} %get-tuple-element.60), channel_id=1, source_target_pairs={{1,2},{2,1},{3,4},{4,3},{5,6},{6,5},{7,8},{8,7},{9,10},{10,9},{11,... | collective-permute-start | bytes 196616 | tf_op jit(solution)/shard_map/ppermute | solution.py:318
  32.8 2.1 %collective-permute-start.4 = (bf16[2304,128]{1,0:T(8,128)(2,1)S(1)}, bf16[2304,128]{1,0:T(8,128)(2,1)S(1)}, u32[]{:S(2)}, u32[]{:S(2)}) collective-permute-start(bf16[2304,128]{1,0:T(8,128)(2,1)S(1)} %get-tuple-element.67), channel_id=1, source_target_pairs={{0,1},{1,0},{2,3},{3,2},{4,5},{5,4},{6,7},{7,6},{8,9},{9,8},{10,11... | collective-permute-start | bytes 1769480 | tf_op jit(solution)/shard_map/ppermute | solution.py:374
  35.1 11.1 %collective-permute-start.5 = (bf16[576,128]{1,0:T(8,128)(2,1)S(1)}, bf16[576,128]{1,0:T(8,128)(2,1)S(1)}, u32[]{:S(2)}, u32[]{:S(2)}) collective-permute-start(bf16[576,128]{1,0:T(8,128)(2,1)S(1)} %get-tuple-element.73), channel_id=1, source_target_pairs={{0,32},{1,9},{2,34},{3,11},{4,36},{5,13},{6,38},{7,15},{8,40},{9,1... | collective-permute-start | bytes 442376 | tf_op jit(solution)/shard_map/ppermute | solution.py:374
  37.8 8.4 %collective-permute-start.6 = (bf16[576,128]{1,0:T(8,128)(2,1)S(1)}, bf16[576,128]{1,0:T(8,128)(2,1)S(1)}, u32[]{:S(2)}, u32[]{:S(2)}) collective-permute-start(bf16[576,128]{1,0:T(8,128)(2,1)S(1)} %get-tuple-element.74), channel_id=1, source_target_pairs={{0,64},{1,17},{2,66},{3,19},{4,68},{5,21},{6,70},{7,23},{8,72},{9,... | collective-permute-start | bytes 442376 | tf_op jit(solution)/shard_map/ppermute | solution.py:374
  40.5 5.7 %collective-permute-start.7 = (bf16[576,128]{1,0:T(8,128)(2,1)S(1)}, bf16[576,128]{1,0:T(8,128)(2,1)S(1)}, u32[]{:S(2)}, u32[]{:S(2)}) collective-permute-start(bf16[576,128]{1,0:T(8,128)(2,1)S(1)} %get-tuple-element.75), channel_id=1, source_target_pairs={{0,96},{1,25},{2,98},{3,27},{4,100},{5,29},{6,102},{7,31},{8,104},... | collective-permute-start | bytes 442376 | tf_op jit(solution)/shard_map/ppermute | solution.py:374
  46.2 10.1 %collective-permute-start.10 = (bf16[576,128]{1,0:T(8,128)(2,1)S(1)}, bf16[576,128]{1,0:T(8,128)(2,1)S(1)}, u32[]{:S(2)}, u32[]{:S(2)}) collective-permute-start(bf16[576,128]{1,0:T(8,128)(2,1)S(1)} %shard_map.108.own_ref), channel_id=1, source_target_pairs={{0,24},{1,7},{2,26},{3,1},{4,28},{5,3},{6,30},{7,5},{8,0},{9,15},{... | collective-permute-start | bytes 442376 | tf_op jit(solution)/shard_map/ppermute | solution.py:374
  46.3 10.0 %collective-permute-start.9 = (bf16[576,128]{1,0:T(8,128)(2,1)S(1)}, bf16[576,128]{1,0:T(8,128)(2,1)S(1)}, u32[]{:S(2)}, u32[]{:S(2)}) collective-permute-start(bf16[576,128]{1,0:T(8,128)(2,1)S(1)} %shard_map.108.own_ref), channel_id=1, source_target_pairs={{0,16},{1,5},{2,18},{3,7},{4,20},{5,1},{6,22},{7,3},{8,24},{9,13},... | collective-permute-start | bytes 442376 | tf_op jit(solution)/shard_map/ppermute | solution.py:374
  49.4 7.0 %collective-permute-start.8 = (bf16[576,128]{1,0:T(8,128)(2,1)S(1)}, bf16[576,128]{1,0:T(8,128)(2,1)S(1)}, u32[]{:S(2)}, u32[]{:S(2)}) collective-permute-start(bf16[576,128]{1,0:T(8,128)(2,1)S(1)} %shard_map.108.own_ref), channel_id=1, source_target_pairs={{0,8},{1,3},{2,10},{3,5},{4,12},{5,7},{6,14},{7,1},{8,16},{9,11},{... | collective-permute-start | bytes 442376 | tf_op jit(solution)/shard_map/ppermute | solution.py:374
  56.5 19.4 %collective-permute-start.13 = (bf16[576,128]{1,0:T(8,128)(2,1)S(1)}, bf16[576,128]{1,0:T(8,128)(2,1)S(1)}, u32[]{:S(2)}, u32[]{:S(2)}) collective-permute-start(bf16[576,128]{1,0:T(8,128)(2,1)S(1)} %shard_map.110.own_ref), channel_id=1, source_target_pairs={{0,6},{1,97},{2,0},{3,99},{4,2},{5,101},{6,4},{7,103},{8,14},{9,10... | collective-permute-start | bytes 442376 | tf_op jit(solution)/shard_map/ppermute | solution.py:374
  59.5 16.4 %collective-permute-start.12 = (bf16[576,128]{1,0:T(8,128)(2,1)S(1)}, bf16[576,128]{1,0:T(8,128)(2,1)S(1)}, u32[]{:S(2)}, u32[]{:S(2)}) collective-permute-start(bf16[576,128]{1,0:T(8,128)(2,1)S(1)} %shard_map.110.own_ref), channel_id=1, source_target_pairs={{0,4},{1,65},{2,6},{3,67},{4,0},{5,69},{6,2},{7,71},{8,12},{9,73},... | collective-permute-start | bytes 442376 | tf_op jit(solution)/shard_map/ppermute | solution.py:374
  59.5 16.4 %collective-permute-start.11 = (bf16[576,128]{1,0:T(8,128)(2,1)S(1)}, bf16[576,128]{1,0:T(8,128)(2,1)S(1)}, u32[]{:S(2)}, u32[]{:S(2)}) collective-permute-start(bf16[576,128]{1,0:T(8,128)(2,1)S(1)} %shard_map.110.own_ref), channel_id=1, source_target_pairs={{0,2},{1,33},{2,4},{3,35},{4,6},{5,37},{6,0},{7,39},{8,10},{9,41},... | collective-permute-start | bytes 442376 | tf_op jit(solution)/shard_map/ppermute | solution.py:374
  60.5 6.2 %collective-permute-start.14 = (bf16[256,128]{1,0:T(8,128)(2,1)S(1)}, bf16[256,128]{1,0:T(8,128)(2,1)S(1)}, u32[]{:S(2)}, u32[]{:S(2)}) collective-permute-start(bf16[256,128]{1,0:T(8,128)(2,1)S(1)} %get-tuple-element.89), channel_id=1, source_target_pairs={{32,0},{64,32},{96,64},{33,1},{65,33},{97,65},{34,2},{66,34},{98,6... | collective-permute-start | bytes 196616 | tf_op jit(solution)/shard_map/ppermute | solution.py:399
  61.8 6.4 %collective-permute-start.15 = (bf16[256,128]{1,0:T(8,128)(2,1)S(1)}, bf16[256,128]{1,0:T(8,128)(2,1)S(1)}, u32[]{:S(2)}, u32[]{:S(2)}) collective-permute-start(bf16[256,128]{1,0:T(8,128)(2,1)S(1)} %get-tuple-element.90), channel_id=1, source_target_pairs={{0,32},{32,64},{64,96},{1,33},{33,65},{65,97},{2,34},{34,66},{66,9... | collective-permute-start | bytes 196616 | tf_op jit(solution)/shard_map/ppermute | solution.py:400
  66.6 5.4 %collective-permute-start.16 = (bf16[256,128]{1,0:T(8,128)(2,1)S(1)}, bf16[256,128]{1,0:T(8,128)(2,1)S(1)}, u32[]{:S(2)}, u32[]{:S(2)}) collective-permute-start(bf16[256,128]{1,0:T(8,128)(2,1)S(1)} %get-tuple-element.91), channel_id=1, source_target_pairs={{0,1},{1,0},{2,3},{3,2},{4,5},{5,4},{6,7},{7,6},{8,9},{9,8},{10,11... | collective-permute-start | bytes 196616 | tf_op jit(solution)/shard_map/ppermute | solution.py:401
  68.2 7.7 %collective-permute-start.17 = (bf16[256,128]{1,0:T(8,128)(2,1)S(1)}, bf16[256,128]{1,0:T(8,128)(2,1)S(1)}, u32[]{:S(2)}, u32[]{:S(2)}) collective-permute-start(bf16[256,128]{1,0:T(8,128)(2,1)S(1)} %get-tuple-element.92), channel_id=1, source_target_pairs={{1,2},{2,1},{3,4},{4,3},{5,6},{6,5},{7,8},{8,7},{9,10},{10,9},{11,... | collective-permute-start | bytes 196616 | tf_op jit(solution)/shard_map/ppermute | solution.py:402
  76.0 7.4 %collective-permute-start.20 = (bf16[576,128]{1,0:T(8,128)(2,1)S(1)}, bf16[576,128]{1,0:T(8,128)(2,1)S(1)}, u32[]{:S(2)}, u32[]{:S(2)}) collective-permute-start(bf16[576,128]{1,0:T(8,128)(2,1)S(1)} %shard_map.112.own_ref), channel_id=1, source_target_pairs={{0,96},{1,25},{2,98},{3,27},{4,100},{5,29},{6,102},{7,31},{8,104},... | collective-permute-start | bytes 442376 | tf_op jit(solution)/shard_map/ppermute | solution.py:374
  78.9 6.7 %collective-permute-start.19 = (bf16[576,128]{1,0:T(8,128)(2,1)S(1)}, bf16[576,128]{1,0:T(8,128)(2,1)S(1)}, u32[]{:S(2)}, u32[]{:S(2)}) collective-permute-start(bf16[576,128]{1,0:T(8,128)(2,1)S(1)} %shard_map.112.own_ref), channel_id=1, source_target_pairs={{0,64},{1,17},{2,66},{3,19},{4,68},{5,21},{6,70},{7,23},{8,72},{9,... | collective-permute-start | bytes 442376 | tf_op jit(solution)/shard_map/ppermute | solution.py:374
  80.5 6.7 %collective-permute-start.18 = (bf16[576,128]{1,0:T(8,128)(2,1)S(1)}, bf16[576,128]{1,0:T(8,128)(2,1)S(1)}, u32[]{:S(2)}, u32[]{:S(2)}) collective-permute-start(bf16[576,128]{1,0:T(8,128)(2,1)S(1)} %shard_map.112.own_ref), channel_id=1, source_target_pairs={{0,32},{1,9},{2,34},{3,11},{4,36},{5,13},{6,38},{7,15},{8,40},{9,1... | collective-permute-start | bytes 442376 | tf_op jit(solution)/shard_map/ppermute | solution.py:374
  87.2 2.1 %collective-permute-start.21 = (bf16[2304,128]{1,0:T(8,128)(2,1)S(1)}, bf16[2304,128]{1,0:T(8,128)(2,1)S(1)}, u32[]{:S(2)}, u32[]{:S(2)}) collective-permute-start(bf16[2304,128]{1,0:T(8,128)(2,1)S(1)} %shard_map.114.own_ref), channel_id=1, source_target_pairs={{0,1},{1,0},{2,3},{3,2},{4,5},{5,4},{6,7},{7,6},{8,9},{9,8},{10,11... | collective-permute-start | bytes 1769480 | tf_op jit(solution)/shard_map/ppermute | solution.py:374

commit v6 on v5

--- a/solution.py
+++ b/solution.py
@@ -189,25 +189,33 @@
             far_ref[one * BLOCK : (one + 1) * BLOCK, :] = table_ref[blocks + each * slot + one].astype(BF)
 
 
-def add_kernel(table_ref, rows_ref, g0_ref, g1_ref, g2_ref, g3_ref, out_ref, ret_ref):
-    blocks = out_ref.shape[0] // BLOCK
+def add_rows(start, rows_ref, lists, ret_ref, out_ref):
+    ids = sub_iota(BLOCK, BF)
+    groups = [rows[:, g * BLOCK : (g + 1) * BLOCK] for rows in lists for g in range(rows_ref.shape[1] // BLOCK)]
+    for b in range(out_ref.shape[0] // BLOCK):
+        hot = jnp.concatenate([onehot_t((row - b * BLOCK).astype(F32), ids) for row in groups], axis=1)
+        out_ref[b * BLOCK : (b + 1) * BLOCK, :] = start(b) + mm(hot, ret_ref[...])
+
+
+def add_tile_kernel(table_ref, rows_ref, g2_ref, g3_ref, out_ref, ret_ref):
     length = rows_ref.shape[1]
-    ids = sub_iota(BLOCK, BF)
+    ret_ref[0:length, :] = g2_ref[...]
+    ret_ref[length:, :] = g3_ref[...]
+    add_rows(lambda b: table_ref[b], rows_ref, list_order(core_id(), rows_ref)[2:], ret_ref, out_ref)
+
+
+def add_slab_kernel(part_ref, rows_ref, a0_ref, b0_ref, a1_ref, b1_ref, out_ref, ret_ref):
+    length = rows_ref.shape[1]
     nothing = jnp.zeros((length, BLOCK), BF)
     slab = lax.axis_index("slab")
-    ret_ref[0:length, :] = jnp.where(slab < lax.axis_size("slab") - 1, g0_ref[g0_ref.shape[0] - length :, :], nothing)
-    ret_ref[length : 2 * length, :] = jnp.where(slab > 0, g1_ref[g1_ref.shape[0] - length :, :], nothing)
-    ret_ref[2 * length : 3 * length, :] = g2_ref[...]
-    ret_ref[3 * length :, :] = g3_ref[...]
-    groups = [
-        rows[:, g * BLOCK : (g + 1) * BLOCK]
-        for rows in list_order(core_id(), rows_ref)
-        for g in range(length // BLOCK)
-    ]
-    for b in range(blocks):
-        hot = jnp.concatenate([onehot_t((row - b * BLOCK).astype(F32), ids) for row in groups], axis=1)
-        spot = slice(b * BLOCK, (b + 1) * BLOCK)
-        out_ref[spot, :] = table_ref[b] + mm(hot, ret_ref[...])
+    first = core_id() == 0
+    tail = pl.ds(a0_ref.shape[0] - length, length)
+    above = jnp.where(first, a0_ref[tail, :], b0_ref[tail, :])
+    below = jnp.where(first, a1_ref[tail, :], b1_ref[tail, :])
+    ret_ref[0:length, :] = jnp.where(slab < lax.axis_size("slab") - 1, above, nothing)
+    ret_ref[length:, :] = jnp.where(slab > 0, below, nothing)
+    start = lambda b: part_ref[b * BLOCK : (b + 1) * BLOCK, :]
+    add_rows(start, rows_ref, list_order(core_id(), rows_ref)[:2], ret_ref, out_ref)
 
 
 def wide(v):
@@ -230,16 +238,21 @@
         out_ref[...] = (wide(keep_ref[at, :]) + wide(swap_ref[at, :])).astype(BF)
 
 
-def four_kernel(own_ref, g1_ref, g2_ref, g3_ref, out_ref):
-    total = (wide(own_ref[...]) + wide(g2_ref[...])) + (wide(g1_ref[...]) + wide(g3_ref[...]))
-    out_ref[...] = total.astype(BF)
+def four_kernel(own_ref, g1_ref, g2_ref, g3_ref, *refs):
+    m = own_ref.shape[0]
+    total = (wide(own_ref[...]) + wide(g2_ref[...])) + (wide(g1_ref[0:m, :]) + wide(g3_ref[0:m, :]))
+    outs = refs[0:1] if len(refs) == 1 else refs[2:]
+    for out_ref in outs:
+        out_ref[0:m, :] = total.astype(BF)
+    for out_ref, tail_ref in zip(outs[1:], refs):
+        out_ref[m:, :] = tail_ref[...]
 
 
 def join_kernel(own_ref, g1_ref, g2_ref, g3_ref, full_ref):
     m = own_ref.shape[0]
     place = first_axis() + 4
     for sh, ref in enumerate((own_ref, g1_ref, g2_ref, g3_ref)):
-        full_ref[quarter_at(place - sh, m), :] = ref[...]
+        full_ref[quarter_at(place - sh, m), :] = ref[0:m, :]
 
 
 def spread_kernel(own_ref, other_ref, conv_ref, down_ref):
@@ -385,34 +398,39 @@
     swap, acc = tie(swap, acc)
     m = part_rows // 8
     near_piece = ((m, out_chans), BF, near)
+    long_piece = ((m + list_len, out_chans), BF, near)
     y, *pieces = call(8, pair_kernel, [near_piece] * 4, [VM] * 2)(here(keep), here(swap))
 
-    for ph, (lo, hi) in enumerate(((1, 4), (4, pairs), (pairs, pairs))):
-        y, acc = tie(y, acc)
-        got = shifts(order[ph], pieces)
-        if lo < hi:
-            acc = back_part(acc, lo, hi)
-            *got, acc = tie(*got, acc)
-        else:
-            far = call(8, far_kernel, [((list_len, chans), BF, near)] * 4, [VM])(here(acc))
-            returned = [
-                lax.ppermute(far[0], "slab", down),
-                lax.ppermute(far[1], "slab", up),
-                lax.ppermute(far[2], "tile", chip),
-                lax.ppermute(far[3], "tile", beside),
-            ]
-            g1, g2, g3, *returned = tie(*got, *returned)
-            got = [g1, g2, g3]
-        y = call(8, four_kernel, [near_piece], [VM] * 4)(*map(here, (y, *got)))
-        pieces = [y] * 3
-
-    got = shifts(order[3], [y] * 3)
-    input_grad = call(
-        12, add_kernel, [((row_count, chans), F32)], [VM] * 6, [pltpu.VMEM((far_rows, chans), BF)]
-    )(here(acc), afar(boundary_rows), *map(here, returned))
-    *got, input_grad = tie(*got, input_grad)
+    got = shifts(order[0], pieces)
+    acc = back_part(acc, 1, 4)
+    *got, acc = tie(*got, acc)
+    y = call(8, four_kernel, [near_piece], [VM] * 4)(*map(here, (y, *got)))
+
+    y, acc = tie(y, acc)
+    got = shifts(order[1], [y] * 3)
+    acc = back_part(acc, 4, pairs)
+    far = call(8, far_kernel, [((list_len, chans), BF, near)] * 4, [VM])(here(acc))
+    *got, far0, far1, far2, far3 = tie(*got, *far)
+
+    longs = [near_piece, long_piece, long_piece]
+    y, low, high = call(8, four_kernel, longs, [VM] * 6)(*map(here, (y, *got, far0, far1)))
+    early = shifts(order[2], [high, y, low])
+    beyond = lax.ppermute(far3, "tile", beside)
+    across = lax.ppermute(far2, "tile", chip)
+    *early, beyond, across = tie(*early, beyond, across)
+    y, low, high = call(8, four_kernel, longs, [VM] * 6)(*map(here, (y, *early, far0, far1)))
+    got = shifts(order[3], [high, y, low])
+    part = call(
+        12, add_tile_kernel, [((row_count, chans), F32, near)], [VM] * 4, [pltpu.VMEM((2 * list_len, chans), BF)]
+    )(here(acc), afar(boundary_rows), here(across), here(beyond))
+    *got, part = tie(*got, part)
+    returned = [got[2], early[2], got[0], early[0]]
     full = call(8, join_kernel, [((4 * m, out_chans), BF, near)], [VM] * 4)(*map(here, (y, *got)))
     other = send(full, "cc", lambda q: 1 - q)
+    input_grad = call(
+        12, add_slab_kernel, [((row_count, chans), F32)], [VM] * 6, [pltpu.VMEM((2 * list_len, chans), BF)]
+    )(here(part), afar(boundary_rows), *map(here, returned))
+    other, input_grad = tie(other, input_grad)
     conv_grad, down_grad = call(
         12,
         spread_kernel,

time: 91.5 us -> 84.5 us (0.923)
  the two profiles are of different devices: /device:TPU:8 before, /device:TPU:1 now
where the time goes in v6:
time: 84.5 us; the launch traced here: 84.2 us
  Pallas kernels  38.2 us (45%)
  starting transfers between devices  37.3 us (44%)
  waiting for transfers between devices  7.85 us (9%)
    ppermute x14, starting transfers between devices, send(): return lax.ppermute(v, ('slab', 'tile'), links)  23 us
    pallas_call x1, Pallas kernels, body(): call(32, main_kernel, [((coarse_rows, out_chans), BF), ((pairs, 2 * BLOCK...  16.8 us
    pallas_call x3, Pallas kernels, back_part(): call(12, functools.partial(back_kernel, lo, hi, pairs), [((table, BLOCK,...  11 us
    ppermute x14, waiting for transfers between devices, send(): return lax.ppermute(v, ('slab', 'tile'), links)  5.67 us
    ppermute x1, starting transfers between devices, body(): beyond = lax.ppermute(far3, 'tile', beside)  4.52 us
    ppermute x1, starting transfers between devices, body(): lax.ppermute(outgoing[0], 'slab', up)  3.95 us
    ppermute x1, starting transfers between devices, body(): lax.ppermute(outgoing[3], 'tile', beside)  3.45 us
    pallas_call x1, Pallas kernels, body(): call(12, pick_kernel, [((list_len, chans), BF, near)] * 4 + [((blocks, BL...  2.56 us
  transfers between devices with their start and end apart: 20, of which 4 were waited for; matrix products, arithmetic and copies ran while one was open for 0% of the time, Pallas kernels for 20%

profile of v6, /device:TPU:1, one launch (start us, length us, event | category | flops | bytes accessed | tf_op | source)
XLA Modules:
  0.0 84.2 jit_solution(449383349645651952)
XLA Ops:
  0.6 2.6 %shard_map.103 = (bf16[256,128]{1,0:T(8,128)(2,1)S(1)}, bf16[256,128]{1,0:T(8,128)(2,1)S(1)}, bf16[256,128]{1,0:T(8,128)(2,1)S(1)}, bf16[256,128]{1,0:T(8,128)(2,1)S(1)}, bf16[16,128,128]{2,1,0:T(8,128)(2,1)S(1)}) custom-call(bf16[2048,128]{1,0:T(8,128)(2,1)} %feat_ref.1, s32[4,256]{1,0:T(4,128)} %rows_ref.5), custom_call_target="tpu_custom_call" | custom-call | tf_op jit(solution)/shard_map/pallas_call | solution.py:316
  3.2 4.0 %collective-permute-start = (bf16[256,128]{1,0:T(8,128)(2,1)S(1)}, bf16[256,128]{1,0:T(8,128)(2,1)S(1)}, u32[]{:S(2)}, u32[]{:S(2)}) collective-permute-start(bf16[256,128]{1,0:T(8,128)(2,1)S(1)} %get-tuple-element.62), channel_id=1, source_target_pairs={{0,32},{32,64},{64,96},{1,33},{33,65},{65,97},{2,34},{34,66},{66,9... | collective-permute-start | bytes 196616 | tf_op jit(solution)/shard_map/ppermute | solution.py:328
  7.2 1.3 %collective-permute-start.1 = (bf16[256,128]{1,0:T(8,128)(2,1)S(1)}, bf16[256,128]{1,0:T(8,128)(2,1)S(1)}, u32[]{:S(2)}, u32[]{:S(2)}) collective-permute-start(bf16[256,128]{1,0:T(8,128)(2,1)S(1)} %get-tuple-element.63), channel_id=1, source_target_pairs={{32,0},{64,32},{96,64},{33,1},{65,33},{97,65},{34,2},{66,34},{98,6... | collective-permute-start | bytes 196616 | tf_op jit(solution)/shard_map/ppermute | solution.py:329
  8.5 1.0 %collective-permute-start.2 = (bf16[256,128]{1,0:T(8,128)(2,1)S(1)}, bf16[256,128]{1,0:T(8,128)(2,1)S(1)}, u32[]{:S(2)}, u32[]{:S(2)}) collective-permute-start(bf16[256,128]{1,0:T(8,128)(2,1)S(1)} %get-tuple-element.64), channel_id=1, source_target_pairs={{0,1},{1,0},{2,3},{3,2},{4,5},{5,4},{6,7},{7,6},{8,9},{9,8},{10,11... | collective-permute-start | bytes 196616 | tf_op jit(solution)/shard_map/ppermute | solution.py:330
  9.5 3.5 %collective-permute-start.3 = (bf16[256,128]{1,0:T(8,128)(2,1)S(1)}, bf16[256,128]{1,0:T(8,128)(2,1)S(1)}, u32[]{:S(2)}, u32[]{:S(2)}) collective-permute-start(bf16[256,128]{1,0:T(8,128)(2,1)S(1)} %get-tuple-element.65), channel_id=1, source_target_pairs={{1,2},{2,1},{3,4},{4,3},{5,6},{6,5},{7,8},{8,7},{9,10},{10,9},{11,... | collective-permute-start | bytes 196616 | tf_op jit(solution)/shard_map/ppermute | solution.py:331
  12.9 2.0 %shard_map.102 = (s32[27,128]{1,0:T(8,128)S(1)}, f32[16,27,128]{2,1,0:T(8,128)S(1)}, f32[16,128]{1,0:T(8,128)S(1)}, bf16[128,3456]{1,0:T(8,128)(2,1)S(1)}, bf16[16,256,128]{2,1,0:T(8,128)(2,1)S(1)}) custom-call(s32[27,2048]{1,0:T(8,128)} %book_ref.1, s32[1,2048]{1,0:T(1,128)} %bitcast.3, bf16[27,128,128]{2,1,0:T(8,128)(2,1)} %w_ref.1, ...), custom_call_target="tpu_custom_call" | custom-call | tf_op jit(solution)/shard_map/pallas_call | solution.py:333
  15.1 16.8 %shard_map.104 = (bf16[512,128]{1,0:T(8,128)(2,1)}, bf16[8,256,128]{2,1,0:T(8,128)(2,1)S(1)}, bf16[2304,128]{1,0:T(8,128)(2,1)S(1)}, bf16[2304,128]{1,0:T(8,128)(2,1)S(1)}) custom-call(s32[27,128]{1,0:T(8,128)S(1)} %get-tuple-element.60.src_ref, bf16[16,128,128]{2,1,0:T(8,128)(2,1)S(1)} %get-tuple-element.61.xt_loc_ref, ...), custom_call_target="tpu_custom_call" | custom-call | tf_op jit(solution)/shard_map/pallas_call | solution.py:349
  31.8 0.1 collective-permute-start.4
  31.9 2.0 %shard_map.105.refs_0_ = f32[25,128,128]{2,1,0:T(8,128)S(1)} custom-call(s32[27,128]{1,0:T(8,128)S(1)} %get-tuple-element.60.src_ref, f32[16,27,128]{2,1,0:T(8,128)S(1)} %get-tuple-element.66.book_ref, bf16[128,3456]{1,0:T(8,128)(2,1)S(1)} %get-tuple-element.68.wt_ref, bf16[8,256,128]{2,1,0:T(8,128)(2,1)S(1)} %get-tuple-element.73.pg_ref), custom_call_target="tpu_custom_call" | custom-call | tf_op jit(solution)/shard_map/pallas_call | solution.py:369
  33.9 0.2 shard_map.106
  34.1 3.8 %collective-permute-start.5 = (bf16[576,128]{1,0:T(8,128)(2,1)S(1)}, bf16[576,128]{1,0:T(8,128)(2,1)S(1)}, u32[]{:S(2)}, u32[]{:S(2)}) collective-permute-start(bf16[576,128]{1,0:T(8,128)(2,1)S(1)} %get-tuple-element.76), channel_id=1, source_target_pairs={{0,32},{1,9},{2,34},{3,11},{4,36},{5,13},{6,38},{7,15},{8,40},{9,1... | collective-permute-start | bytes 442376 | tf_op jit(solution)/shard_map/ppermute | solution.py:387
  37.9 2.9 %collective-permute-start.6 = (bf16[576,128]{1,0:T(8,128)(2,1)S(1)}, bf16[576,128]{1,0:T(8,128)(2,1)S(1)}, u32[]{:S(2)}, u32[]{:S(2)}) collective-permute-start(bf16[576,128]{1,0:T(8,128)(2,1)S(1)} %get-tuple-element.77), channel_id=1, source_target_pairs={{0,64},{1,17},{2,66},{3,19},{4,68},{5,21},{6,70},{7,23},{8,72},{9,... | collective-permute-start | bytes 442376 | tf_op jit(solution)/shard_map/ppermute | solution.py:387
  40.8 0.8 collective-permute-start.7
  41.6 4.2 %shard_map.107.refs_0_ = f32[25,128,128]{2,1,0:T(8,128)S(1)} custom-call(s32[27,128]{1,0:T(8,128)S(1)} %get-tuple-element.60.src_ref, f32[16,27,128]{2,1,0:T(8,128)S(1)} %get-tuple-element.66.book_ref, bf16[128,3456]{1,0:T(8,128)(2,1)S(1)} %get-tuple-element.68.wt_ref, bf16[8,256,128]{2,1,0:T(8,128)(2,1)S(1)} %get-tuple-element.73.pg_ref, ...), custom_call_target="tpu_custom_call" | custom-call | tf_op jit(solution)/shard_map/pallas_call | solution.py:369
  45.9 3.5 %collective-permute-start.10 = (bf16[576,128]{1,0:T(8,128)(2,1)S(1)}, bf16[576,128]{1,0:T(8,128)(2,1)S(1)}, u32[]{:S(2)}, u32[]{:S(2)}) collective-permute-start(bf16[576,128]{1,0:T(8,128)(2,1)S(1)} %shard_map.108.own_ref), channel_id=1, source_target_pairs={{0,24},{1,7},{2,26},{3,1},{4,28},{5,3},{6,30},{7,5},{8,0},{9,15},{... | collective-permute-start | bytes 442376 | tf_op jit(solution)/shard_map/ppermute | solution.py:387
  49.4 0.7 collective-permute-start.8
  50.1 4.8 %shard_map.109.table_ref = f32[25,128,128]{2,1,0:T(8,128)S(1)} custom-call(s32[27,128]{1,0:T(8,128)S(1)} %get-tuple-element.60.src_ref, f32[16,27,128]{2,1,0:T(8,128)S(1)} %get-tuple-element.66.book_ref, bf16[128,3456]{1,0:T(8,128)(2,1)S(1)} %get-tuple-element.68.wt_ref, bf16[8,256,128]{2,1,0:T(8,128)(2,1)S(1)} %get-tuple-element.73.pg_ref, ...), custom_call_target="tpu_custom_call" | custom-call | tf_op jit(solution)/shard_map/pallas_call | solution.py:369
  55.0 1.5 %collective-permute-done.8.g1_ref = bf16[576,128]{1,0:T(8,128)(2,1)S(1)} collective-permute-done((bf16[576,128]{1,0:T(8,128)(2,1)S(1)}, bf16[576,128]{1,0:T(8,128)(2,1)S(1)}, u32[]{:S(2)}, u32[]{:S(2)}) %collective-permute-start.8) | collective-permute-done | bytes 147488 | tf_op jit(solution)/shard_map/ppermute | solution.py:387
  56.6 2.4 %collective-permute-start.11 = (bf16[832,128]{1,0:T(8,128)(2,1)S(1)}, bf16[832,128]{1,0:T(8,128)(2,1)S(1)}, u32[]{:S(2)}, u32[]{:S(2)}) collective-permute-start(bf16[832,128]{1,0:T(8,128)(2,1)S(1)} %get-tuple-element.96), channel_id=1, source_target_pairs={{0,2},{1,33},{2,4},{3,35},{4,6},{5,37},{6,0},{7,39},{8,10},{9,41},... | collective-permute-start | bytes 638984 | tf_op jit(solution)/shard_map/ppermute | solution.py:387
  59.0 1.3 %collective-permute-start.13 = (bf16[832,128]{1,0:T(8,128)(2,1)S(1)}, bf16[832,128]{1,0:T(8,128)(2,1)S(1)}, u32[]{:S(2)}, u32[]{:S(2)}) collective-permute-start(bf16[832,128]{1,0:T(8,128)(2,1)S(1)} %get-tuple-element.97), channel_id=1, source_target_pairs={{0,6},{1,97},{2,0},{3,99},{4,2},{5,101},{6,4},{7,103},{8,14},{9,10... | collective-permute-start | bytes 638984 | tf_op jit(solution)/shard_map/ppermute | solution.py:387
  60.4 1.7 %collective-permute-start.12 = (bf16[576,128]{1,0:T(8,128)(2,1)S(1)}, bf16[576,128]{1,0:T(8,128)(2,1)S(1)}, u32[]{:S(2)}, u32[]{:S(2)}) collective-permute-start(bf16[576,128]{1,0:T(8,128)(2,1)S(1)} %get-tuple-element.95.own_ref), channel_id=1, source_target_pairs={{0,4},{1,65},{2,6},{3,67},{4,0},{5,69},{6,2},{7,71},{8,12},{9,73},... | collective-permute-start | bytes 442376 | tf_op jit(solution)/shard_map/ppermute | solution.py:387
  62.0 4.5 %collective-permute-start.14 = (bf16[256,128]{1,0:T(8,128)(2,1)S(1)}, bf16[256,128]{1,0:T(8,128)(2,1)S(1)}, u32[]{:S(2)}, u32[]{:S(2)}) collective-permute-start(bf16[256,128]{1,0:T(8,128)(2,1)S(1)} %get-tuple-element.98), channel_id=1, source_target_pairs={{1,2},{2,1},{3,4},{4,3},{5,6},{6,5},{7,8},{8,7},{9,10},{10,9},{11,... | collective-permute-start | bytes 196616 | tf_op jit(solution)/shard_map/ppermute | solution.py:418
  66.5 0.1 collective-permute-start.15
  66.6 2.1 %collective-permute-done.14.g3_ref = bf16[256,128]{1,0:T(8,128)(2,1)S(1)} collective-permute-done((bf16[256,128]{1,0:T(8,128)(2,1)S(1)}, bf16[256,128]{1,0:T(8,128)(2,1)S(1)}, u32[]{:S(2)}, u32[]{:S(2)}) %collective-permute-start.14) | collective-permute-done | bytes 65568 | tf_op jit(solution)/shard_map/ppermute | solution.py:418
  68.8 0.1 shard_map.112
  68.9 0.2 collective-permute-start.16
  69.1 2.5 %collective-permute-start.18 = (bf16[832,128]{1,0:T(8,128)(2,1)S(1)}, bf16[832,128]{1,0:T(8,128)(2,1)S(1)}, u32[]{:S(2)}, u32[]{:S(2)}) collective-permute-start(bf16[832,128]{1,0:T(8,128)(2,1)S(1)} %get-tuple-element.105), channel_id=1, source_target_pairs={{0,96},{1,25},{2,98},{3,27},{4,100},{5,29},{6,102},{7,31},{8,104},... | collective-permute-start | bytes 638984 | tf_op jit(solution)/shard_map/ppermute | solution.py:387
  71.6 1.4 %shard_map.113.part_ref = f32[2048,128]{1,0:T(8,128)S(1)} custom-call(f32[25,128,128]{2,1,0:T(8,128)S(1)} %shard_map.109.table_ref, s32[4,256]{1,0:T(4,128)} %rows_ref.5, bf16[256,128]{1,0:T(8,128)(2,1)S(1)} %collective-permute-done.15.g2_ref, bf16[256,128]{1,0:T(8,128)(2,1)S(1)} %collective-permute-done.14.g3_ref), custom_call_target="tpu_custom_call" | custom-call | tf_op jit(solution)/shard_map/pallas_call | solution.py:423
  73.0 4.1 %collective-permute-done.17.g2_ref = bf16[576,128]{1,0:T(8,128)(2,1)S(1)} collective-permute-done((bf16[576,128]{1,0:T(8,128)(2,1)S(1)}, bf16[576,128]{1,0:T(8,128)(2,1)S(1)}, u32[]{:S(2)}, u32[]{:S(2)}) %collective-permute-start.17) | collective-permute-done | bytes 147488 | tf_op jit(solution)/shard_map/ppermute | solution.py:387
  77.2 3.1 %collective-permute-start.19 = (bf16[2304,128]{1,0:T(8,128)(2,1)S(1)}, bf16[2304,128]{1,0:T(8,128)(2,1)S(1)}, u32[]{:S(2)}, u32[]{:S(2)}) collective-permute-start(bf16[2304,128]{1,0:T(8,128)(2,1)S(1)} %shard_map.114.own_ref), channel_id=1, source_target_pairs={{0,1},{1,0},{2,3},{3,2},{4,5},{5,4},{6,7},{7,6},{8,9},{9,8},{10,11... | collective-permute-start | bytes 1769480 | tf_op jit(solution)/shard_map/ppermute | solution.py:387
  80.3 2.4 %shard_map.115 = f32[2048,128]{1,0:T(8,128)} custom-call(f32[2048,128]{1,0:T(8,128)S(1)} %shard_map.113.part_ref, s32[4,256]{1,0:T(4,128)} %rows_ref.5, bf16[832,128]{1,0:T(8,128)(2,1)S(1)} %collective-permute-done.18.g3_ref.a0_ref, bf16[832,128]{1,0:T(8,128)(2,1)S(1)} %collective-permute-done.13.g3_ref.b0_ref, ...), custom_call_target="tpu_custom_call" | custom-call | tf_op jit(solution)/shard_map/pallas_call | solution.py:430
  82.7 1.5 %shard_map.116 = (f32[3456,128]{1,0:T(8,128)}, f32[1024,128]{1,0:T(8,128)}) custom-call(bf16[2304,128]{1,0:T(8,128)(2,1)S(1)} %shard_map.114.own_ref, bf16[2304,128]{1,0:T(8,128)(2,1)S(1)} %collective-permute-done.19.other_ref), custom_call_target="tpu_custom_call" | custom-call | tf_op jit(solution)/shard_map/pallas_call | solution.py:434
  (23 shorter events, 0.4 us)
Async XLA Ops:
  3.2 11.8 %collective-permute-start = (bf16[256,128]{1,0:T(8,128)(2,1)S(1)}, bf16[256,128]{1,0:T(8,128)(2,1)S(1)}, u32[]{:S(2)}, u32[]{:S(2)}) collective-permute-start(bf16[256,128]{1,0:T(8,128)(2,1)S(1)} %get-tuple-element.62), channel_id=1, source_target_pairs={{0,32},{32,64},{64,96},{1,33},{33,65},{65,97},{2,34},{34,66},{66,9... | collective-permute-start | bytes 196616 | tf_op jit(solution)/shard_map/ppermute | solution.py:328
  7.2 7.8 %collective-permute-start.1 = (bf16[256,128]{1,0:T(8,128)(2,1)S(1)}, bf16[256,128]{1,0:T(8,128)(2,1)S(1)}, u32[]{:S(2)}, u32[]{:S(2)}) collective-permute-start(bf16[256,128]{1,0:T(8,128)(2,1)S(1)} %get-tuple-element.63), channel_id=1, source_target_pairs={{32,0},{64,32},{96,64},{33,1},{65,33},{97,65},{34,2},{66,34},{98,6... | collective-permute-start | bytes 196616 | tf_op jit(solution)/shard_map/ppermute | solution.py:329
  8.5 6.6 %collective-permute-start.2 = (bf16[256,128]{1,0:T(8,128)(2,1)S(1)}, bf16[256,128]{1,0:T(8,128)(2,1)S(1)}, u32[]{:S(2)}, u32[]{:S(2)}) collective-permute-start(bf16[256,128]{1,0:T(8,128)(2,1)S(1)} %get-tuple-element.64), channel_id=1, source_target_pairs={{0,1},{1,0},{2,3},{3,2},{4,5},{5,4},{6,7},{7,6},{8,9},{9,8},{10,11... | collective-permute-start | bytes 196616 | tf_op jit(solution)/shard_map/ppermute | solution.py:330
  9.5 5.6 %collective-permute-start.3 = (bf16[256,128]{1,0:T(8,128)(2,1)S(1)}, bf16[256,128]{1,0:T(8,128)(2,1)S(1)}, u32[]{:S(2)}, u32[]{:S(2)}) collective-permute-start(bf16[256,128]{1,0:T(8,128)(2,1)S(1)} %get-tuple-element.65), channel_id=1, source_target_pairs={{1,2},{2,1},{3,4},{4,3},{5,6},{6,5},{7,8},{8,7},{9,10},{10,9},{11,... | collective-permute-start | bytes 196616 | tf_op jit(solution)/shard_map/ppermute | solution.py:331
  31.8 2.1 %collective-permute-start.4 = (bf16[2304,128]{1,0:T(8,128)(2,1)S(1)}, bf16[2304,128]{1,0:T(8,128)(2,1)S(1)}, u32[]{:S(2)}, u32[]{:S(2)}) collective-permute-start(bf16[2304,128]{1,0:T(8,128)(2,1)S(1)} %get-tuple-element.72), channel_id=1, source_target_pairs={{0,1},{1,0},{2,3},{3,2},{4,5},{5,4},{6,7},{7,6},{8,9},{9,8},{10,11... | collective-permute-start | bytes 1769480 | tf_op jit(solution)/shard_map/ppermute | solution.py:387
  34.1 11.7 %collective-permute-start.5 = (bf16[576,128]{1,0:T(8,128)(2,1)S(1)}, bf16[576,128]{1,0:T(8,128)(2,1)S(1)}, u32[]{:S(2)}, u32[]{:S(2)}) collective-permute-start(bf16[576,128]{1,0:T(8,128)(2,1)S(1)} %get-tuple-element.76), channel_id=1, source_target_pairs={{0,32},{1,9},{2,34},{3,11},{4,36},{5,13},{6,38},{7,15},{8,40},{9,1... | collective-permute-start | bytes 442376 | tf_op jit(solution)/shard_map/ppermute | solution.py:387
  37.9 7.9 %collective-permute-start.6 = (bf16[576,128]{1,0:T(8,128)(2,1)S(1)}, bf16[576,128]{1,0:T(8,128)(2,1)S(1)}, u32[]{:S(2)}, u32[]{:S(2)}) collective-permute-start(bf16[576,128]{1,0:T(8,128)(2,1)S(1)} %get-tuple-element.77), channel_id=1, source_target_pairs={{0,64},{1,17},{2,66},{3,19},{4,68},{5,21},{6,70},{7,23},{8,72},{9,... | collective-permute-start | bytes 442376 | tf_op jit(solution)/shard_map/ppermute | solution.py:387
  40.8 5.0 %collective-permute-start.7 = (bf16[576,128]{1,0:T(8,128)(2,1)S(1)}, bf16[576,128]{1,0:T(8,128)(2,1)S(1)}, u32[]{:S(2)}, u32[]{:S(2)}) collective-permute-start(bf16[576,128]{1,0:T(8,128)(2,1)S(1)} %get-tuple-element.78), channel_id=1, source_target_pairs={{0,96},{1,25},{2,98},{3,27},{4,100},{5,29},{6,102},{7,31},{8,104},... | collective-permute-start | bytes 442376 | tf_op jit(solution)/shard_map/ppermute | solution.py:387
  45.9 9.1 %collective-permute-start.10 = (bf16[576,128]{1,0:T(8,128)(2,1)S(1)}, bf16[576,128]{1,0:T(8,128)(2,1)S(1)}, u32[]{:S(2)}, u32[]{:S(2)}) collective-permute-start(bf16[576,128]{1,0:T(8,128)(2,1)S(1)} %shard_map.108.own_ref), channel_id=1, source_target_pairs={{0,24},{1,7},{2,26},{3,1},{4,28},{5,3},{6,30},{7,5},{8,0},{9,15},{... | collective-permute-start | bytes 442376 | tf_op jit(solution)/shard_map/ppermute | solution.py:387
  49.4 5.6 %collective-permute-start.9 = (bf16[576,128]{1,0:T(8,128)(2,1)S(1)}, bf16[576,128]{1,0:T(8,128)(2,1)S(1)}, u32[]{:S(2)}, u32[]{:S(2)}) collective-permute-start(bf16[576,128]{1,0:T(8,128)(2,1)S(1)} %shard_map.108.own_ref), channel_id=1, source_target_pairs={{0,16},{1,5},{2,18},{3,7},{4,20},{5,1},{6,22},{7,3},{8,24},{9,13},... | collective-permute-start | bytes 442376 | tf_op jit(solution)/shard_map/ppermute | solution.py:387
  49.4 7.1 %collective-permute-start.8 = (bf16[576,128]{1,0:T(8,128)(2,1)S(1)}, bf16[576,128]{1,0:T(8,128)(2,1)S(1)}, u32[]{:S(2)}, u32[]{:S(2)}) collective-permute-start(bf16[576,128]{1,0:T(8,128)(2,1)S(1)} %shard_map.108.own_ref), channel_id=1, source_target_pairs={{0,8},{1,3},{2,10},{3,5},{4,12},{5,7},{6,14},{7,1},{8,16},{9,11},{... | collective-permute-start | bytes 442376 | tf_op jit(solution)/shard_map/ppermute | solution.py:387
  56.6 12.2 %collective-permute-start.11 = (bf16[832,128]{1,0:T(8,128)(2,1)S(1)}, bf16[832,128]{1,0:T(8,128)(2,1)S(1)}, u32[]{:S(2)}, u32[]{:S(2)}) collective-permute-start(bf16[832,128]{1,0:T(8,128)(2,1)S(1)} %get-tuple-element.96), channel_id=1, source_target_pairs={{0,2},{1,33},{2,4},{3,35},{4,6},{5,37},{6,0},{7,39},{8,10},{9,41},... | collective-permute-start | bytes 638984 | tf_op jit(solution)/shard_map/ppermute | solution.py:387
  59.0 9.8 %collective-permute-start.13 = (bf16[832,128]{1,0:T(8,128)(2,1)S(1)}, bf16[832,128]{1,0:T(8,128)(2,1)S(1)}, u32[]{:S(2)}, u32[]{:S(2)}) collective-permute-start(bf16[832,128]{1,0:T(8,128)(2,1)S(1)} %get-tuple-element.97), channel_id=1, source_target_pairs={{0,6},{1,97},{2,0},{3,99},{4,2},{5,101},{6,4},{7,103},{8,14},{9,10... | collective-permute-start | bytes 638984 | tf_op jit(solution)/shard_map/ppermute | solution.py:387
  60.4 8.4 %collective-permute-start.12 = (bf16[576,128]{1,0:T(8,128)(2,1)S(1)}, bf16[576,128]{1,0:T(8,128)(2,1)S(1)}, u32[]{:S(2)}, u32[]{:S(2)}) collective-permute-start(bf16[576,128]{1,0:T(8,128)(2,1)S(1)} %get-tuple-element.95.own_ref), channel_id=1, source_target_pairs={{0,4},{1,65},{2,6},{3,67},{4,0},{5,69},{6,2},{7,71},{8,12},{9,73},... | collective-permute-start | bytes 442376 | tf_op jit(solution)/shard_map/ppermute | solution.py:387
  62.0 6.8 %collective-permute-start.14 = (bf16[256,128]{1,0:T(8,128)(2,1)S(1)}, bf16[256,128]{1,0:T(8,128)(2,1)S(1)}, u32[]{:S(2)}, u32[]{:S(2)}) collective-permute-start(bf16[256,128]{1,0:T(8,128)(2,1)S(1)} %get-tuple-element.98), channel_id=1, source_target_pairs={{1,2},{2,1},{3,4},{4,3},{5,6},{6,5},{7,8},{8,7},{9,10},{10,9},{11,... | collective-permute-start | bytes 196616 | tf_op jit(solution)/shard_map/ppermute | solution.py:418
  66.5 2.2 %collective-permute-start.15 = (bf16[256,128]{1,0:T(8,128)(2,1)S(1)}, bf16[256,128]{1,0:T(8,128)(2,1)S(1)}, u32[]{:S(2)}, u32[]{:S(2)}) collective-permute-start(bf16[256,128]{1,0:T(8,128)(2,1)S(1)} %get-tuple-element.99), channel_id=1, source_target_pairs={{0,1},{1,0},{2,3},{3,2},{4,5},{5,4},{6,7},{7,6},{8,9},{9,8},{10,11... | collective-permute-start | bytes 196616 | tf_op jit(solution)/shard_map/ppermute | solution.py:419
  68.9 8.2 %collective-permute-start.16 = (bf16[832,128]{1,0:T(8,128)(2,1)S(1)}, bf16[832,128]{1,0:T(8,128)(2,1)S(1)}, u32[]{:S(2)}, u32[]{:S(2)}) collective-permute-start(bf16[832,128]{1,0:T(8,128)(2,1)S(1)} %get-tuple-element.104), channel_id=1, source_target_pairs={{0,32},{1,9},{2,34},{3,11},{4,36},{5,13},{6,38},{7,15},{8,40},{9,1... | collective-permute-start | bytes 638984 | tf_op jit(solution)/shard_map/ppermute | solution.py:387
  69.1 8.0 %collective-permute-start.18 = (bf16[832,128]{1,0:T(8,128)(2,1)S(1)}, bf16[832,128]{1,0:T(8,128)(2,1)S(1)}, u32[]{:S(2)}, u32[]{:S(2)}) collective-permute-start(bf16[832,128]{1,0:T(8,128)(2,1)S(1)} %get-tuple-element.105), channel_id=1, source_target_pairs={{0,96},{1,25},{2,98},{3,27},{4,100},{5,29},{6,102},{7,31},{8,104},... | collective-permute-start | bytes 638984 | tf_op jit(solution)/shard_map/ppermute | solution.py:387
  71.6 5.5 %collective-permute-start.17 = (bf16[576,128]{1,0:T(8,128)(2,1)S(1)}, bf16[576,128]{1,0:T(8,128)(2,1)S(1)}, u32[]{:S(2)}, u32[]{:S(2)}) collective-permute-start(bf16[576,128]{1,0:T(8,128)(2,1)S(1)} %get-tuple-element.103.own_ref), channel_id=1, source_target_pairs={{0,64},{1,17},{2,66},{3,19},{4,68},{5,21},{6,70},{7,23},{8,72},{9,... | collective-permute-start | bytes 442376 | tf_op jit(solution)/shard_map/ppermute | solution.py:387
  77.2 5.5 %collective-permute-start.19 = (bf16[2304,128]{1,0:T(8,128)(2,1)S(1)}, bf16[2304,128]{1,0:T(8,128)(2,1)S(1)}, u32[]{:S(2)}, u32[]{:S(2)}) collective-permute-start(bf16[2304,128]{1,0:T(8,128)(2,1)S(1)} %shard_map.114.own_ref), channel_id=1, source_target_pairs={{0,1},{1,0},{2,3},{3,2},{4,5},{5,4},{6,7},{7,6},{8,9},{9,8},{10,11... | collective-permute-start | bytes 1769480 | tf_op jit(solution)/shard_map/ppermute | solution.py:387
